TPU v7x, 128 devices: a whole 4x4x4 slice. The times are simulated.
128 devices in a mesh: band: 32 (over z_lo, y, x), member: 4 (over z_hi, core).
Axes of the slice: x: 4, y: 4, z: 4 (z_hi: 2, z_lo: 2; z = z_hi * 2 + z_lo), core: 2. Of those that a mesh axis runs over, the one named last changes fastest.
Arguments:
- state_field: bfloat16 [128, 1440, 128], P('band'), may hold values from -6 to 6
- observed_target: bfloat16 [128, 1440, 128], P('band'), may hold values from -6 to 6
- feature_jitter_amplitude: float32 [128], replicated, may hold values from 0.2 to 1
- leading_filter: bfloat16 [3, 3, 128, 128], replicated, may hold values from -0.1875 to 0.1875
- trailing_filter: bfloat16 [3, 3, 128, 128], replicated, may hold values from -0.1875 to 0.1875
- parallels_each_strip: int32 [32], replicated, may hold values from 1 to 4, 96 in all
- realization_random_keys: int32 [4], P('member'), may hold values from 0 to 999999
Outputs:
- crps_cells: float32 [128, 1440], P('band', 'member')
- mean_loss: float32 [], replicated
- grad_one: float32 [3, 3, 128, 128], replicated
- trailing_filter_derivative: float32 [3, 3, 128, 128], replicated
Inputs may be any that keep to these rules, and one draw needn't show every extreme that they name: `parallels_each_strip`: each band holds 1 to 4 rows, together 96, and some band holds exactly 4.
All inputs are finite; a program needn't handle non-finite values.
Results may differ from a plain program's by a relative error of at most 0.00075.
The roundings to bfloat16 on the way count: a program that leaves them out, or rounds other values in their place, can miss the bound.
Values may be sent and summed in bfloat16 or wider, within the bound.
No kernel may reach another device: no remote copies, remote signals or barrier semaphores. Data moves between devices by JAX's collectives and lax.ppermute only.
A program may use at most 128 MiB of HBM per device.

v0:
```python
import math

import jax
import jax.numpy as jnp
import numpy as np
from jax import lax
from jax.experimental import pallas as pl
from jax.experimental.pallas import tpu as pltpu
from jax.sharding import PartitionSpec as P

GRID_ROWS = 721
ROWS_TOTAL = 96
SMOOTH = 0.01
LON = 1440
OWN = 360
LEFT = 8
J = 384
C = 128
MEM = 4
SLOTS = 4
DEPTH = 3
EXT = SLOTS + 2 * DEPTH
PAD = 8
R = 2368
BF = jnp.bfloat16
F32 = jnp.float32
BM = ("band", "member")


def coords(i):
    return [i // 64, i // 16 % 4, i // 4 % 4, i // 2 % 2, i % 2]


def index(v):
    return (((v[0] * 4 + v[1]) * 4 + v[2]) * 2 + v[3]) * 2 + v[4]


SIZES = [2, 4, 4, 2, 2]


def shift(value, dim, by):
    pairs = []
    for i in range(128):
        v = coords(i)
        v[dim] = (v[dim] + by) % SIZES[dim]
        pairs.append((i, index(v)))
    return lax.ppermute(value, BM, pairs)


def scatter_sum(value, dim, place):
    n = SIZES[dim]
    parts = value.reshape(n, value.shape[0] // n, C)
    total = lax.dynamic_index_in_dim(parts, place, 0, keepdims=False)
    got = [
        shift(lax.dynamic_index_in_dim(parts, (place + d) % n, 0, keepdims=False), dim, d)
        for d in range(1, n)
    ]
    for g in got:
        total = total + g
    return total


def exchange_sum(value, dim):
    got = [shift(value, dim, d) for d in range(1, SIZES[dim])]
    for g in got:
        value = value + g
    return value


def gather(value, dim, place):
    n = SIZES[dim]
    got = [shift(value, dim, d) for d in range(1, n)]
    out = jnp.zeros((n,) + value.shape, value.dtype)
    out = lax.dynamic_update_index_in_dim(out, value, place, 0)
    for d, g in enumerate(got, 1):
        out = lax.dynamic_update_index_in_dim(out, g, (place - d) % n, 0)
    return out.reshape(n * value.shape[0], C)


def sigmoid(a):
    return 1.0 / (1.0 + jnp.exp(-a))


def kernel(
    counts_ref, seeds_ref, place_ref, weight_ref,
    own_ref, fwd1_ref, fwd2_ref, fwd3_ref, bwd1_ref, bwd2_ref, bwd3_ref,
    target_ref, amp_ref, w1_ref, w2_ref, wt_ref,
    grads_ref, cells_ref,
    state_s, tgt_s, hash_s, buf_s, in3_s, hid3_s, cot3_s, pre_s, fc_s, ya_s, yb_s, acc_s,
):
    band = place_ref[0]
    quarter = place_ref[1]
    n = counts_ref[band]

    def count(b):
        inside = (b >= 0) & (b < 32)
        return jnp.where(inside, counts_ref[jnp.clip(b, 0, 31)], 4)

    offset = lax.fori_loop(0, band, lambda b, s: s + counts_ref[b], jnp.int32(0))
    up1, up2 = count(band - 1), count(band - 2)
    dn1, dn2 = count(band + 1), count(band + 2)

    state_s[DEPTH : DEPTH + SLOTS] = own_ref[...]
    state_s[2] = fwd1_ref[2]

    def pick(dst, cond, a, b):
        @pl.when(cond)
        def _():
            state_s[dst] = a()

        @pl.when(jnp.logical_not(cond))
        def _():
            state_s[dst] = b()

    pick(1, up1 >= 2, lambda: fwd1_ref[1], lambda: fwd2_ref[1])
    pick(0, up2 >= 2, lambda: fwd2_ref[0], lambda: fwd3_ref[0])

    @pl.when(up1 == 2)
    def _():
        state_s[0] = fwd2_ref[1]

    @pl.when(up1 >= 3)
    def _():
        state_s[0] = fwd1_ref[0]

    below = DEPTH + n
    state_s[below] = bwd1_ref[0]
    pick(below + 1, dn1 >= 2, lambda: bwd1_ref[1], lambda: bwd2_ref[0])
    pick(below + 2, dn2 >= 2, lambda: bwd2_ref[1], lambda: bwd3_ref[0])

    @pl.when(dn1 == 2)
    def _():
        state_s[below + 2] = bwd2_ref[0]

    @pl.when(dn1 >= 3)
    def _():
        state_s[below + 2] = bwd1_ref[2]

    tgt_s[1 : 1 + SLOTS] = target_ref[...]
    tgt_s[0] = fwd1_ref[3]
    tgt_s[1 + n] = bwd1_ref[3]

    buf_s[0:PAD] = jnp.zeros((PAD, C), F32)
    buf_s[PAD + J :] = jnp.zeros((PAD, C), F32)

    cols = lax.broadcasted_iota(jnp.int32, (J, C), 0)
    chan = lax.broadcasted_iota(jnp.int32, (J, C), 1)
    lon = quarter * OWN - LEFT + cols
    lon = jnp.where(lon < 0, lon + LON, jnp.where(lon >= LON, lon - LON, lon))
    hash_s[...] = lon * 668265263 + chan * 1274126177
    own_col = ((cols >= LEFT) & (cols < LEFT + OWN)).astype(F32)

    def valid(e):
        g = offset - DEPTH + e
        return ((g >= 0) & (g < ROWS_TOTAL)).astype(F32)

    def put3(ref, m, e, v):
        buf_s[PAD : PAD + J] = v
        ref[m, e, :, C : 2 * C] = v.astype(BF)
        ref[m, e, :, 0:C] = buf_s[PAD - 1 : PAD - 1 + J].astype(BF)
        ref[m, e, :, 2 * C :] = buf_s[PAD + 1 : PAD + 1 + J].astype(BF)

    amp = amp_ref[...]

    def make_inputs(i, _):
        e, m = i // MEM, i % MEM
        base = (offset - DEPTH + e) * 374761393 + seeds_ref[m] * 1103515245
        h = hash_s[...] + base
        h = h ^ (h >> 13)
        h = h * 1274126177
        h = h ^ (h >> 16)
        noise = (h & 65535).astype(F32) * (1.0 / 32768.0) + (0.5 / 32768.0 - 1.0)
        v = (state_s[e].astype(F32) + amp * noise) * valid(e)
        put3(in3_s, m, e, v)
        return 0

    lax.fori_loop(0, EXT * MEM, make_inputs, 0)

    def conv_pair(ref, m, e, w):
        lhs = jnp.concatenate([ref[m, e + s] for s in range(4)], axis=1)
        return jnp.dot(lhs, w[...], preferred_element_type=F32)

    def make_hidden(i, _):
        p, m = i // MEM, i % MEM
        out = conv_pair(in3_s, m, 2 * p, w1_ref)
        for k in range(2):
            e = 1 + 2 * p + k
            a = out[:, k * C : (k + 1) * C]

            @pl.when((e >= DEPTH) & (e < DEPTH + SLOTS))
            def _():
                pre_s[m, e - DEPTH] = a

            put3(hid3_s, m, e - 1, a * sigmoid(a) * valid(e))
        return 0

    lax.fori_loop(0, 4 * MEM, make_hidden, 0)

    def make_forecast(i, _):
        p, m = i // MEM, i % MEM
        out = conv_pair(hid3_s, m, 2 * p, w2_ref)
        for k in range(2):
            e = 2 + 2 * p + k
            v = (in3_s[m, e, :, C : 2 * C].astype(F32) + out[:, k * C : (k + 1) * C]) * valid(e)
            fc_s[m, e - 2] = v.astype(BF)
        return 0

    lax.fori_loop(0, 3 * MEM, make_forecast, 0)

    pair_scale = 1.0 / (MEM * (MEM - 1))
    factor = 1.0 / math.sqrt(ROWS_TOTAL * LON)

    def make_crps(r, loss):
        e = r + 2
        g = jnp.clip(offset - DEPTH + e, 0, ROWS_TOTAL - 1)
        weight = weight_ref[g] * valid(e)
        mine = ((r >= 1) & (r < 1 + n)).astype(F32)
        t = tgt_s[r].astype(F32)
        f = [fc_s[m, r].astype(F32) for m in range(MEM)]
        skill = jnp.zeros_like(t)
        spread = jnp.zeros_like(t)
        slopes = []
        for m in range(MEM):
            d = f[m] - t
            q = d * d + SMOOTH
            inv = lax.rsqrt(q)
            skill = skill + q * inv
            slopes.append(d * inv * (1.0 / MEM))
        for a in range(MEM):
            for b in range(a + 1, MEM):
                d = f[a] - f[b]
                q = d * d + SMOOTH
                inv = lax.rsqrt(q)
                spread = spread + q * inv
                tilt = d * inv * pair_scale
                slopes[a] = slopes[a] - tilt
                slopes[b] = slopes[b] + tilt
        crps = skill * (1.0 / MEM) - spread * pair_scale
        for m in range(MEM):
            v = slopes[m] * (weight * factor)
            put3(cot3_s, m, r, v)

            @pl.when((r >= 1) & (r < 1 + SLOTS))
            def _():
                ya_s[m, r - 1] = (v * (own_col * mine)).astype(BF)

        cell = jnp.sum(jnp.transpose(crps), axis=0, keepdims=True) * (weight * mine / C)

        @pl.when((r >= 1) & (r < 1 + SLOTS))
        def _():
            cells_ref[r - 1] = cell

        return loss + cell

    loss = lax.fori_loop(0, SLOTS + 2, make_crps, jnp.zeros((1, J), F32))
    lane = lax.broadcasted_iota(jnp.int32, (1, J), 1)
    loss = jnp.where((lane >= LEFT) & (lane < LEFT + OWN), loss, 0.0)

    def make_pre_cot(i, _):
        p, m = i // MEM, i % MEM
        out = conv_pair(cot3_s, m, 2 * p, wt_ref)
        for k in range(2):
            s = 2 * p + k
            a = pre_s[m, s]
            sig = sigmoid(a)
            mine = (s < n).astype(F32)
            v = out[:, k * C : (k + 1) * C] * (sig * (1.0 + a * (1.0 - sig))) * (own_col * mine)
            yb_s[m, s] = v.astype(BF)
        return 0

    lax.fori_loop(0, 2 * MEM, make_pre_cot, 0)

    def weight_grad(x3, first, y, row0):
        acc_s[...] = jnp.zeros_like(acc_s)

        def step(m, _):
            ys = jnp.concatenate(
                [
                    jnp.concatenate([y[m, 0], y[m, 1]], axis=1),
                    jnp.concatenate([y[m, 2], y[m, 3]], axis=1),
                ],
                axis=0,
            )
            for s in range(4):
                xs = jnp.concatenate([x3[m, first + s], x3[m, first + 2 + s]], axis=0)
                acc_s[:, s * 384 : (s + 1) * 384] += lax.dot_general(
                    ys, xs, (((0,), (0,)), ((), ())), preferred_element_type=F32
                )
            return 0

        lax.fori_loop(0, MEM, step, 0)
        for k in range(9):
            blk = acc_s[0:C, k * C : (k + 1) * C] + acc_s[C:, 384 + k * C : 384 + (k + 1) * C]
            grads_ref[row0 + k * C : row0 + (k + 1) * C] = jnp.transpose(blk)

    weight_grad(in3_s, 2, yb_s, 0)
    weight_grad(hid3_s, 1, ya_s, 1152)
    total = jnp.sum(loss, axis=1, keepdims=True) * (1.0 / (ROWS_TOTAL * LON))
    grads_ref[2304:R] = jnp.broadcast_to(total, (R - 2304, C))


def local_step(counts, seeds, place, weights, own, f1, f2, f3, b1, b2, b3, target, amp, w1, w2, wt):
    smem = pl.BlockSpec(memory_space=pltpu.SMEM)
    vmem = pl.BlockSpec(memory_space=pltpu.VMEM)
    return pl.pallas_call(
        kernel,
        out_shape=(
            jax.ShapeDtypeStruct((R, C), F32),
            jax.ShapeDtypeStruct((SLOTS, 1, J), F32),
        ),
        in_specs=[smem] * 4 + [vmem] * 12,
        out_specs=(vmem, vmem),
        scratch_shapes=[
            pltpu.VMEM((EXT, J, C), BF),
            pltpu.VMEM((SLOTS + 2, J, C), BF),
            pltpu.VMEM((J, C), jnp.int32),
            pltpu.VMEM((J + 2 * PAD, C), F32),
            pltpu.VMEM((MEM, EXT, J, 3 * C), BF),
            pltpu.VMEM((MEM, EXT - 2, J, 3 * C), BF),
            pltpu.VMEM((MEM, EXT - 4, J, 3 * C), BF),
            pltpu.VMEM((MEM, SLOTS, J, C), F32),
            pltpu.VMEM((MEM, EXT - 4, J, C), BF),
            pltpu.VMEM((MEM, SLOTS, J, C), BF),
            pltpu.VMEM((MEM, SLOTS, J, C), BF),
            pltpu.VMEM((2 * C, 4 * 384), F32),
        ],
        compiler_params=pltpu.CompilerParams(vmem_limit_bytes=60 * 1024 * 1024),
        name="ensemble_step",
    )(counts, seeds, place, weights, own, f1, f2, f3, b1, b2, b3, target, amp, w1, w2, wt)


def paired(filt):
    flat = filt.reshape(9 * C, C)
    return jnp.concatenate(
        [jnp.pad(flat, ((0, 3 * C), (0, 0))), jnp.pad(flat, ((3 * C, 0), (0, 0)))], axis=1
    )


def window(field, start):
    wide = jnp.concatenate([field[:, LON - LEFT :], field, field[:, : J - OWN - LEFT]], axis=1)
    return lax.dynamic_slice_in_dim(wide, start, J, 1)


def body(state, target, amp, filt1, filt2, counts, seed):
    band = lax.axis_index("band")
    member = lax.axis_index("member")
    n = counts[band]
    x = band % 4
    core = member % 2
    weights = jnp.asarray(
        np.cos(np.pi * ((np.arange(ROWS_TOTAL) + 0.5) / GRID_ROWS - 0.5)).astype(np.float32)
    )
    seeds = jnp.where(jnp.arange(MEM) == member, seed, 0)
    seeds = seeds + shift(seeds, 4, 1)
    seeds = seeds + shift(seeds, 3, 1)

    own = window(state, member * OWN)
    tgt = window(target, member * OWN)

    def send(value, by):
        pairs = [(i, i + by) for i in range(32) if 0 <= i + by < 32]
        return lax.ppermute(value, "band", pairs)

    padded = jnp.concatenate([jnp.zeros((3, J, C), BF), own], axis=0)
    last3 = lax.dynamic_slice_in_dim(padded, n, 3, 0)
    last_t = lax.dynamic_slice_in_dim(tgt, n - 1, 1, 0)
    f1 = send(jnp.concatenate([last3, last_t], axis=0), 1)
    b1 = send(jnp.concatenate([own[:3], tgt[:1]], axis=0), -1)
    f2 = send(last3[1:], 2)
    b2 = send(own[:2], -2)
    f3 = send(last3[2:], 3)
    b3 = send(own[:1], -3)

    w1 = paired(filt1)
    w2 = paired(filt2)
    wt = paired(jnp.transpose(filt2[::-1, ::-1], (0, 1, 3, 2)))
    place = jnp.stack([band, member]).astype(jnp.int32)
    grads, cells = local_step(
        counts, seeds, place, weights, own, f1, f2, f3, b1, b2, b3, tgt, amp[None], w1, w2, wt
    )

    part = scatter_sum(grads, 4, core)
    part = scatter_sum(part, 2, x)
    part = exchange_sum(part, 1)
    part = exchange_sum(part, 3)
    part = exchange_sum(part, 0)
    part = gather(part, 2, x)
    full = gather(part, 4, core)

    return (
        cells[:, 0, LEFT : LEFT + OWN],
        full[2304, 0],
        full[:1152].reshape(3, 3, C, C),
        full[1152:2304].reshape(3, 3, C, C),
    )


def solution(mesh):
    in_specs = (P("band", None, None), P("band", None, None), P(), P(), P(), P(), P("member"))
    out_specs = (P("band", "member"), P(), P(), P())
    return jax.shard_map(body, mesh=mesh, in_specs=in_specs, out_specs=out_specs, check_vma=False)
```

profile of v0, /device:TPU:1, one launch (start us, length us, event | category | flops | bytes accessed | tf_op | source)
XLA Modules:
  0.0 152.2 jit_solution(7461771881276002946)
XLA Ops:
  2.1 1.2 dynamic_slice.37
  5.9 1.6 %pad_maximum_fusion = bf16[4,1464,128]{2,1,0:T(8,128)(2,1)S(1)} fusion(bf16[4,16,128]{2,1,0:T(8,128)(2,1)S(1)} %slice.45, bf16[4,1440,128]{2,1,0:T(8,128)(2,1)} %param.9, bf16[4,8,128]{2,1,0:T(8,128)(2,1)S(1)} %slice.44), kind=kLoop, calls=%fused_computation.11 | loop fusion | flops 4497408 | bytes 2998272 | tf_op jit(solution)/shard_map/concatenate | solution.py:340
  8.6 1.3 collective-permute-start.5
  10.7 4.6 %collective-permute-start.2 = (bf16[4,384,128]{2,1,0:T(8,128)(2,1)}, bf16[4,384,128]{2,1,0:T(8,128)(2,1)S(1)}, u32[]{:S(2)}, u32[]{:S(2)}) collective-permute-start(bf16[4,384,128]{2,1,0:T(8,128)(2,1)} %pad_maximum_fusion.1), channel_id=1, source_target_pairs={{0,4},{4,8},{8,12},{12,16},{16,20},{20,24},{24,28},{28,32},{32,36}... | collective-permute-start | bytes 1179656 | tf_op jit(solution)/shard_map/ppermute | solution.py:362
  16.1 5.5 %collective-permute-start.3 = (bf16[2,384,128]{2,1,0:T(8,128)(2,1)}, bf16[2,384,128]{2,1,0:T(8,128)(2,1)}, u32[]{:S(2)}, u32[]{:S(2)}) collective-permute-start(bf16[2,384,128]{2,1,0:T(8,128)(2,1)} %get-tuple-element.20), channel_id=1, source_target_pairs={{0,8},{4,12},{8,16},{12,20},{16,24},{20,28},{24,32},{28,36},{32,40... | collective-permute-start | bytes 589832 | tf_op jit(solution)/shard_map/ppermute | solution.py:362
  22.3 3.8 %collective-permute-start.4 = (bf16[1,384,128]{2,1,0:T(8,128)(2,1)}, bf16[1,384,128]{2,1,0:T(8,128)(2,1)}, u32[]{:S(2)}, u32[]{:S(2)}) collective-permute-start(bf16[1,384,128]{2,1,0:T(8,128)(2,1)} %get-tuple-element.18), channel_id=1, source_target_pairs={{0,12},{4,16},{8,20},{12,24},{16,28},{20,32},{24,36},{28,40},{32,4... | collective-permute-start | bytes 294920 | tf_op jit(solution)/shard_map/ppermute | solution.py:362
  26.7 1.9 %collective-permute-start = (s32[4]{0:T(128)S(1)}, s32[4]{0:T(128)S(1)}, u32[]{:S(2)}, u32[]{:S(2)}) collective-permute-start(s32[4]{0:T(128)S(1)} %compare_select_fusion), channel_id=1, source_target_pairs={{0,1},{1,0},{2,3},{3,2},{4,5},{5,4},{6,7},{7,6},{8,9},{9,8},{10,11... | collective-permute-start | bytes 56 | tf_op jit(solution)/shard_map/ppermute | solution.py:47
  31.2 2.3 %fusion.6 = (bf16[1536,256]{1,0:T(8,128)(2,1)}, bf16[1536,256]{1,0:T(8,128)(2,1)}) fusion(bf16[1152,128]{1,0:T(8,128)(2,1)} %bitcast.64, bf16[1152,128]{1,0:T(8,128)(2,1)S(1)} %bitcast.60), kind=kLoop, calls=%fused_computation.15 | loop fusion | flops 5505024 | bytes 2162688 | tf_op jit(solution)/shard_map/concatenate | solution.py:334
  33.5 3.7 %collective-permute-start.1 = (s32[4]{0:T(128)S(1)}, s32[4]{0:T(128)S(1)}, u32[]{:S(2)}, u32[]{:S(2)}) collective-permute-start(s32[4]{0:T(128)S(1)} %fusion.17), channel_id=1, source_target_pairs={{0,2},{1,3},{2,0},{3,1},{4,6},{5,7},{6,4},{7,5},{8,10},{9,11},{10,... | collective-permute-start | bytes 56 | tf_op jit(solution)/shard_map/ppermute | solution.py:47
  38.2 1.3 collective-permute-start.6
  39.5 1.3 collective-permute-start.7
  41.3 9.5 %collective-permute-done.7.bwd3_ref = bf16[1,384,128]{2,1,0:T(8,128)(2,1)S(1)} collective-permute-done((bf16[1,384,128]{2,1,0:T(8,128)(2,1)S(1)}, bf16[1,384,128]{2,1,0:T(8,128)(2,1)S(1)}, u32[]{:S(2)}, u32[]{:S(2)}) %collective-permute-start.7) | collective-permute-done | bytes 98336 | tf_op jit(solution)/shard_map/ppermute | solution.py:362
  51.8 47.4 %ensemble_step.1 = (f32[2368,128]{1,0:T(8,128)}, f32[4,1,384]{2,1,0:T(1,128)}) custom-call(s32[32]{0:T(128)} %counts_ref.1, s32[4]{0:T(128)} %fusion.18.seeds_ref, s32[2]{0:T(128)} %pad_add_fusion.place_ref, f32[96]{0:T(128)} %constant.140.clone.weight_ref, bf16[4,384,128]{2,1,0:T(8,128)(2,1)} %copy-done, bf16[4,384,128]{2,1,0:T(8,128)(2,1)} %copy-done.5, ...), custom_call_target="tpu_custom_call" | custom-call | tf_op jit(solution)/shard_map/ensemble_step/pallas_call | solution.py:305
  99.3 1.2 dynamic-slice_bitcast_fusion
  101.1 1.7 %collective-permute-done.8 = f32[1184,128]{1,0:T(8,128)S(1)} collective-permute-done((f32[1184,128]{1,0:T(8,128)S(1)}, f32[1184,128]{1,0:T(8,128)S(1)}, u32[]{:S(2)}, u32[]{:S(2)}) %collective-permute-start.8) | collective-permute-done | bytes 606240 | tf_op jit(solution)/shard_map/ppermute | solution.py:47
  102.8 3.9 %collective-permute-start.10 = (f32[296,128]{1,0:T(8,128)S(1)}, f32[296,128]{1,0:T(8,128)S(1)}, u32[]{:S(2)}, u32[]{:S(2)}) collective-permute-start(f32[296,128]{1,0:T(8,128)S(1)} %get-tuple-element.16), channel_id=1, source_target_pairs={{0,8},{1,9},{2,10},{3,11},{4,12},{5,13},{6,14},{7,15},{8,0},{9,1},... | collective-permute-start | bytes 454664 | tf_op jit(solution)/shard_map/ppermute | solution.py:47
  108.2 2.5 %collective-permute-done.10 = f32[296,128]{1,0:T(8,128)S(1)} collective-permute-done((f32[296,128]{1,0:T(8,128)S(1)}, f32[296,128]{1,0:T(8,128)S(1)}, u32[]{:S(2)}, u32[]{:S(2)}) %collective-permute-start.10) | collective-permute-done | bytes 151584 | tf_op jit(solution)/shard_map/ppermute | solution.py:47
  110.7 1.5 %collective-permute-done.11 = f32[296,128]{1,0:T(8,128)S(1)} collective-permute-done((f32[296,128]{1,0:T(8,128)S(1)}, f32[296,128]{1,0:T(8,128)S(1)}, u32[]{:S(2)}, u32[]{:S(2)}) %collective-permute-start.11) | collective-permute-done | bytes 151584 | tf_op jit(solution)/shard_map/ppermute | solution.py:47
  112.2 1.4 collective-permute-done.9
  113.7 1.6 %collective-permute-start.12 = (f32[296,128]{1,0:T(8,128)S(1)}, f32[296,128]{1,0:T(8,128)S(1)}, u32[]{:S(2)}, u32[]{:S(2)}) collective-permute-start(f32[296,128]{1,0:T(8,128)S(1)} %fusion.12), channel_id=1, source_target_pairs={{0,16},{1,17},{2,18},{3,19},{4,20},{5,21},{6,22},{7,23},{8,24},{9,... | collective-permute-start | bytes 454664 | tf_op jit(solution)/shard_map/ppermute | solution.py:47
  115.3 4.1 %collective-permute-start.13 = (f32[296,128]{1,0:T(8,128)S(1)}, f32[296,128]{1,0:T(8,128)S(1)}, u32[]{:S(2)}, u32[]{:S(2)}) collective-permute-start(f32[296,128]{1,0:T(8,128)S(1)} %fusion.12), channel_id=1, source_target_pairs={{0,32},{1,33},{2,34},{3,35},{4,36},{5,37},{6,38},{7,39},{8,40},{9,... | collective-permute-start | bytes 454664 | tf_op jit(solution)/shard_map/ppermute | solution.py:47
  120.0 1.2 collective-permute-done.12
  121.2 3.8 %collective-permute-done.13 = f32[296,128]{1,0:T(8,128)S(1)} collective-permute-done((f32[296,128]{1,0:T(8,128)S(1)}, f32[296,128]{1,0:T(8,128)S(1)}, u32[]{:S(2)}, u32[]{:S(2)}) %collective-permute-start.13) | collective-permute-done | bytes 151584 | tf_op jit(solution)/shard_map/ppermute | solution.py:47
  125.5 3.3 %collective-permute-start.15 = (f32[296,128]{1,0:T(8,128)S(1)}, f32[296,128]{1,0:T(8,128)S(1)}, u32[]{:S(2)}, u32[]{:S(2)}) collective-permute-start(f32[296,128]{1,0:T(8,128)S(1)} %add_add_fusion), channel_id=1, source_target_pairs={{0,2},{1,3},{2,0},{3,1},{4,6},{5,7},{6,4},{7,5},{8,10},{9,11},{10,... | collective-permute-start | bytes 454664 | tf_op jit(solution)/shard_map/ppermute | solution.py:47
  128.8 2.6 %collective-permute-done.15 = f32[296,128]{1,0:T(8,128)S(1)} collective-permute-done((f32[296,128]{1,0:T(8,128)S(1)}, f32[296,128]{1,0:T(8,128)S(1)}, u32[]{:S(2)}, u32[]{:S(2)}) %collective-permute-start.15) | collective-permute-done | bytes 151584 | tf_op jit(solution)/shard_map/ppermute | solution.py:47
  131.4 1.5 collective-permute-start.16
  132.9 3.3 %collective-permute-done.16 = f32[296,128]{1,0:T(8,128)S(1)} collective-permute-done((f32[296,128]{1,0:T(8,128)S(1)}, f32[296,128]{1,0:T(8,128)S(1)}, u32[]{:S(2)}, u32[]{:S(2)}) %collective-permute-start.16) | collective-permute-done | bytes 151584 | tf_op jit(solution)/shard_map/ppermute | solution.py:47
  136.4 3.1 %collective-permute-start.18 = (f32[296,128]{1,0:T(8,128)S(1)}, f32[296,128]{1,0:T(8,128)S(1)}, u32[]{:S(2)}, u32[]{:S(2)}) collective-permute-start(f32[296,128]{1,0:T(8,128)S(1)} %get-tuple-element.9), channel_id=1, source_target_pairs={{0,8},{1,9},{2,10},{3,11},{4,12},{5,13},{6,14},{7,15},{8,0},{9,1},... | collective-permute-start | bytes 454664 | tf_op jit(solution)/shard_map/ppermute | solution.py:47
  139.6 1.9 %collective-permute-start.19 = (f32[296,128]{1,0:T(8,128)S(1)}, f32[296,128]{1,0:T(8,128)S(1)}, u32[]{:S(2)}, u32[]{:S(2)}) collective-permute-start(f32[296,128]{1,0:T(8,128)S(1)} %get-tuple-element.9), channel_id=1, source_target_pairs={{0,12},{1,13},{2,14},{3,15},{4,0},{5,1},{6,2},{7,3},{8,4},{9,5},{1... | collective-permute-start | bytes 454664 | tf_op jit(solution)/shard_map/ppermute | solution.py:47
  141.6 2.0 %collective-permute-done.18 = f32[296,128]{1,0:T(8,128)S(1)} collective-permute-done((f32[296,128]{1,0:T(8,128)S(1)}, f32[296,128]{1,0:T(8,128)S(1)}, u32[]{:S(2)}, u32[]{:S(2)}) %collective-permute-start.18) | collective-permute-done | bytes 151584 | tf_op jit(solution)/shard_map/ppermute | solution.py:47
  143.8 5.1 %collective-permute-start.20 = (f32[1184,128]{1,0:T(8,128)S(1)}, f32[1184,128]{1,0:T(8,128)S(1)}, u32[]{:S(2)}, u32[]{:S(2)}) collective-permute-start(f32[1184,128]{1,0:T(8,128)S(1)} %bitcast.54), channel_id=1, source_target_pairs={{0,1},{1,0},{2,3},{3,2},{4,5},{5,4},{6,7},{7,6},{8,9},{9,8},{10,11... | collective-permute-start | bytes 1818632 | tf_op jit(solution)/shard_map/ppermute | solution.py:47
  150.6 1.1 fusion.13
  (73 shorter events, 15.0 us)
Async XLA Ops:
  5.9 2.3 %copy-start.1 = (bf16[4,1440,128]{2,1,0:T(8,128)(2,1)S(1)}, bf16[4,1440,128]{2,1,0:T(8,128)(2,1)}, u32[]{:S(2)}) copy-start(bf16[4,1440,128]{2,1,0:T(8,128)(2,1)} %param.8) | copy-start | bytes 4423684
  5.9 2.3 %slice-start = ((bf16[4,1440,128]{2,1,0:T(8,128)(2,1)}), bf16[4,16,128]{2,1,0:T(8,128)(2,1)S(1)}, s32[]{:S(2)}) async-start(bf16[4,1440,128]{2,1,0:T(8,128)(2,1)} %param.8), calls=%async_computation | async-start | bytes 32768 | tf_op jit(solution)/shard_map/slice | solution.py:340
  5.9 2.3 %slice-start.1 = ((bf16[4,1440,128]{2,1,0:T(8,128)(2,1)}), bf16[4,8,128]{2,1,0:T(8,128)(2,1)S(1)}, s32[]{:S(2)}) async-start(bf16[4,1440,128]{2,1,0:T(8,128)(2,1)} %param.8), calls=%async_computation.1 | async-start | bytes 16384 | tf_op jit(solution)/shard_map/slice | solution.py:340
  8.4 13.2 %copy-start = (bf16[4,384,128]{2,1,0:T(8,128)(2,1)}, bf16[4,384,128]{2,1,0:T(8,128)(2,1)S(1)}, u32[]{:S(2)}) copy-start(bf16[4,384,128]{2,1,0:T(8,128)(2,1)S(1)} %fusion.10.own_ref) | copy-start | bytes 1179652
  8.6 42.3 %collective-permute-start.5 = (bf16[4,384,128]{2,1,0:T(8,128)(2,1)S(1)}, bf16[4,384,128]{2,1,0:T(8,128)(2,1)S(1)}, u32[]{:S(2)}, u32[]{:S(2)}) collective-permute-start(bf16[4,384,128]{2,1,0:T(8,128)(2,1)S(1)} %pad_maximum_fusion.2), channel_id=1, source_target_pairs={{4,0},{8,4},{12,8},{16,12},{20,16},{24,20},{28,24},{32,28},{36,32}... | collective-permute-start | bytes 1179656 | tf_op jit(solution)/shard_map/ppermute | solution.py:362
  9.9 19.4 %copy-start.3 = (bf16[3,3,128,128]{3,2,1,0:T(8,128)(2,1)S(1)}, bf16[3,3,128,128]{3,2,1,0:T(8,128)(2,1)}, u32[]{:S(2)}) copy-start(bf16[3,3,128,128]{3,2,1,0:T(8,128)(2,1)} %param.12) | copy-start | bytes 884740
  10.7 40.2 %collective-permute-start.2 = (bf16[4,384,128]{2,1,0:T(8,128)(2,1)}, bf16[4,384,128]{2,1,0:T(8,128)(2,1)S(1)}, u32[]{:S(2)}, u32[]{:S(2)}) collective-permute-start(bf16[4,384,128]{2,1,0:T(8,128)(2,1)} %pad_maximum_fusion.1), channel_id=1, source_target_pairs={{0,4},{4,8},{8,12},{12,16},{16,20},{20,24},{24,28},{28,32},{32,36}... | collective-permute-start | bytes 1179656 | tf_op jit(solution)/shard_map/ppermute | solution.py:362
  16.1 34.8 %collective-permute-start.3 = (bf16[2,384,128]{2,1,0:T(8,128)(2,1)}, bf16[2,384,128]{2,1,0:T(8,128)(2,1)}, u32[]{:S(2)}, u32[]{:S(2)}) collective-permute-start(bf16[2,384,128]{2,1,0:T(8,128)(2,1)} %get-tuple-element.20), channel_id=1, source_target_pairs={{0,8},{4,12},{8,16},{12,20},{16,24},{20,28},{24,32},{28,36},{32,40... | collective-permute-start | bytes 589832 | tf_op jit(solution)/shard_map/ppermute | solution.py:362
  22.3 17.2 %collective-permute-start.4 = (bf16[1,384,128]{2,1,0:T(8,128)(2,1)}, bf16[1,384,128]{2,1,0:T(8,128)(2,1)}, u32[]{:S(2)}, u32[]{:S(2)}) collective-permute-start(bf16[1,384,128]{2,1,0:T(8,128)(2,1)} %get-tuple-element.18), channel_id=1, source_target_pairs={{0,12},{4,16},{8,20},{12,24},{16,28},{20,32},{24,36},{28,40},{32,4... | collective-permute-start | bytes 294920 | tf_op jit(solution)/shard_map/ppermute | solution.py:362
  26.7 6.8 %collective-permute-start = (s32[4]{0:T(128)S(1)}, s32[4]{0:T(128)S(1)}, u32[]{:S(2)}, u32[]{:S(2)}) collective-permute-start(s32[4]{0:T(128)S(1)} %compare_select_fusion), channel_id=1, source_target_pairs={{0,1},{1,0},{2,3},{3,2},{4,5},{5,4},{6,7},{7,6},{8,9},{9,8},{10,11... | collective-permute-start | bytes 56 | tf_op jit(solution)/shard_map/ppermute | solution.py:47
  29.6 8.6 %copy-start.7 = (bf16[2,384,128]{2,1,0:T(8,128)(2,1)S(1)}, bf16[2,384,128]{2,1,0:T(8,128)(2,1)}, u32[]{:S(2)}) copy-start(bf16[2,384,128]{2,1,0:T(8,128)(2,1)} %get-tuple-element.19) | copy-start | bytes 589828
  33.5 4.7 %collective-permute-start.1 = (s32[4]{0:T(128)S(1)}, s32[4]{0:T(128)S(1)}, u32[]{:S(2)}, u32[]{:S(2)}) collective-permute-start(s32[4]{0:T(128)S(1)} %fusion.17), channel_id=1, source_target_pairs={{0,2},{1,3},{2,0},{3,1},{4,6},{5,7},{6,4},{7,5},{8,10},{9,11},{10,... | collective-permute-start | bytes 56 | tf_op jit(solution)/shard_map/ppermute | solution.py:47
  38.2 12.7 %collective-permute-start.6 = (bf16[2,384,128]{2,1,0:T(8,128)(2,1)S(1)}, bf16[2,384,128]{2,1,0:T(8,128)(2,1)S(1)}, u32[]{:S(2)}, u32[]{:S(2)}) collective-permute-start(bf16[2,384,128]{2,1,0:T(8,128)(2,1)S(1)} %copy-done.7), channel_id=1, source_target_pairs={{8,0},{12,4},{16,8},{20,12},{24,16},{28,20},{32,24},{36,28},{40,32... | collective-permute-start | bytes 589832 | tf_op jit(solution)/shard_map/ppermute | solution.py:362
  39.5 11.4 %collective-permute-start.7 = (bf16[1,384,128]{2,1,0:T(8,128)(2,1)S(1)}, bf16[1,384,128]{2,1,0:T(8,128)(2,1)S(1)}, u32[]{:S(2)}, u32[]{:S(2)}) collective-permute-start(bf16[1,384,128]{2,1,0:T(8,128)(2,1)S(1)} %get-tuple-element.17), channel_id=1, source_target_pairs={{12,0},{16,4},{20,8},{24,12},{28,16},{32,20},{36,24},{40,28},{44,3... | collective-permute-start | bytes 294920 | tf_op jit(solution)/shard_map/ppermute | solution.py:362
  50.9 0.7 copy-start.6
  50.9 0.8 copy-start.4
  50.9 0.9 copy-start.5
  99.3 3.5 %copy-start.2 = (f32[2368,128]{1,0:T(8,128)S(1)}, f32[2368,128]{1,0:T(8,128)}, u32[]{:S(2)}) copy-start(f32[2368,128]{1,0:T(8,128)} %get-tuple-element.7) | copy-start | bytes 3637252
  100.5 2.2 %collective-permute-start.8 = (f32[1184,128]{1,0:T(8,128)S(1)}, f32[1184,128]{1,0:T(8,128)S(1)}, u32[]{:S(2)}, u32[]{:S(2)}) collective-permute-start(f32[1184,128]{1,0:T(8,128)S(1)} %dynamic-slice_bitcast_fusion), channel_id=1, source_target_pairs={{0,1},{1,0},{2,3},{3,2},{4,5},{5,4},{6,7},{7,6},{8,9},{9,8},{10,11... | collective-permute-start | bytes 1818632 | tf_op jit(solution)/shard_map/ppermute | solution.py:47
  102.8 7.9 %collective-permute-start.10 = (f32[296,128]{1,0:T(8,128)S(1)}, f32[296,128]{1,0:T(8,128)S(1)}, u32[]{:S(2)}, u32[]{:S(2)}) collective-permute-start(f32[296,128]{1,0:T(8,128)S(1)} %get-tuple-element.16), channel_id=1, source_target_pairs={{0,8},{1,9},{2,10},{3,11},{4,12},{5,13},{6,14},{7,15},{8,0},{9,1},... | collective-permute-start | bytes 454664 | tf_op jit(solution)/shard_map/ppermute | solution.py:47
  106.8 5.5 %collective-permute-start.11 = (f32[296,128]{1,0:T(8,128)S(1)}, f32[296,128]{1,0:T(8,128)S(1)}, u32[]{:S(2)}, u32[]{:S(2)}) collective-permute-start(f32[296,128]{1,0:T(8,128)S(1)} %get-tuple-element.15), channel_id=1, source_target_pairs={{0,12},{1,13},{2,14},{3,15},{4,0},{5,1},{6,2},{7,3},{8,4},{9,5},{1... | collective-permute-start | bytes 454664 | tf_op jit(solution)/shard_map/ppermute | solution.py:47
  107.7 6.0 %collective-permute-start.9 = (f32[296,128]{1,0:T(8,128)S(1)}, f32[296,128]{1,0:T(8,128)S(1)}, u32[]{:S(2)}, u32[]{:S(2)}) collective-permute-start(f32[296,128]{1,0:T(8,128)S(1)} %get-tuple-element.14), channel_id=1, source_target_pairs={{0,4},{1,5},{2,6},{3,7},{4,8},{5,9},{6,10},{7,11},{8,12},{9,13},{1... | collective-permute-start | bytes 454664 | tf_op jit(solution)/shard_map/ppermute | solution.py:47
  113.7 7.5 %collective-permute-start.12 = (f32[296,128]{1,0:T(8,128)S(1)}, f32[296,128]{1,0:T(8,128)S(1)}, u32[]{:S(2)}, u32[]{:S(2)}) collective-permute-start(f32[296,128]{1,0:T(8,128)S(1)} %fusion.12), channel_id=1, source_target_pairs={{0,16},{1,17},{2,18},{3,19},{4,20},{5,21},{6,22},{7,23},{8,24},{9,... | collective-permute-start | bytes 454664 | tf_op jit(solution)/shard_map/ppermute | solution.py:47
  115.3 9.7 %collective-permute-start.13 = (f32[296,128]{1,0:T(8,128)S(1)}, f32[296,128]{1,0:T(8,128)S(1)}, u32[]{:S(2)}, u32[]{:S(2)}) collective-permute-start(f32[296,128]{1,0:T(8,128)S(1)} %fusion.12), channel_id=1, source_target_pairs={{0,32},{1,33},{2,34},{3,35},{4,36},{5,37},{6,38},{7,39},{8,40},{9,... | collective-permute-start | bytes 454664 | tf_op jit(solution)/shard_map/ppermute | solution.py:47
  119.5 6.0 %collective-permute-start.14 = (f32[296,128]{1,0:T(8,128)S(1)}, f32[296,128]{1,0:T(8,128)S(1)}, u32[]{:S(2)}, u32[]{:S(2)}) collective-permute-start(f32[296,128]{1,0:T(8,128)S(1)} %fusion.12), channel_id=1, source_target_pairs={{0,48},{1,49},{2,50},{3,51},{4,52},{5,53},{6,54},{7,55},{8,56},{9,... | collective-permute-start | bytes 454664 | tf_op jit(solution)/shard_map/ppermute | solution.py:47
  125.5 23.4 %copy-start.9 = (f32[4,1,384]{2,1,0:T(1,128)S(1)}, f32[4,1,384]{2,1,0:T(1,128)}, u32[]{:S(2)}) copy-start(f32[4,1,384]{2,1,0:T(1,128)} %get-tuple-element.6) | copy-start | bytes 18436
  125.5 5.9 %collective-permute-start.15 = (f32[296,128]{1,0:T(8,128)S(1)}, f32[296,128]{1,0:T(8,128)S(1)}, u32[]{:S(2)}, u32[]{:S(2)}) collective-permute-start(f32[296,128]{1,0:T(8,128)S(1)} %add_add_fusion), channel_id=1, source_target_pairs={{0,2},{1,3},{2,0},{3,1},{4,6},{5,7},{6,4},{7,5},{8,10},{9,11},{10,... | collective-permute-start | bytes 454664 | tf_op jit(solution)/shard_map/ppermute | solution.py:47
  131.4 4.8 %collective-permute-start.16 = (f32[296,128]{1,0:T(8,128)S(1)}, f32[296,128]{1,0:T(8,128)S(1)}, u32[]{:S(2)}, u32[]{:S(2)}) collective-permute-start(f32[296,128]{1,0:T(8,128)S(1)} %add.178), channel_id=1, source_target_pairs={{0,64},{1,65},{2,66},{3,67},{4,68},{5,69},{6,70},{7,71},{8,72},{9,... | collective-permute-start | bytes 454664 | tf_op jit(solution)/shard_map/ppermute | solution.py:47
  136.3 5.3 %collective-permute-start.17 = (f32[296,128]{1,0:T(8,128)S(1)}, f32[296,128]{1,0:T(8,128)S(1)}, u32[]{:S(2)}, u32[]{:S(2)}) collective-permute-start(f32[296,128]{1,0:T(8,128)S(1)} %get-tuple-element.9), channel_id=1, source_target_pairs={{0,4},{1,5},{2,6},{3,7},{4,8},{5,9},{6,10},{7,11},{8,12},{9,13},{1... | collective-permute-start | bytes 454664 | tf_op jit(solution)/shard_map/ppermute | solution.py:47
  136.4 7.2 %collective-permute-start.18 = (f32[296,128]{1,0:T(8,128)S(1)}, f32[296,128]{1,0:T(8,128)S(1)}, u32[]{:S(2)}, u32[]{:S(2)}) collective-permute-start(f32[296,128]{1,0:T(8,128)S(1)} %get-tuple-element.9), channel_id=1, source_target_pairs={{0,8},{1,9},{2,10},{3,11},{4,12},{5,13},{6,14},{7,15},{8,0},{9,1},... | collective-permute-start | bytes 454664 | tf_op jit(solution)/shard_map/ppermute | solution.py:47
  139.6 4.2 %collective-permute-start.19 = (f32[296,128]{1,0:T(8,128)S(1)}, f32[296,128]{1,0:T(8,128)S(1)}, u32[]{:S(2)}, u32[]{:S(2)}) collective-permute-start(f32[296,128]{1,0:T(8,128)S(1)} %get-tuple-element.9), channel_id=1, source_target_pairs={{0,12},{1,13},{2,14},{3,15},{4,0},{5,1},{6,2},{7,3},{8,4},{9,5},{1... | collective-permute-start | bytes 454664 | tf_op jit(solution)/shard_map/ppermute | solution.py:47
  143.8 6.7 %collective-permute-start.20 = (f32[1184,128]{1,0:T(8,128)S(1)}, f32[1184,128]{1,0:T(8,128)S(1)}, u32[]{:S(2)}, u32[]{:S(2)}) collective-permute-start(f32[1184,128]{1,0:T(8,128)S(1)} %bitcast.54), channel_id=1, source_target_pairs={{0,1},{1,0},{2,3},{3,2},{4,5},{5,4},{6,7},{7,6},{8,9},{9,8},{10,11... | collective-permute-start | bytes 1818632 | tf_op jit(solution)/shard_map/ppermute | solution.py:47
  (1 other events, 0.6 us)
where the time goes:
time: 153 us; the launch traced here: 152 us
  starting transfers between devices  50.5 us (33%)
  Pallas kernels  47.4 us (31%)
  waiting for transfers between devices  32.1 us (21%)
  local copies, waits for them, and re-layouts  10 us (7%)
  other arithmetic  7.25 us (5%)
  between operations  4.88 us (3%)
    pallas_call x1, Pallas kernels, local_step(): pl.pallas_call(kernel, out_shape=(jax.ShapeDtypeStruct((R, C), F32), jax....  47.4 us
    ppermute x15, starting transfers between devices, shift(): return lax.ppermute(value, BM, pairs)  32.8 us
    ppermute x15, waiting for transfers between devices, shift(): return lax.ppermute(value, BM, pairs)  22.6 us
    ppermute x6, starting transfers between devices, send(): return lax.ppermute(value, 'band', pairs)  17.7 us
    ppermute x6, waiting for transfers between devices, send(): return lax.ppermute(value, 'band', pairs)  9.54 us
    concatenate x2, other arithmetic, paired(): jnp.concatenate([jnp.pad(flat, ((0, 3 * C), (0, 0))), jnp.pad(flat, ((3 *...  3.29 us
  transfers between devices with their start and end apart: 21, of which 15 were waited for; matrix products, arithmetic and copies ran while one was open for 6% of the time, Pallas kernels for 0%

commit v1 on v0

--- a/solution.py
+++ b/solution.py
@@ -9,6 +9,7 @@
 from jax.sharding import PartitionSpec as P
 
 GRID_ROWS = 721
+HALF = 720
 ROWS_TOTAL = 96
 SMOOTH = 0.01
 LON = 1440
@@ -21,6 +22,7 @@
 DEPTH = 3
 EXT = SLOTS + 2 * DEPTH
 PAD = 8
+W = 752
 R = 2368
 BF = jnp.bfloat16
 F32 = jnp.float32
@@ -78,67 +80,125 @@
 
 
 def sigmoid(a):
-    return 1.0 / (1.0 + jnp.exp(-a))
+    return 0.5 * jnp.tanh(0.5 * a) + 0.5
+
+
+def chip_row(half, src, r, dst, sem):
+    cut = LON - (HALF - LEFT)
+    left = [
+        pltpu.make_async_copy(src.at[r, pl.ds(LON - LEFT, LEFT)], dst.at[pl.ds(0, LEFT)], sem.at[0]),
+        pltpu.make_async_copy(
+            src.at[r, pl.ds(0, W - LEFT)], dst.at[pl.ds(LEFT, W - LEFT)], sem.at[1]
+        ),
+    ]
+    right = [
+        pltpu.make_async_copy(src.at[r, pl.ds(HALF - LEFT, cut)], dst.at[pl.ds(0, cut)], sem.at[0]),
+        pltpu.make_async_copy(src.at[r, pl.ds(0, W - cut)], dst.at[pl.ds(cut, W - cut)], sem.at[1]),
+    ]
+    return [(half == 0, left), (half == 1, right)]
+
+
+def own_window(quarter, src, dst, sem):
+    cut = LON - (3 * OWN - LEFT)
+    middle = pl.multiple_of(quarter * OWN - LEFT, 8)
+    first = [
+        pltpu.make_async_copy(
+            src.at[:, pl.ds(LON - LEFT, LEFT)], dst.at[:, pl.ds(0, LEFT)], sem.at[0]
+        ),
+        pltpu.make_async_copy(
+            src.at[:, pl.ds(0, J - LEFT)], dst.at[:, pl.ds(LEFT, J - LEFT)], sem.at[1]
+        ),
+    ]
+    inner = [pltpu.make_async_copy(src.at[:, pl.ds(middle, J)], dst, sem.at[0])]
+    last = [
+        pltpu.make_async_copy(
+            src.at[:, pl.ds(3 * OWN - LEFT, cut)], dst.at[:, pl.ds(0, cut)], sem.at[0]
+        ),
+        pltpu.make_async_copy(
+            src.at[:, pl.ds(0, J - cut)], dst.at[:, pl.ds(cut, J - cut)], sem.at[1]
+        ),
+    ]
+    return [(quarter == 0, first), ((quarter == 1) | (quarter == 2), inner), (quarter == 3, last)]
+
+
+def start(cases):
+    for cond, copies in cases:
+
+        @pl.when(cond)
+        def _():
+            for c in copies:
+                c.start()
+
+
+def wait(cases):
+    for cond, copies in cases:
+
+        @pl.when(cond)
+        def _():
+            for c in copies:
+                c.wait()
+
+
+def edge_kernel(counts_ref, place_ref, state_ref, target_ref, send_ref, second_ref, third_ref, flag_ref, sem):
+    n = counts_ref[place_ref[0]]
+    member = place_ref[1]
+    half, core = member // 2, member % 2
+    row = lambda k: jnp.where(core == 0, jnp.maximum(n - 1 - k, 0), k)
+    cases = (
+        chip_row(half, state_ref, row(0), send_ref.at[0], sem.at[0])
+        + chip_row(half, target_ref, row(0), send_ref.at[1], sem.at[1])
+        + chip_row(half, state_ref, row(1), second_ref.at[0], sem.at[2])
+        + chip_row(half, state_ref, row(2), third_ref.at[0], sem.at[3])
+    )
+    start(cases)
+    ones = jnp.ones((1, C), F32)
+    flag_ref[0:1] = ones * (n >= 2).astype(F32)
+    flag_ref[1:2] = ones * (n >= 3).astype(F32)
+    flag_ref[2:3] = ones * (n == 2).astype(F32)
+    flag_ref[3:8] = jnp.zeros((5, C), F32)
+    wait(cases)
+
+
+def edges(counts, place, state, target):
+    smem = pl.BlockSpec(memory_space=pltpu.SMEM)
+    vmem = pl.BlockSpec(memory_space=pltpu.VMEM)
+    hbm = pl.BlockSpec(memory_space=pl.ANY)
+    row = jax.ShapeDtypeStruct((1, W, C), BF)
+    return pl.pallas_call(
+        edge_kernel,
+        out_shape=(jax.ShapeDtypeStruct((2, W, C), BF), row, row, jax.ShapeDtypeStruct((8, C), F32)),
+        in_specs=[smem, smem, hbm, hbm],
+        out_specs=(vmem,) * 4,
+        scratch_shapes=[pltpu.SemaphoreType.DMA((4, 2))],
+        name="edge_rows",
+    )(counts, place, state, target)
 
 
 def kernel(
     counts_ref, seeds_ref, place_ref, weight_ref,
-    own_ref, fwd1_ref, fwd2_ref, fwd3_ref, bwd1_ref, bwd2_ref, bwd3_ref,
-    target_ref, amp_ref, w1_ref, w2_ref, wt_ref,
+    state_ref, target_ref, r1_ref, r2_ref, r3_ref, other_ref,
+    amp_ref, w1_ref, w2_ref, wt_ref,
     grads_ref, cells_ref,
-    state_s, tgt_s, hash_s, buf_s, in3_s, hid3_s, cot3_s, pre_s, fc_s, ya_s, yb_s, acc_s,
+    state_s, tgt_s, mine_s, hash_s, buf_s, cbuf_s, crps_s,
+    in3_s, hid3_s, cot3_s, pre_s, fc_s, ya_s, yb_s, acc_s, sem,
 ):
     band = place_ref[0]
     quarter = place_ref[1]
+    core = quarter % 2
     n = counts_ref[band]
-
-    def count(b):
-        inside = (b >= 0) & (b < 32)
-        return jnp.where(inside, counts_ref[jnp.clip(b, 0, 31)], 4)
-
     offset = lax.fori_loop(0, band, lambda b, s: s + counts_ref[b], jnp.int32(0))
-    up1, up2 = count(band - 1), count(band - 2)
-    dn1, dn2 = count(band + 1), count(band + 2)
-
-    state_s[DEPTH : DEPTH + SLOTS] = own_ref[...]
-    state_s[2] = fwd1_ref[2]
-
-    def pick(dst, cond, a, b):
-        @pl.when(cond)
-        def _():
-            state_s[dst] = a()
-
-        @pl.when(jnp.logical_not(cond))
-        def _():
-            state_s[dst] = b()
-
-    pick(1, up1 >= 2, lambda: fwd1_ref[1], lambda: fwd2_ref[1])
-    pick(0, up2 >= 2, lambda: fwd2_ref[0], lambda: fwd3_ref[0])
-
-    @pl.when(up1 == 2)
-    def _():
-        state_s[0] = fwd2_ref[1]
-
-    @pl.when(up1 >= 3)
-    def _():
-        state_s[0] = fwd1_ref[0]
-
-    below = DEPTH + n
-    state_s[below] = bwd1_ref[0]
-    pick(below + 1, dn1 >= 2, lambda: bwd1_ref[1], lambda: bwd2_ref[0])
-    pick(below + 2, dn2 >= 2, lambda: bwd2_ref[1], lambda: bwd3_ref[0])
-
-    @pl.when(dn1 == 2)
-    def _():
-        state_s[below + 2] = bwd2_ref[0]
-
-    @pl.when(dn1 >= 3)
-    def _():
-        state_s[below + 2] = bwd1_ref[2]
-
-    tgt_s[1 : 1 + SLOTS] = target_ref[...]
-    tgt_s[0] = fwd1_ref[3]
-    tgt_s[1 + n] = bwd1_ref[3]
+
+    copies = own_window(quarter, state_ref, state_s.at[pl.ds(DEPTH, SLOTS)], sem.at[0])
+    copies += own_window(quarter, target_ref, tgt_s.at[pl.ds(1, SLOTS)], sem.at[1])
+    lane0 = pl.multiple_of(core * OWN, 8)
+    near = [
+        pltpu.make_async_copy(r1_ref.at[:, pl.ds(lane0, J)], mine_s.at[pl.ds(0, 2)], sem.at[2, 0]),
+        pltpu.make_async_copy(r2_ref.at[:, pl.ds(lane0, J)], mine_s.at[pl.ds(2, 1)], sem.at[2, 1]),
+        pltpu.make_async_copy(r3_ref.at[:, pl.ds(lane0, J)], mine_s.at[pl.ds(3, 1)], sem.at[3, 0]),
+    ]
+    start(copies)
+    for c in near:
+        c.start()
 
     buf_s[0:PAD] = jnp.zeros((PAD, C), F32)
     buf_s[PAD + J :] = jnp.zeros((PAD, C), F32)
@@ -150,6 +210,26 @@
     hash_s[...] = lon * 668265263 + chan * 1274126177
     own_col = ((cols >= LEFT) & (cols < LEFT + OWN)).astype(F32)
 
+    wait(copies)
+    for c in near:
+        c.wait()
+
+    def put_edges(above, below):
+        for slot, k in ((2, 0), (1, 2), (0, 3)):
+            state_s[slot] = above[k]
+        for slot, k in ((0, 0), (1, 2), (2, 3)):
+            state_s[DEPTH + n + slot] = below[k]
+        tgt_s[0] = above[1]
+        tgt_s[1 + n] = below[1]
+
+    @pl.when(core == 0)
+    def _():
+        put_edges(mine_s, other_ref)
+
+    @pl.when(core == 1)
+    def _():
+        put_edges(other_ref, mine_s)
+
     def valid(e):
         g = offset - DEPTH + e
         return ((g >= 0) & (g < ROWS_TOTAL)).astype(F32)
@@ -162,16 +242,27 @@
 
     amp = amp_ref[...]
 
+    amp_step = amp * (1.0 / 32768.0)
+    amp_base = amp * (0.5 / 32768.0 - 1.0)
+
     def make_inputs(i, _):
         e, m = i // MEM, i % MEM
-        base = (offset - DEPTH + e) * 374761393 + seeds_ref[m] * 1103515245
-        h = hash_s[...] + base
-        h = h ^ (h >> 13)
-        h = h * 1274126177
-        h = h ^ (h >> 16)
-        noise = (h & 65535).astype(F32) * (1.0 / 32768.0) + (0.5 / 32768.0 - 1.0)
-        v = (state_s[e].astype(F32) + amp * noise) * valid(e)
-        put3(in3_s, m, e, v)
+        g = offset - DEPTH + e
+        inside = (g >= 0) & (g < ROWS_TOTAL)
+
+        @pl.when(inside)
+        def _():
+            h = hash_s[...] + (g * 374761393 + seeds_ref[m] * 1103515245)
+            h = h ^ (h >> 13)
+            h = h * 1274126177
+            h = h ^ (h >> 16)
+            v = (state_s[e].astype(F32) + amp_base) + (h & 65535).astype(F32) * amp_step
+            put3(in3_s, m, e, v)
+
+        @pl.when(jnp.logical_not(inside))
+        def _():
+            in3_s[m, e] = jnp.zeros((J, 3 * C), BF)
+
         return 0
 
     lax.fori_loop(0, EXT * MEM, make_inputs, 0)
@@ -210,49 +301,65 @@
     pair_scale = 1.0 / (MEM * (MEM - 1))
     factor = 1.0 / math.sqrt(ROWS_TOTAL * LON)
 
+    step = 32
+
     def make_crps(r, loss):
         e = r + 2
         g = jnp.clip(offset - DEPTH + e, 0, ROWS_TOTAL - 1)
         weight = weight_ref[g] * valid(e)
         mine = ((r >= 1) & (r < 1 + n)).astype(F32)
-        t = tgt_s[r].astype(F32)
-        f = [fc_s[m, r].astype(F32) for m in range(MEM)]
-        skill = jnp.zeros_like(t)
-        spread = jnp.zeros_like(t)
-        slopes = []
-        for m in range(MEM):
-            d = f[m] - t
-            q = d * d + SMOOTH
-            inv = lax.rsqrt(q)
-            skill = skill + q * inv
-            slopes.append(d * inv * (1.0 / MEM))
-        for a in range(MEM):
-            for b in range(a + 1, MEM):
-                d = f[a] - f[b]
+        scale = weight * (factor * pair_scale)
+        slot = jnp.clip(r - 1, 0, SLOTS - 1)
+
+        def chunk(k, _):
+            at = pl.ds(pl.multiple_of(k * step, step), step)
+            t = tgt_s[r, at].astype(F32)
+            f = [fc_s[m, r, at].astype(F32) for m in range(MEM)]
+            skill = None
+            spread = None
+            slopes = []
+            for m in range(MEM):
+                d = f[m] - t
                 q = d * d + SMOOTH
                 inv = lax.rsqrt(q)
-                spread = spread + q * inv
-                tilt = d * inv * pair_scale
-                slopes[a] = slopes[a] - tilt
-                slopes[b] = slopes[b] + tilt
-        crps = skill * (1.0 / MEM) - spread * pair_scale
+                skill = q * inv if skill is None else skill + q * inv
+                slopes.append(d * inv * (MEM - 1.0))
+            for a in range(MEM):
+                for b in range(a + 1, MEM):
+                    d = f[a] - f[b]
+                    q = d * d + SMOOTH
+                    inv = lax.rsqrt(q)
+                    spread = q * inv if spread is None else spread + q * inv
+                    tilt = d * inv
+                    slopes[a] = slopes[a] - tilt
+                    slopes[b] = slopes[b] + tilt
+            crps_s[at] = (skill * (MEM - 1.0) - spread) * pair_scale
+            for m in range(MEM):
+                cbuf_s[m, pl.ds(pl.multiple_of(PAD + k * step, 8), step)] = slopes[m] * scale
+            return 0
+
+        lax.fori_loop(0, J // step, chunk, 0)
         for m in range(MEM):
-            v = slopes[m] * (weight * factor)
-            put3(cot3_s, m, r, v)
-
-            @pl.when((r >= 1) & (r < 1 + SLOTS))
-            def _():
-                ya_s[m, r - 1] = (v * (own_col * mine)).astype(BF)
-
-        cell = jnp.sum(jnp.transpose(crps), axis=0, keepdims=True) * (weight * mine / C)
+            mid = cbuf_s[m, PAD : PAD + J]
+            cot3_s[m, r, :, C : 2 * C] = mid.astype(BF)
+            cot3_s[m, r, :, 0:C] = cbuf_s[m, PAD - 1 : PAD - 1 + J].astype(BF)
+            cot3_s[m, r, :, 2 * C :] = cbuf_s[m, PAD + 1 : PAD + 1 + J].astype(BF)
 
         @pl.when((r >= 1) & (r < 1 + SLOTS))
         def _():
-            cells_ref[r - 1] = cell
-
-        return loss + cell
-
-    loss = lax.fori_loop(0, SLOTS + 2, make_crps, jnp.zeros((1, J), F32))
+            for m in range(MEM):
+                ya_s[m, slot] = (cbuf_s[m, PAD : PAD + J] * (own_col * mine)).astype(BF)
+            cells_ref[slot] = jnp.sum(jnp.transpose(crps_s[...]), axis=0, keepdims=True) * (
+                weight * mine * (1.0 / C)
+            )
+
+        return loss
+
+    for m in range(MEM):
+        cbuf_s[m, 0:PAD] = jnp.zeros((PAD, C), F32)
+        cbuf_s[m, PAD + J :] = jnp.zeros((PAD, C), F32)
+    lax.fori_loop(0, SLOTS + 2, make_crps, 0)
+    loss = cells_ref[0] + cells_ref[1] + cells_ref[2] + cells_ref[3]
     lane = lax.broadcasted_iota(jnp.int32, (1, J), 1)
     loss = jnp.where((lane >= LEFT) & (lane < LEFT + OWN), loss, 0.0)
 
@@ -299,22 +406,26 @@
     grads_ref[2304:R] = jnp.broadcast_to(total, (R - 2304, C))
 
 
-def local_step(counts, seeds, place, weights, own, f1, f2, f3, b1, b2, b3, target, amp, w1, w2, wt):
+def local_step(counts, seeds, place, weights, state, target, r1, r2, r3, other, amp, w1, w2, wt):
     smem = pl.BlockSpec(memory_space=pltpu.SMEM)
     vmem = pl.BlockSpec(memory_space=pltpu.VMEM)
+    hbm = pl.BlockSpec(memory_space=pl.ANY)
     return pl.pallas_call(
         kernel,
         out_shape=(
             jax.ShapeDtypeStruct((R, C), F32),
             jax.ShapeDtypeStruct((SLOTS, 1, J), F32),
         ),
-        in_specs=[smem] * 4 + [vmem] * 12,
+        in_specs=[smem] * 4 + [hbm] * 5 + [vmem] * 5,
         out_specs=(vmem, vmem),
         scratch_shapes=[
             pltpu.VMEM((EXT, J, C), BF),
             pltpu.VMEM((SLOTS + 2, J, C), BF),
+            pltpu.VMEM((4, J, C), BF),
             pltpu.VMEM((J, C), jnp.int32),
             pltpu.VMEM((J + 2 * PAD, C), F32),
+            pltpu.VMEM((MEM, J + 2 * PAD, C), F32),
+            pltpu.VMEM((J, C), F32),
             pltpu.VMEM((MEM, EXT, J, 3 * C), BF),
             pltpu.VMEM((MEM, EXT - 2, J, 3 * C), BF),
             pltpu.VMEM((MEM, EXT - 4, J, 3 * C), BF),
@@ -323,10 +434,11 @@
             pltpu.VMEM((MEM, SLOTS, J, C), BF),
             pltpu.VMEM((MEM, SLOTS, J, C), BF),
             pltpu.VMEM((2 * C, 4 * 384), F32),
+            pltpu.SemaphoreType.DMA((4, 2)),
         ],
         compiler_params=pltpu.CompilerParams(vmem_limit_bytes=60 * 1024 * 1024),
         name="ensemble_step",
-    )(counts, seeds, place, weights, own, f1, f2, f3, b1, b2, b3, target, amp, w1, w2, wt)
+    )(counts, seeds, place, weights, state, target, r1, r2, r3, other, amp, w1, w2, wt)
 
 
 def paired(filt):
@@ -336,15 +448,9 @@
     )
 
 
-def window(field, start):
-    wide = jnp.concatenate([field[:, LON - LEFT :], field, field[:, : J - OWN - LEFT]], axis=1)
-    return lax.dynamic_slice_in_dim(wide, start, J, 1)
-
-
 def body(state, target, amp, filt1, filt2, counts, seed):
     band = lax.axis_index("band")
     member = lax.axis_index("member")
-    n = counts[band]
     x = band % 4
     core = member % 2
     weights = jnp.asarray(
@@ -354,29 +460,34 @@
     seeds = seeds + shift(seeds, 4, 1)
     seeds = seeds + shift(seeds, 3, 1)
 
-    own = window(state, member * OWN)
-    tgt = window(target, member * OWN)
-
-    def send(value, by):
-        pairs = [(i, i + by) for i in range(32) if 0 <= i + by < 32]
-        return lax.ppermute(value, "band", pairs)
-
-    padded = jnp.concatenate([jnp.zeros((3, J, C), BF), own], axis=0)
-    last3 = lax.dynamic_slice_in_dim(padded, n, 3, 0)
-    last_t = lax.dynamic_slice_in_dim(tgt, n - 1, 1, 0)
-    f1 = send(jnp.concatenate([last3, last_t], axis=0), 1)
-    b1 = send(jnp.concatenate([own[:3], tgt[:1]], axis=0), -1)
-    f2 = send(last3[1:], 2)
-    b2 = send(own[:2], -2)
-    f3 = send(last3[2:], 3)
-    b3 = send(own[:1], -3)
+    place = jnp.stack([band, member]).astype(jnp.int32)
+    send, second, third, flags = edges(counts, place, state, target)
+
+    pairs = []
+    for i in range(128):
+        b, core_of = i // 4, i % 2
+        to = b + 1 - 2 * core_of
+        if 0 <= to < 32:
+            pairs.append((i, to * 4 + i % 4))
+
+    def relay(value):
+        return lax.ppermute(value, BM, pairs)
+
+    def flag(k):
+        return flags[k : k + 1][None] > 0.5
+
+    r1 = relay(send)
+    r2 = relay(jnp.where(flag(0), second, r1[:1]))
+    r3 = relay(jnp.where(flag(1), third, jnp.where(flag(2), r1[:1], r2)))
+    other = shift(
+        lax.dynamic_slice_in_dim(jnp.concatenate([r1, r2, r3], axis=0), OWN * (1 - core), J, 1), 4, 1
+    )
 
     w1 = paired(filt1)
     w2 = paired(filt2)
     wt = paired(jnp.transpose(filt2[::-1, ::-1], (0, 1, 3, 2)))
-    place = jnp.stack([band, member]).astype(jnp.int32)
     grads, cells = local_step(
-        counts, seeds, place, weights, own, f1, f2, f3, b1, b2, b3, tgt, amp[None], w1, w2, wt
+        counts, seeds, place, weights, state, target, r1, r2, r3, other, amp[None], w1, w2, wt
     )
 
     part = scatter_sum(grads, 4, core)

time: 153 us -> 147 us (0.961)
  waiting for transfers between devices: 32.1 us -> 37.4 us
  local copies, waits for them, and re-layouts: 10 us -> 4.8 us
  between operations: 4.88 us -> 1.48 us
  other arithmetic: 7.25 us -> 5.7 us
    ppermute x6 -> x3, starting transfers between devices: 17.7 us -> 4 us  [relay(): return lax.ppermute(value, BM, pairs)]
    ppermute x15 -> x16, starting transfers between devices: 32.8 us -> 46.2 us  [shift(): return lax.ppermute(value, BM, pairs)]
    ppermute x15 -> x16, waiting for transfers between devices: 22.6 us -> 26.5 us  [shift(): return lax.ppermute(value, BM, pairs)]
    pallas_call x0 -> x1, Pallas kernels: none -> 3.04 us  [edges(): pl.pallas_call(edge_kernel, out_shape=(jax.ShapeDtypeStruct((2, W, C), BF...]
    slice x10 -> x0, local copies, waits for them, and re-layouts: 3.02 us -> none  [the longest x1 0.81 us: body(): b2 = send(own[:2], -2)]
    pallas_call x1, Pallas kernels: 47.4 us -> 44.4 us  [local_step(): pl.pallas_call(kernel, out_shape=(jax.ShapeDtypeStruct((R, C), F32), jax....]
    concatenate x4 -> x1, other arithmetic: 2.62 us -> 0.03 us  [body(): jnp.concatenate([r1, r2, r3], axis=0)]
    dynamic_slice x2 -> x0, local copies, waits for them, and re-layouts: 2 us -> none  [the longest x1 1.24 us: body(): n = counts[band]]
  transfers between devices with their start and end apart: 21 -> 19, of which waited for: 15 -> 16; matrix products, arithmetic and copies ran while one was open for 6% -> 4% of each run, Pallas kernels for 0% -> 0%
where the time goes in v1:
time: 147 us
  starting transfers between devices  50.2 us (34%)
  Pallas kernels  47.5 us (32%)
  waiting for transfers between devices  37.4 us (25%)
  other arithmetic  5.7 us (4%)
  local copies, waits for them, and re-layouts  4.8 us (3%)
  between operations  1.48 us (1%)
    ppermute x16, starting transfers between devices, shift(): return lax.ppermute(value, BM, pairs)  46.2 us
    pallas_call x1, Pallas kernels, local_step(): pl.pallas_call(kernel, out_shape=(jax.ShapeDtypeStruct((R, C), F32), jax....  44.4 us
    ppermute x16, waiting for transfers between devices, shift(): return lax.ppermute(value, BM, pairs)  26.5 us
    ppermute x3, waiting for transfers between devices, relay(): return lax.ppermute(value, BM, pairs)  10.9 us
    ppermute x3, starting transfers between devices, relay(): return lax.ppermute(value, BM, pairs)  4 us
    pallas_call x1, Pallas kernels, edges(): pl.pallas_call(edge_kernel, out_shape=(jax.ShapeDtypeStruct((2, W, C), BF...  3.04 us
  transfers between devices with their start and end apart: 19, of which 16 were waited for; matrix products, arithmetic and copies ran while one was open for 4% of the time, Pallas kernels for 0%

profile of v1, /device:TPU:1, one launch (start us, length us, event | category | flops | bytes accessed | tf_op | source)
XLA Modules:
  0.0 147.1 jit_solution(3152850615562384066)
XLA Ops:
  1.3 3.0 %edge_rows.1 = (bf16[2,752,128]{2,1,0:T(8,128)(2,1)}, bf16[1,752,128]{2,1,0:T(8,128)(2,1)}, bf16[1,752,128]{2,1,0:T(8,128)(2,1)}, f32[8,128]{1,0:T(8,128)}) custom-call(s32[32]{0:T(128)} %counts_ref.3, s32[2]{0:T(128)} %pad_add_fusion.place_ref, bf16[4,1440,128]{2,1,0:T(8,128)(2,1)} %state_ref.3, bf16[4,1440,128]{2,1,0:T(8,128)(2,1)} %target_ref.3), custom_call_target="tpu_custom_call" | custom-call | tf_op jit(solution)/shard_map/edge_rows/pallas_call | solution.py:167
  4.3 1.4 collective-permute-start.2
  6.4 3.7 %collective-permute-start = (s32[4]{0:T(128)S(1)}, s32[4]{0:T(128)S(1)}, u32[]{:S(2)}, u32[]{:S(2)}) collective-permute-start(s32[4]{0:T(128)S(1)} %compare_select_fusion), channel_id=1, source_target_pairs={{0,1},{1,0},{2,3},{3,2},{4,5},{5,4},{6,7},{7,6},{8,9},{9,8},{10,11... | collective-permute-start | bytes 56 | tf_op jit(solution)/shard_map/ppermute | solution.py:49
  11.2 2.5 %collective-permute-done.2.r1_ref = bf16[2,752,128]{2,1,0:T(8,128)(2,1)S(1)} collective-permute-done((bf16[2,752,128]{2,1,0:T(8,128)(2,1)}, bf16[2,752,128]{2,1,0:T(8,128)(2,1)S(1)}, u32[]{:S(2)}, u32[]{:S(2)}) %collective-permute-start.2) | collective-permute-done | bytes 385056 | tf_op jit(solution)/shard_map/ppermute | solution.py:474
  13.7 1.1 broadcast_select_fusion
  14.8 1.3 collective-permute-start.3
  16.1 1.3 fusion.6
  17.4 4.0 %collective-permute-done.3.r2_ref = bf16[1,752,128]{2,1,0:T(8,128)(2,1)S(1)} collective-permute-done((bf16[1,752,128]{2,1,0:T(8,128)(2,1)S(1)}, bf16[1,752,128]{2,1,0:T(8,128)(2,1)S(1)}, u32[]{:S(2)}, u32[]{:S(2)}) %collective-permute-start.3) | collective-permute-done | bytes 192544 | tf_op jit(solution)/shard_map/ppermute | solution.py:474
  21.5 1.3 collective-permute-start.4
  23.8 4.4 %collective-permute-done.4.r3_ref = bf16[1,752,128]{2,1,0:T(8,128)(2,1)S(1)} collective-permute-done((bf16[1,752,128]{2,1,0:T(8,128)(2,1)S(1)}, bf16[1,752,128]{2,1,0:T(8,128)(2,1)S(1)}, u32[]{:S(2)}, u32[]{:S(2)}) %collective-permute-start.4) | collective-permute-done | bytes 192544 | tf_op jit(solution)/shard_map/ppermute | solution.py:474
  28.2 2.9 %collective-permute-start.5 = (bf16[4,384,128]{2,1,0:T(8,128)(2,1)S(1)}, bf16[4,384,128]{2,1,0:T(8,128)(2,1)S(1)}, u32[]{:S(2)}, u32[]{:S(2)}) collective-permute-start(bf16[4,384,128]{2,1,0:T(8,128)(2,1)S(1)} %fusion.10), channel_id=1, source_target_pairs={{0,1},{1,0},{2,3},{3,2},{4,5},{5,4},{6,7},{7,6},{8,9},{9,8},{10,11... | collective-permute-start | bytes 1179656 | tf_op jit(solution)/shard_map/ppermute | solution.py:49
  31.1 3.6 %collective-permute-start.1 = (s32[4]{0:T(128)S(1)}, s32[4]{0:T(128)S(1)}, u32[]{:S(2)}, u32[]{:S(2)}) collective-permute-start(s32[4]{0:T(128)S(1)} %fusion.14), channel_id=1, source_target_pairs={{0,2},{1,3},{2,0},{3,1},{4,6},{5,7},{6,4},{7,5},{8,10},{9,11},{10,... | collective-permute-start | bytes 56 | tf_op jit(solution)/shard_map/ppermute | solution.py:49
  37.0 44.4 %ensemble_step.1 = (f32[2368,128]{1,0:T(8,128)}, f32[4,1,384]{2,1,0:T(1,128)}) custom-call(s32[32]{0:T(128)} %counts_ref.3, s32[4]{0:T(128)} %fusion.15.seeds_ref, s32[2]{0:T(128)} %pad_add_fusion.place_ref, f32[96]{0:T(128)} %constant.119.clone.weight_ref, bf16[4,1440,128]{2,1,0:T(8,128)(2,1)} %state_ref.3, bf16[4,1440,128]{2,1,0:T(8,128)(2,1)} %target_ref.3, ...), custom_call_target="tpu_custom_call" | custom-call | tf_op jit(solution)/shard_map/ensemble_step/pallas_call | solution.py:413
  81.4 1.2 dynamic-slice_bitcast_fusion
  83.7 1.7 %collective-permute-done.6 = f32[1184,128]{1,0:T(8,128)S(1)} collective-permute-done((f32[1184,128]{1,0:T(8,128)S(1)}, f32[1184,128]{1,0:T(8,128)S(1)}, u32[]{:S(2)}, u32[]{:S(2)}) %collective-permute-start.6) | collective-permute-done | bytes 606240 | tf_op jit(solution)/shard_map/ppermute | solution.py:49
  85.5 2.7 %collective-permute-start.7 = (f32[296,128]{1,0:T(8,128)S(1)}, f32[296,128]{1,0:T(8,128)S(1)}, u32[]{:S(2)}, u32[]{:S(2)}) collective-permute-start(f32[296,128]{1,0:T(8,128)S(1)} %get-tuple-element.20), channel_id=1, source_target_pairs={{0,4},{1,5},{2,6},{3,7},{4,8},{5,9},{6,10},{7,11},{8,12},{9,13},{1... | collective-permute-start | bytes 454664 | tf_op jit(solution)/shard_map/ppermute | solution.py:49
  88.2 6.6 %collective-permute-start.8 = (f32[296,128]{1,0:T(8,128)S(1)}, f32[296,128]{1,0:T(8,128)S(1)}, u32[]{:S(2)}, u32[]{:S(2)}) collective-permute-start(f32[296,128]{1,0:T(8,128)S(1)} %get-tuple-element.22), channel_id=1, source_target_pairs={{0,8},{1,9},{2,10},{3,11},{4,12},{5,13},{6,14},{7,15},{8,0},{9,1},... | collective-permute-start | bytes 454664 | tf_op jit(solution)/shard_map/ppermute | solution.py:49
  94.8 2.8 %collective-permute-done.7 = f32[296,128]{1,0:T(8,128)S(1)} collective-permute-done((f32[296,128]{1,0:T(8,128)S(1)}, f32[296,128]{1,0:T(8,128)S(1)}, u32[]{:S(2)}, u32[]{:S(2)}) %collective-permute-start.7) | collective-permute-done | bytes 151584 | tf_op jit(solution)/shard_map/ppermute | solution.py:49
  97.6 4.1 %collective-permute-done.8 = f32[296,128]{1,0:T(8,128)S(1)} collective-permute-done((f32[296,128]{1,0:T(8,128)S(1)}, f32[296,128]{1,0:T(8,128)S(1)}, u32[]{:S(2)}, u32[]{:S(2)}) %collective-permute-start.8) | collective-permute-done | bytes 151584 | tf_op jit(solution)/shard_map/ppermute | solution.py:49
  101.8 3.9 %collective-permute-start.10 = (f32[296,128]{1,0:T(8,128)S(1)}, f32[296,128]{1,0:T(8,128)S(1)}, u32[]{:S(2)}, u32[]{:S(2)}) collective-permute-start(f32[296,128]{1,0:T(8,128)S(1)} %fusion.12), channel_id=1, source_target_pairs={{0,16},{1,17},{2,18},{3,19},{4,20},{5,21},{6,22},{7,23},{8,24},{9,... | collective-permute-start | bytes 454664 | tf_op jit(solution)/shard_map/ppermute | solution.py:49
  105.6 5.9 %collective-permute-start.11 = (f32[296,128]{1,0:T(8,128)S(1)}, f32[296,128]{1,0:T(8,128)S(1)}, u32[]{:S(2)}, u32[]{:S(2)}) collective-permute-start(f32[296,128]{1,0:T(8,128)S(1)} %fusion.12), channel_id=1, source_target_pairs={{0,32},{1,33},{2,34},{3,35},{4,36},{5,37},{6,38},{7,39},{8,40},{9,... | collective-permute-start | bytes 454664 | tf_op jit(solution)/shard_map/ppermute | solution.py:49
  111.5 1.9 %collective-permute-done.10 = f32[296,128]{1,0:T(8,128)S(1)} collective-permute-done((f32[296,128]{1,0:T(8,128)S(1)}, f32[296,128]{1,0:T(8,128)S(1)}, u32[]{:S(2)}, u32[]{:S(2)}) %collective-permute-start.10) | collective-permute-done | bytes 151584 | tf_op jit(solution)/shard_map/ppermute | solution.py:49
  113.4 3.8 %collective-permute-done.11 = f32[296,128]{1,0:T(8,128)S(1)} collective-permute-done((f32[296,128]{1,0:T(8,128)S(1)}, f32[296,128]{1,0:T(8,128)S(1)}, u32[]{:S(2)}, u32[]{:S(2)}) %collective-permute-start.11) | collective-permute-done | bytes 151584 | tf_op jit(solution)/shard_map/ppermute | solution.py:49
  117.5 3.3 %collective-permute-start.13 = (f32[296,128]{1,0:T(8,128)S(1)}, f32[296,128]{1,0:T(8,128)S(1)}, u32[]{:S(2)}, u32[]{:S(2)}) collective-permute-start(f32[296,128]{1,0:T(8,128)S(1)} %add_add_fusion), channel_id=1, source_target_pairs={{0,2},{1,3},{2,0},{3,1},{4,6},{5,7},{6,4},{7,5},{8,10},{9,11},{10,... | collective-permute-start | bytes 454664 | tf_op jit(solution)/shard_map/ppermute | solution.py:49
  120.8 2.6 %collective-permute-done.13 = f32[296,128]{1,0:T(8,128)S(1)} collective-permute-done((f32[296,128]{1,0:T(8,128)S(1)}, f32[296,128]{1,0:T(8,128)S(1)}, u32[]{:S(2)}, u32[]{:S(2)}) %collective-permute-start.13) | collective-permute-done | bytes 151584 | tf_op jit(solution)/shard_map/ppermute | solution.py:49
  123.4 4.3 %collective-permute-start.14 = (f32[296,128]{1,0:T(8,128)S(1)}, f32[296,128]{1,0:T(8,128)S(1)}, u32[]{:S(2)}, u32[]{:S(2)}) collective-permute-start(f32[296,128]{1,0:T(8,128)S(1)} %add.157), channel_id=1, source_target_pairs={{0,64},{1,65},{2,66},{3,67},{4,68},{5,69},{6,70},{7,71},{8,72},{9,... | collective-permute-start | bytes 454664 | tf_op jit(solution)/shard_map/ppermute | solution.py:49
  127.7 3.2 %collective-permute-done.14 = f32[296,128]{1,0:T(8,128)S(1)} collective-permute-done((f32[296,128]{1,0:T(8,128)S(1)}, f32[296,128]{1,0:T(8,128)S(1)}, u32[]{:S(2)}, u32[]{:S(2)}) %collective-permute-start.14) | collective-permute-done | bytes 151584 | tf_op jit(solution)/shard_map/ppermute | solution.py:49
  131.9 3.1 %collective-permute-start.16 = (f32[296,128]{1,0:T(8,128)S(1)}, f32[296,128]{1,0:T(8,128)S(1)}, u32[]{:S(2)}, u32[]{:S(2)}) collective-permute-start(f32[296,128]{1,0:T(8,128)S(1)} %get-tuple-element.17), channel_id=1, source_target_pairs={{0,8},{1,9},{2,10},{3,11},{4,12},{5,13},{6,14},{7,15},{8,0},{9,1},... | collective-permute-start | bytes 454664 | tf_op jit(solution)/shard_map/ppermute | solution.py:49
  135.0 1.4 collective-permute-done.15
  136.4 2.9 %collective-permute-done.16 = f32[296,128]{1,0:T(8,128)S(1)} collective-permute-done((f32[296,128]{1,0:T(8,128)S(1)}, f32[296,128]{1,0:T(8,128)S(1)}, u32[]{:S(2)}, u32[]{:S(2)}) %collective-permute-start.16) | collective-permute-done | bytes 151584 | tf_op jit(solution)/shard_map/ppermute | solution.py:49
  139.5 4.3 %collective-permute-start.18 = (f32[1184,128]{1,0:T(8,128)S(1)}, f32[1184,128]{1,0:T(8,128)S(1)}, u32[]{:S(2)}, u32[]{:S(2)}) collective-permute-start(f32[1184,128]{1,0:T(8,128)S(1)} %bitcast.59), channel_id=1, source_target_pairs={{0,1},{1,0},{2,3},{3,2},{4,5},{5,4},{6,7},{7,6},{8,9},{9,8},{10,11... | collective-permute-start | bytes 1818632 | tf_op jit(solution)/shard_map/ppermute | solution.py:49
  145.5 1.1 fusion.13
  (56 shorter events, 9.9 us)
Async XLA Ops:
  1.3 8.9 %copy-start.3 = (bf16[3,3,128,128]{3,2,1,0:T(8,128)(2,1)S(1)}, bf16[3,3,128,128]{3,2,1,0:T(8,128)(2,1)}, u32[]{:S(2)}) copy-start(bf16[3,3,128,128]{3,2,1,0:T(8,128)(2,1)} %param.12) | copy-start | bytes 884740
  4.3 11.8 %copy-start.6 = (bf16[3,3,128,128]{3,2,1,0:T(8,128)(2,1)S(1)}, bf16[3,3,128,128]{3,2,1,0:T(8,128)(2,1)}, u32[]{:S(2)}) copy-start(bf16[3,3,128,128]{3,2,1,0:T(8,128)(2,1)} %param.11) | copy-start | bytes 884740
  4.3 9.3 %collective-permute-start.2 = (bf16[2,752,128]{2,1,0:T(8,128)(2,1)}, bf16[2,752,128]{2,1,0:T(8,128)(2,1)S(1)}, u32[]{:S(2)}, u32[]{:S(2)}) collective-permute-start(bf16[2,752,128]{2,1,0:T(8,128)(2,1)} %get-tuple-element.10), channel_id=1, source_target_pairs={{0,4},{2,6},{4,8},{5,1},{6,10},{7,3},{8,12},{9,5},{10,14},{11,7},{... | collective-permute-start | bytes 1155080 | tf_op jit(solution)/shard_map/ppermute | solution.py:474
  6.4 24.6 %collective-permute-start = (s32[4]{0:T(128)S(1)}, s32[4]{0:T(128)S(1)}, u32[]{:S(2)}, u32[]{:S(2)}) collective-permute-start(s32[4]{0:T(128)S(1)} %compare_select_fusion), channel_id=1, source_target_pairs={{0,1},{1,0},{2,3},{3,2},{4,5},{5,4},{6,7},{7,6},{8,9},{9,8},{10,11... | collective-permute-start | bytes 56 | tf_op jit(solution)/shard_map/ppermute | solution.py:49
  10.4 11.1 %copy-start.7 = (bf16[1,752,128]{2,1,0:T(8,128)(2,1)S(1)}, bf16[1,752,128]{2,1,0:T(8,128)(2,1)}, u32[]{:S(2)}) copy-start(bf16[1,752,128]{2,1,0:T(8,128)(2,1)} %get-tuple-element.13) | copy-start | bytes 577540
  13.7 14.5 %copy-start = (bf16[2,752,128]{2,1,0:T(8,128)(2,1)}, bf16[2,752,128]{2,1,0:T(8,128)(2,1)S(1)}, u32[]{:S(2)}) copy-start(bf16[2,752,128]{2,1,0:T(8,128)(2,1)S(1)} %collective-permute-done.2.r1_ref) | copy-start | bytes 1155076
  14.8 6.7 %collective-permute-start.3 = (bf16[1,752,128]{2,1,0:T(8,128)(2,1)S(1)}, bf16[1,752,128]{2,1,0:T(8,128)(2,1)S(1)}, u32[]{:S(2)}, u32[]{:S(2)}) collective-permute-start(bf16[1,752,128]{2,1,0:T(8,128)(2,1)S(1)} %broadcast_select_fusion), channel_id=1, source_target_pairs={{0,4},{2,6},{4,8},{5,1},{6,10},{7,3},{8,12},{9,5},{10,14},{11,7},{... | collective-permute-start | bytes 577544 | tf_op jit(solution)/shard_map/ppermute | solution.py:474
  21.5 6.8 %copy-start.1 = (bf16[1,752,128]{2,1,0:T(8,128)(2,1)}, bf16[1,752,128]{2,1,0:T(8,128)(2,1)S(1)}, u32[]{:S(2)}) copy-start(bf16[1,752,128]{2,1,0:T(8,128)(2,1)S(1)} %collective-permute-done.3.r2_ref) | copy-start | bytes 577540
  21.5 6.7 %collective-permute-start.4 = (bf16[1,752,128]{2,1,0:T(8,128)(2,1)S(1)}, bf16[1,752,128]{2,1,0:T(8,128)(2,1)S(1)}, u32[]{:S(2)}, u32[]{:S(2)}) collective-permute-start(bf16[1,752,128]{2,1,0:T(8,128)(2,1)S(1)} %select_select_fusion), channel_id=1, source_target_pairs={{0,4},{2,6},{4,8},{5,1},{6,10},{7,3},{8,12},{9,5},{10,14},{11,7},{... | collective-permute-start | bytes 577544 | tf_op jit(solution)/shard_map/ppermute | solution.py:474
  28.2 8.1 %copy-start.4 = (bf16[1,752,128]{2,1,0:T(8,128)(2,1)}, bf16[1,752,128]{2,1,0:T(8,128)(2,1)S(1)}, u32[]{:S(2)}) copy-start(bf16[1,752,128]{2,1,0:T(8,128)(2,1)S(1)} %collective-permute-done.4.r3_ref) | copy-start | bytes 577540
  28.2 8.0 %collective-permute-start.5 = (bf16[4,384,128]{2,1,0:T(8,128)(2,1)S(1)}, bf16[4,384,128]{2,1,0:T(8,128)(2,1)S(1)}, u32[]{:S(2)}, u32[]{:S(2)}) collective-permute-start(bf16[4,384,128]{2,1,0:T(8,128)(2,1)S(1)} %fusion.10), channel_id=1, source_target_pairs={{0,1},{1,0},{2,3},{3,2},{4,5},{5,4},{6,7},{7,6},{8,9},{9,8},{10,11... | collective-permute-start | bytes 1179656 | tf_op jit(solution)/shard_map/ppermute | solution.py:49
  31.1 4.5 %collective-permute-start.1 = (s32[4]{0:T(128)S(1)}, s32[4]{0:T(128)S(1)}, u32[]{:S(2)}, u32[]{:S(2)}) collective-permute-start(s32[4]{0:T(128)S(1)} %fusion.14), channel_id=1, source_target_pairs={{0,2},{1,3},{2,0},{3,1},{4,6},{5,7},{6,4},{7,5},{8,10},{9,11},{10,... | collective-permute-start | bytes 56 | tf_op jit(solution)/shard_map/ppermute | solution.py:49
  36.2 0.7 copy-start.5
  81.4 4.0 %copy-start.2 = (f32[2368,128]{1,0:T(8,128)S(1)}, f32[2368,128]{1,0:T(8,128)}, u32[]{:S(2)}) copy-start(f32[2368,128]{1,0:T(8,128)} %get-tuple-element.15) | copy-start | bytes 3637252
  82.6 2.7 %collective-permute-start.6 = (f32[1184,128]{1,0:T(8,128)S(1)}, f32[1184,128]{1,0:T(8,128)S(1)}, u32[]{:S(2)}, u32[]{:S(2)}) collective-permute-start(f32[1184,128]{1,0:T(8,128)S(1)} %dynamic-slice_bitcast_fusion), channel_id=1, source_target_pairs={{0,1},{1,0},{2,3},{3,2},{4,5},{5,4},{6,7},{7,6},{8,9},{9,8},{10,11... | collective-permute-start | bytes 1818632 | tf_op jit(solution)/shard_map/ppermute | solution.py:49
  85.5 12.1 %collective-permute-start.7 = (f32[296,128]{1,0:T(8,128)S(1)}, f32[296,128]{1,0:T(8,128)S(1)}, u32[]{:S(2)}, u32[]{:S(2)}) collective-permute-start(f32[296,128]{1,0:T(8,128)S(1)} %get-tuple-element.20), channel_id=1, source_target_pairs={{0,4},{1,5},{2,6},{3,7},{4,8},{5,9},{6,10},{7,11},{8,12},{9,13},{1... | collective-permute-start | bytes 454664 | tf_op jit(solution)/shard_map/ppermute | solution.py:49
  88.2 13.5 %collective-permute-start.8 = (f32[296,128]{1,0:T(8,128)S(1)}, f32[296,128]{1,0:T(8,128)S(1)}, u32[]{:S(2)}, u32[]{:S(2)}) collective-permute-start(f32[296,128]{1,0:T(8,128)S(1)} %get-tuple-element.22), channel_id=1, source_target_pairs={{0,8},{1,9},{2,10},{3,11},{4,12},{5,13},{6,14},{7,15},{8,0},{9,1},... | collective-permute-start | bytes 454664 | tf_op jit(solution)/shard_map/ppermute | solution.py:49
  94.8 6.9 %collective-permute-start.9 = (f32[296,128]{1,0:T(8,128)S(1)}, f32[296,128]{1,0:T(8,128)S(1)}, u32[]{:S(2)}, u32[]{:S(2)}) collective-permute-start(f32[296,128]{1,0:T(8,128)S(1)} %get-tuple-element.21), channel_id=1, source_target_pairs={{0,12},{1,13},{2,14},{3,15},{4,0},{5,1},{6,2},{7,3},{8,4},{9,5},{1... | collective-permute-start | bytes 454664 | tf_op jit(solution)/shard_map/ppermute | solution.py:49
  101.8 11.7 %collective-permute-start.10 = (f32[296,128]{1,0:T(8,128)S(1)}, f32[296,128]{1,0:T(8,128)S(1)}, u32[]{:S(2)}, u32[]{:S(2)}) collective-permute-start(f32[296,128]{1,0:T(8,128)S(1)} %fusion.12), channel_id=1, source_target_pairs={{0,16},{1,17},{2,18},{3,19},{4,20},{5,21},{6,22},{7,23},{8,24},{9,... | collective-permute-start | bytes 454664 | tf_op jit(solution)/shard_map/ppermute | solution.py:49
  105.6 11.6 %collective-permute-start.11 = (f32[296,128]{1,0:T(8,128)S(1)}, f32[296,128]{1,0:T(8,128)S(1)}, u32[]{:S(2)}, u32[]{:S(2)}) collective-permute-start(f32[296,128]{1,0:T(8,128)S(1)} %fusion.12), channel_id=1, source_target_pairs={{0,32},{1,33},{2,34},{3,35},{4,36},{5,37},{6,38},{7,39},{8,40},{9,... | collective-permute-start | bytes 454664 | tf_op jit(solution)/shard_map/ppermute | solution.py:49
  111.5 6.0 %collective-permute-start.12 = (f32[296,128]{1,0:T(8,128)S(1)}, f32[296,128]{1,0:T(8,128)S(1)}, u32[]{:S(2)}, u32[]{:S(2)}) collective-permute-start(f32[296,128]{1,0:T(8,128)S(1)} %fusion.12), channel_id=1, source_target_pairs={{0,48},{1,49},{2,50},{3,51},{4,52},{5,53},{6,54},{7,55},{8,56},{9,... | collective-permute-start | bytes 454664 | tf_op jit(solution)/shard_map/ppermute | solution.py:49
  117.5 26.2 %copy-start.8 = (f32[4,1,384]{2,1,0:T(1,128)S(1)}, f32[4,1,384]{2,1,0:T(1,128)}, u32[]{:S(2)}) copy-start(f32[4,1,384]{2,1,0:T(1,128)} %get-tuple-element.14) | copy-start | bytes 18436
  117.5 5.9 %collective-permute-start.13 = (f32[296,128]{1,0:T(8,128)S(1)}, f32[296,128]{1,0:T(8,128)S(1)}, u32[]{:S(2)}, u32[]{:S(2)}) collective-permute-start(f32[296,128]{1,0:T(8,128)S(1)} %add_add_fusion), channel_id=1, source_target_pairs={{0,2},{1,3},{2,0},{3,1},{4,6},{5,7},{6,4},{7,5},{8,10},{9,11},{10,... | collective-permute-start | bytes 454664 | tf_op jit(solution)/shard_map/ppermute | solution.py:49
  123.4 7.5 %collective-permute-start.14 = (f32[296,128]{1,0:T(8,128)S(1)}, f32[296,128]{1,0:T(8,128)S(1)}, u32[]{:S(2)}, u32[]{:S(2)}) collective-permute-start(f32[296,128]{1,0:T(8,128)S(1)} %add.157), channel_id=1, source_target_pairs={{0,64},{1,65},{2,66},{3,67},{4,68},{5,69},{6,70},{7,71},{8,72},{9,... | collective-permute-start | bytes 454664 | tf_op jit(solution)/shard_map/ppermute | solution.py:49
  131.0 5.4 %collective-permute-start.15 = (f32[296,128]{1,0:T(8,128)S(1)}, f32[296,128]{1,0:T(8,128)S(1)}, u32[]{:S(2)}, u32[]{:S(2)}) collective-permute-start(f32[296,128]{1,0:T(8,128)S(1)} %get-tuple-element.17), channel_id=1, source_target_pairs={{0,4},{1,5},{2,6},{3,7},{4,8},{5,9},{6,10},{7,11},{8,12},{9,13},{1... | collective-permute-start | bytes 454664 | tf_op jit(solution)/shard_map/ppermute | solution.py:49
  131.9 7.4 %collective-permute-start.16 = (f32[296,128]{1,0:T(8,128)S(1)}, f32[296,128]{1,0:T(8,128)S(1)}, u32[]{:S(2)}, u32[]{:S(2)}) collective-permute-start(f32[296,128]{1,0:T(8,128)S(1)} %get-tuple-element.17), channel_id=1, source_target_pairs={{0,8},{1,9},{2,10},{3,11},{4,12},{5,13},{6,14},{7,15},{8,0},{9,1},... | collective-permute-start | bytes 454664 | tf_op jit(solution)/shard_map/ppermute | solution.py:49
  135.0 4.4 %collective-permute-start.17 = (f32[296,128]{1,0:T(8,128)S(1)}, f32[296,128]{1,0:T(8,128)S(1)}, u32[]{:S(2)}, u32[]{:S(2)}) collective-permute-start(f32[296,128]{1,0:T(8,128)S(1)} %get-tuple-element.17), channel_id=1, source_target_pairs={{0,12},{1,13},{2,14},{3,15},{4,0},{5,1},{6,2},{7,3},{8,4},{9,5},{1... | collective-permute-start | bytes 454664 | tf_op jit(solution)/shard_map/ppermute | solution.py:49
  139.5 6.0 %collective-permute-start.18 = (f32[1184,128]{1,0:T(8,128)S(1)}, f32[1184,128]{1,0:T(8,128)S(1)}, u32[]{:S(2)}, u32[]{:S(2)}) collective-permute-start(f32[1184,128]{1,0:T(8,128)S(1)} %bitcast.59), channel_id=1, source_target_pairs={{0,1},{1,0},{2,3},{3,2},{4,5},{5,4},{6,7},{7,6},{8,9},{9,8},{10,11... | collective-permute-start | bytes 1818632 | tf_op jit(solution)/shard_map/ppermute | solution.py:49

commit v2 on v1

--- a/solution.py
+++ b/solution.py
@@ -139,23 +139,28 @@
                 c.wait()
 
 
-def edge_kernel(counts_ref, place_ref, state_ref, target_ref, send_ref, second_ref, third_ref, flag_ref, sem):
-    n = counts_ref[place_ref[0]]
+def edge_kernel(counts_ref, place_ref, state_ref, target_ref, one_ref, two_ref, three_ref, flag_ref, sem):
+    band = place_ref[0]
     member = place_ref[1]
     half, core = member // 2, member % 2
+    n = counts_ref[band]
+    back = 2 * core - 1
+    near = counts_ref[jnp.clip(band + back, 0, 31)]
+    far = counts_ref[jnp.clip(band + 2 * back, 0, 31)]
     row = lambda k: jnp.where(core == 0, jnp.maximum(n - 1 - k, 0), k)
-    cases = (
-        chip_row(half, state_ref, row(0), send_ref.at[0], sem.at[0])
-        + chip_row(half, target_ref, row(0), send_ref.at[1], sem.at[1])
-        + chip_row(half, state_ref, row(1), second_ref.at[0], sem.at[2])
-        + chip_row(half, state_ref, row(2), third_ref.at[0], sem.at[3])
-    )
+    sends = [(state_ref, 0, one_ref, 0), (state_ref, 1, one_ref, 1), (state_ref, 2, one_ref, 2)]
+    sends += [(target_ref, 0, one_ref, 3)]
+    sends += [(state_ref, 0, two_ref, 0), (state_ref, 1, two_ref, 1), (state_ref, 0, three_ref, 0)]
+    cases = []
+    for i, (src, k, dst, slot) in enumerate(sends):
+        cases += chip_row(half, src, row(k), dst.at[slot], sem.at[i])
     start(cases)
     ones = jnp.ones((1, C), F32)
-    flag_ref[0:1] = ones * (n >= 2).astype(F32)
-    flag_ref[1:2] = ones * (n >= 3).astype(F32)
-    flag_ref[2:3] = ones * (n == 2).astype(F32)
-    flag_ref[3:8] = jnp.zeros((5, C), F32)
+    flag_ref[0:1] = ones * (near >= 2).astype(F32)
+    flag_ref[1:2] = ones * (near >= 3).astype(F32)
+    flag_ref[2:3] = ones * (near == 2).astype(F32)
+    flag_ref[3:4] = ones * (far >= 2).astype(F32)
+    flag_ref[4:8] = jnp.zeros((4, C), F32)
     wait(cases)
 
 
@@ -163,23 +168,23 @@
     smem = pl.BlockSpec(memory_space=pltpu.SMEM)
     vmem = pl.BlockSpec(memory_space=pltpu.VMEM)
     hbm = pl.BlockSpec(memory_space=pl.ANY)
-    row = jax.ShapeDtypeStruct((1, W, C), BF)
+    rows = lambda k: jax.ShapeDtypeStruct((k, W, C), BF)
     return pl.pallas_call(
         edge_kernel,
-        out_shape=(jax.ShapeDtypeStruct((2, W, C), BF), row, row, jax.ShapeDtypeStruct((8, C), F32)),
+        out_shape=(rows(4), rows(2), rows(1), jax.ShapeDtypeStruct((8, C), F32)),
         in_specs=[smem, smem, hbm, hbm],
         out_specs=(vmem,) * 4,
-        scratch_shapes=[pltpu.SemaphoreType.DMA((4, 2))],
+        scratch_shapes=[pltpu.SemaphoreType.DMA((7, 2))],
         name="edge_rows",
     )(counts, place, state, target)
 
 
 def kernel(
     counts_ref, seeds_ref, place_ref, weight_ref,
-    state_ref, target_ref, r1_ref, r2_ref, r3_ref, other_ref,
+    state_ref, target_ref, mine_ref, other_ref,
     amp_ref, w1_ref, w2_ref, wt_ref,
     grads_ref, cells_ref,
-    state_s, tgt_s, mine_s, hash_s, buf_s, cbuf_s, crps_s,
+    state_s, tgt_s, hash_s, buf_s, cbuf_s, crps_s,
     in3_s, hid3_s, cot3_s, pre_s, fc_s, ya_s, yb_s, acc_s, sem,
 ):
     band = place_ref[0]
@@ -190,15 +195,7 @@
 
     copies = own_window(quarter, state_ref, state_s.at[pl.ds(DEPTH, SLOTS)], sem.at[0])
     copies += own_window(quarter, target_ref, tgt_s.at[pl.ds(1, SLOTS)], sem.at[1])
-    lane0 = pl.multiple_of(core * OWN, 8)
-    near = [
-        pltpu.make_async_copy(r1_ref.at[:, pl.ds(lane0, J)], mine_s.at[pl.ds(0, 2)], sem.at[2, 0]),
-        pltpu.make_async_copy(r2_ref.at[:, pl.ds(lane0, J)], mine_s.at[pl.ds(2, 1)], sem.at[2, 1]),
-        pltpu.make_async_copy(r3_ref.at[:, pl.ds(lane0, J)], mine_s.at[pl.ds(3, 1)], sem.at[3, 0]),
-    ]
     start(copies)
-    for c in near:
-        c.start()
 
     buf_s[0:PAD] = jnp.zeros((PAD, C), F32)
     buf_s[PAD + J :] = jnp.zeros((PAD, C), F32)
@@ -211,24 +208,22 @@
     own_col = ((cols >= LEFT) & (cols < LEFT + OWN)).astype(F32)
 
     wait(copies)
-    for c in near:
-        c.wait()
 
     def put_edges(above, below):
-        for slot, k in ((2, 0), (1, 2), (0, 3)):
+        for slot, k in ((2, 0), (1, 1), (0, 2)):
             state_s[slot] = above[k]
-        for slot, k in ((0, 0), (1, 2), (2, 3)):
+        for slot, k in ((0, 0), (1, 1), (2, 2)):
             state_s[DEPTH + n + slot] = below[k]
-        tgt_s[0] = above[1]
-        tgt_s[1 + n] = below[1]
+        tgt_s[0] = above[3]
+        tgt_s[1 + n] = below[3]
 
     @pl.when(core == 0)
     def _():
-        put_edges(mine_s, other_ref)
+        put_edges(mine_ref, other_ref)
 
     @pl.when(core == 1)
     def _():
-        put_edges(other_ref, mine_s)
+        put_edges(other_ref, mine_ref)
 
     def valid(e):
         g = offset - DEPTH + e
@@ -406,7 +401,7 @@
     grads_ref[2304:R] = jnp.broadcast_to(total, (R - 2304, C))
 
 
-def local_step(counts, seeds, place, weights, state, target, r1, r2, r3, other, amp, w1, w2, wt):
+def local_step(counts, seeds, place, weights, state, target, mine, other, amp, w1, w2, wt):
     smem = pl.BlockSpec(memory_space=pltpu.SMEM)
     vmem = pl.BlockSpec(memory_space=pltpu.VMEM)
     hbm = pl.BlockSpec(memory_space=pl.ANY)
@@ -416,12 +411,11 @@
             jax.ShapeDtypeStruct((R, C), F32),
             jax.ShapeDtypeStruct((SLOTS, 1, J), F32),
         ),
-        in_specs=[smem] * 4 + [hbm] * 5 + [vmem] * 5,
+        in_specs=[smem] * 4 + [hbm] * 2 + [vmem] * 6,
         out_specs=(vmem, vmem),
         scratch_shapes=[
             pltpu.VMEM((EXT, J, C), BF),
             pltpu.VMEM((SLOTS + 2, J, C), BF),
-            pltpu.VMEM((4, J, C), BF),
             pltpu.VMEM((J, C), jnp.int32),
             pltpu.VMEM((J + 2 * PAD, C), F32),
             pltpu.VMEM((MEM, J + 2 * PAD, C), F32),
@@ -434,11 +428,11 @@
             pltpu.VMEM((MEM, SLOTS, J, C), BF),
             pltpu.VMEM((MEM, SLOTS, J, C), BF),
             pltpu.VMEM((2 * C, 4 * 384), F32),
-            pltpu.SemaphoreType.DMA((4, 2)),
+            pltpu.SemaphoreType.DMA((2, 2)),
         ],
         compiler_params=pltpu.CompilerParams(vmem_limit_bytes=60 * 1024 * 1024),
         name="ensemble_step",
-    )(counts, seeds, place, weights, state, target, r1, r2, r3, other, amp, w1, w2, wt)
+    )(counts, seeds, place, weights, state, target, mine, other, amp, w1, w2, wt)
 
 
 def paired(filt):
@@ -456,38 +450,37 @@
     weights = jnp.asarray(
         np.cos(np.pi * ((np.arange(ROWS_TOTAL) + 0.5) / GRID_ROWS - 0.5)).astype(np.float32)
     )
+    place = jnp.stack([band, member]).astype(jnp.int32)
     seeds = jnp.where(jnp.arange(MEM) == member, seed, 0)
     seeds = seeds + shift(seeds, 4, 1)
-    seeds = seeds + shift(seeds, 3, 1)
-
-    place = jnp.stack([band, member]).astype(jnp.int32)
-    send, second, third, flags = edges(counts, place, state, target)
-
-    pairs = []
-    for i in range(128):
-        b, core_of = i // 4, i % 2
-        to = b + 1 - 2 * core_of
-        if 0 <= to < 32:
-            pairs.append((i, to * 4 + i % 4))
-
-    def relay(value):
+    one, two, three, flags = edges(counts, place, state, target)
+
+    def send(value, by):
+        pairs = [(i, (i // 4 + by * (1 - 2 * (i % 2))) % 32 * 4 + i % 4) for i in range(128)]
         return lax.ppermute(value, BM, pairs)
 
     def flag(k):
         return flags[k : k + 1][None] > 0.5
 
-    r1 = relay(send)
-    r2 = relay(jnp.where(flag(0), second, r1[:1]))
-    r3 = relay(jnp.where(flag(1), third, jnp.where(flag(2), r1[:1], r2)))
-    other = shift(
-        lax.dynamic_slice_in_dim(jnp.concatenate([r1, r2, r3], axis=0), OWN * (1 - core), J, 1), 4, 1
+    one, seeds = lax.optimization_barrier((one, seeds))
+    g1 = send(one, 1)
+    seeds = seeds + shift(seeds, 3, 1)
+    two, three, seeds = lax.optimization_barrier((two, three, seeds))
+    g2 = send(two, 2)
+    g3 = send(three, 3)
+    row2 = jnp.where(flag(0), g1[1:2], g2[:1])
+    row3 = jnp.where(
+        flag(1), g1[2:3], jnp.where(flag(2), g2[:1], jnp.where(flag(3), g2[1:], g3))
     )
+    halo = jnp.concatenate([g1[:1], row2, row3, g1[3:]], axis=0)
+    mine = lax.dynamic_slice_in_dim(halo, OWN * core, J, 1)
+    other = shift(lax.dynamic_slice_in_dim(halo, OWN * (1 - core), J, 1), 4, 1)
 
     w1 = paired(filt1)
     w2 = paired(filt2)
     wt = paired(jnp.transpose(filt2[::-1, ::-1], (0, 1, 3, 2)))
     grads, cells = local_step(
-        counts, seeds, place, weights, state, target, r1, r2, r3, other, amp[None], w1, w2, wt
+        counts, seeds, place, weights, state, target, mine, other, amp[None], w1, w2, wt
     )
 
     part = scatter_sum(grads, 4, core)

time: 147 us -> 135 us (0.918)
  starting transfers between devices: 50.2 us -> 34.6 us
  waiting for transfers between devices: 37.4 us -> 40.7 us
    ppermute x16, starting transfers between devices: 46.2 us -> 27.5 us  [shift(): return lax.ppermute(value, BM, pairs)]
    ppermute x3, starting transfers between devices: 4 us -> 7.17 us  [send(): return lax.ppermute(value, BM, pairs)]
    ppermute x16, waiting for transfers between devices: 26.5 us -> 28.2 us  [shift(): return lax.ppermute(value, BM, pairs)]
    ppermute x3, waiting for transfers between devices: 10.9 us -> 12.5 us  [send(): return lax.ppermute(value, BM, pairs)]
  transfers between devices with their start and end apart: 19 -> 19, of which waited for: 16 -> 15; matrix products, arithmetic and copies ran while one was open for 4% -> 4% of each run, Pallas kernels for 0% -> 3%
where the time goes in v2:
time: 135 us
  Pallas kernels  47.9 us (35%)
  waiting for transfers between devices  40.7 us (30%)
  starting transfers between devices  34.6 us (26%)
  local copies, waits for them, and re-layouts  5.63 us (4%)
  other arithmetic  4.64 us (3%)
  between operations  1.51 us (1%)
    pallas_call x1, Pallas kernels, local_step(): pl.pallas_call(kernel, out_shape=(jax.ShapeDtypeStruct((R, C), F32), jax....  44.4 us
    ppermute x16, waiting for transfers between devices, shift(): return lax.ppermute(value, BM, pairs)  28.2 us
    ppermute x16, starting transfers between devices, shift(): return lax.ppermute(value, BM, pairs)  27.5 us
    ppermute x3, waiting for transfers between devices, send(): return lax.ppermute(value, BM, pairs)  12.5 us
    ppermute x3, starting transfers between devices, send(): return lax.ppermute(value, BM, pairs)  7.17 us
    pallas_call x1, Pallas kernels, edges(): pl.pallas_call(edge_kernel, out_shape=(rows(4), rows(2), rows(1), jax.Sha...  3.45 us
  transfers between devices with their start and end apart: 19, of which 15 were waited for; matrix products, arithmetic and copies ran while one was open for 4% of the time, Pallas kernels for 3%

profile of v2, /device:TPU:1, one launch (start us, length us, event | category | flops | bytes accessed | tf_op | source)
XLA Modules:
  0.0 134.9 jit_solution(12975995205560669154)
XLA Ops:
  1.3 1.5 %collective-permute-start = (s32[4]{0:T(128)S(1)}, s32[4]{0:T(128)S(1)}, u32[]{:S(2)}, u32[]{:S(2)}) collective-permute-start(s32[4]{0:T(128)S(1)} %compare_select_fusion), channel_id=1, source_target_pairs={{0,1},{1,0},{2,3},{3,2},{4,5},{5,4},{6,7},{7,6},{8,9},{9,8},{10,11... | collective-permute-start | bytes 56 | tf_op jit(solution)/shard_map/ppermute | solution.py:49
  3.4 3.5 %edge_rows.1 = (bf16[4,752,128]{2,1,0:T(8,128)(2,1)}, bf16[2,752,128]{2,1,0:T(8,128)(2,1)}, bf16[1,752,128]{2,1,0:T(8,128)(2,1)}, f32[8,128]{1,0:T(8,128)}) custom-call(s32[32]{0:T(128)} %counts_ref.3, s32[2]{0:T(128)} %pad_add_fusion.place_ref, bf16[4,1440,128]{2,1,0:T(8,128)(2,1)} %state_ref.3, bf16[4,1440,128]{2,1,0:T(8,128)(2,1)} %target_ref.3), custom_call_target="tpu_custom_call" | custom-call | tf_op jit(solution)/shard_map/edge_rows/pallas_call | solution.py:172
  6.9 6.5 %collective-permute-start.2 = (bf16[4,752,128]{2,1,0:T(8,128)(2,1)}, bf16[4,752,128]{2,1,0:T(8,128)(2,1)S(1)}, u32[]{:S(2)}, u32[]{:S(2)}) collective-permute-start(bf16[4,752,128]{2,1,0:T(8,128)(2,1)} %get-tuple-element.20), channel_id=1, source_target_pairs={{0,4},{1,125},{2,6},{3,127},{4,8},{5,1},{6,10},{7,3},{8,12},{9,5},... | collective-permute-start | bytes 2310152 | tf_op jit(solution)/shard_map/ppermute | solution.py:460
  13.3 3.3 %collective-permute-start.1 = (s32[4]{0:T(128)S(1)}, s32[4]{0:T(128)S(1)}, u32[]{:S(2)}, u32[]{:S(2)}) collective-permute-start(s32[4]{0:T(128)S(1)} %fusion.15), channel_id=1, source_target_pairs={{0,2},{1,3},{2,0},{3,1},{4,6},{5,7},{6,4},{7,5},{8,10},{9,11},{10,... | collective-permute-start | bytes 56 | tf_op jit(solution)/shard_map/ppermute | solution.py:49
  16.7 1.3 collective-permute-done.1
  19.4 0.8 compare_bitcast_fusion.3
  20.2 11.0 %collective-permute-done.4 = bf16[1,752,128]{2,1,0:T(8,128)(2,1)S(1)} collective-permute-done((bf16[1,752,128]{2,1,0:T(8,128)(2,1)}, bf16[1,752,128]{2,1,0:T(8,128)(2,1)S(1)}, u32[]{:S(2)}, u32[]{:S(2)}) %collective-permute-start.4) | collective-permute-done | bytes 192544 | tf_op jit(solution)/shard_map/ppermute | solution.py:460
  31.3 1.4 %collective-permute-done.2 = bf16[4,752,128]{2,1,0:T(8,128)(2,1)S(1)} collective-permute-done((bf16[4,752,128]{2,1,0:T(8,128)(2,1)}, bf16[4,752,128]{2,1,0:T(8,128)(2,1)S(1)}, u32[]{:S(2)}, u32[]{:S(2)}) %collective-permute-start.2) | collective-permute-done | bytes 770080 | tf_op jit(solution)/shard_map/ppermute | solution.py:460
  32.9 0.8 constant_dynamic-slice_fusion
  33.8 2.8 %collective-permute-start.5 = (bf16[4,384,128]{2,1,0:T(8,128)(2,1)S(1)}, bf16[4,384,128]{2,1,0:T(8,128)(2,1)S(1)}, u32[]{:S(2)}, u32[]{:S(2)}) collective-permute-start(bf16[4,384,128]{2,1,0:T(8,128)(2,1)S(1)} %get-tuple-element.32), channel_id=1, source_target_pairs={{0,1},{1,0},{2,3},{3,2},{4,5},{5,4},{6,7},{7,6},{8,9},{9,8},{10,11... | collective-permute-start | bytes 1179656 | tf_op jit(solution)/shard_map/ppermute | solution.py:49
  36.5 1.0 fusion.8.wt_ref
  37.5 1.3 fusion.6
  39.6 44.4 %ensemble_step.1 = (f32[2368,128]{1,0:T(8,128)}, f32[4,1,384]{2,1,0:T(1,128)}) custom-call(s32[32]{0:T(128)} %counts_ref.3, s32[4]{0:T(128)} %add.135.seeds_ref, s32[2]{0:T(128)} %pad_add_fusion.place_ref, f32[96]{0:T(128)} %constant.119.clone.weight_ref, bf16[4,1440,128]{2,1,0:T(8,128)(2,1)} %state_ref.3, bf16[4,1440,128]{2,1,0:T(8,128)(2,1)} %target_ref.3, ...), custom_call_target="tpu_custom_call" | custom-call | tf_op jit(solution)/shard_map/ensemble_step/pallas_call | solution.py:408
  84.0 1.2 dynamic-slice_bitcast_fusion
  85.4 1.9 %collective-permute-done.6 = f32[1184,128]{1,0:T(8,128)S(1)} collective-permute-done((f32[1184,128]{1,0:T(8,128)S(1)}, f32[1184,128]{1,0:T(8,128)S(1)}, u32[]{:S(2)}, u32[]{:S(2)}) %collective-permute-start.6) | collective-permute-done | bytes 606240 | tf_op jit(solution)/shard_map/ppermute | solution.py:49
  87.5 1.8 %collective-permute-start.8 = (f32[296,128]{1,0:T(8,128)S(1)}, f32[296,128]{1,0:T(8,128)S(1)}, u32[]{:S(2)}, u32[]{:S(2)}) collective-permute-start(f32[296,128]{1,0:T(8,128)S(1)} %get-tuple-element.40), channel_id=1, source_target_pairs={{0,8},{1,9},{2,10},{3,11},{4,12},{5,13},{6,14},{7,15},{8,0},{9,1},... | collective-permute-start | bytes 454664 | tf_op jit(solution)/shard_map/ppermute | solution.py:49
  89.3 1.7 %collective-permute-start.9 = (f32[296,128]{1,0:T(8,128)S(1)}, f32[296,128]{1,0:T(8,128)S(1)}, u32[]{:S(2)}, u32[]{:S(2)}) collective-permute-start(f32[296,128]{1,0:T(8,128)S(1)} %get-tuple-element.39), channel_id=1, source_target_pairs={{0,12},{1,13},{2,14},{3,15},{4,0},{5,1},{6,2},{7,3},{8,4},{9,5},{1... | collective-permute-start | bytes 454664 | tf_op jit(solution)/shard_map/ppermute | solution.py:49
  91.0 6.3 %collective-permute-done.7 = f32[296,128]{1,0:T(8,128)S(1)} collective-permute-done((f32[296,128]{1,0:T(8,128)S(1)}, f32[296,128]{1,0:T(8,128)S(1)}, u32[]{:S(2)}, u32[]{:S(2)}) %collective-permute-start.7) | collective-permute-done | bytes 151584 | tf_op jit(solution)/shard_map/ppermute | solution.py:49
  97.8 2.9 %collective-permute-start.11 = (f32[296,128]{1,0:T(8,128)S(1)}, f32[296,128]{1,0:T(8,128)S(1)}, u32[]{:S(2)}, u32[]{:S(2)}) collective-permute-start(f32[296,128]{1,0:T(8,128)S(1)} %fusion.12), channel_id=1, source_target_pairs={{0,32},{1,33},{2,34},{3,35},{4,36},{5,37},{6,38},{7,39},{8,40},{9,... | collective-permute-start | bytes 454664 | tf_op jit(solution)/shard_map/ppermute | solution.py:49
  100.7 2.3 %collective-permute-done.10 = f32[296,128]{1,0:T(8,128)S(1)} collective-permute-done((f32[296,128]{1,0:T(8,128)S(1)}, f32[296,128]{1,0:T(8,128)S(1)}, u32[]{:S(2)}, u32[]{:S(2)}) %collective-permute-start.10) | collective-permute-done | bytes 151584 | tf_op jit(solution)/shard_map/ppermute | solution.py:49
  103.0 3.4 %collective-permute-done.11 = f32[296,128]{1,0:T(8,128)S(1)} collective-permute-done((f32[296,128]{1,0:T(8,128)S(1)}, f32[296,128]{1,0:T(8,128)S(1)}, u32[]{:S(2)}, u32[]{:S(2)}) %collective-permute-start.11) | collective-permute-done | bytes 151584 | tf_op jit(solution)/shard_map/ppermute | solution.py:49
  107.2 3.0 %collective-permute-start.13 = (f32[296,128]{1,0:T(8,128)S(1)}, f32[296,128]{1,0:T(8,128)S(1)}, u32[]{:S(2)}, u32[]{:S(2)}) collective-permute-start(f32[296,128]{1,0:T(8,128)S(1)} %add_add_fusion), channel_id=1, source_target_pairs={{0,2},{1,3},{2,0},{3,1},{4,6},{5,7},{6,4},{7,5},{8,10},{9,11},{10,... | collective-permute-start | bytes 454664 | tf_op jit(solution)/shard_map/ppermute | solution.py:49
  110.2 2.6 %collective-permute-done.13 = f32[296,128]{1,0:T(8,128)S(1)} collective-permute-done((f32[296,128]{1,0:T(8,128)S(1)}, f32[296,128]{1,0:T(8,128)S(1)}, u32[]{:S(2)}, u32[]{:S(2)}) %collective-permute-start.13) | collective-permute-done | bytes 151584 | tf_op jit(solution)/shard_map/ppermute | solution.py:49
  112.8 1.6 %collective-permute-start.14 = (f32[296,128]{1,0:T(8,128)S(1)}, f32[296,128]{1,0:T(8,128)S(1)}, u32[]{:S(2)}, u32[]{:S(2)}) collective-permute-start(f32[296,128]{1,0:T(8,128)S(1)} %add.161), channel_id=1, source_target_pairs={{0,64},{1,65},{2,66},{3,67},{4,68},{5,69},{6,70},{7,71},{8,72},{9,... | collective-permute-start | bytes 454664 | tf_op jit(solution)/shard_map/ppermute | solution.py:49
  114.4 4.2 %collective-permute-done.14 = f32[296,128]{1,0:T(8,128)S(1)} collective-permute-done((f32[296,128]{1,0:T(8,128)S(1)}, f32[296,128]{1,0:T(8,128)S(1)}, u32[]{:S(2)}, u32[]{:S(2)}) %collective-permute-start.14) | collective-permute-done | bytes 151584 | tf_op jit(solution)/shard_map/ppermute | solution.py:49
  118.6 0.9 collective-permute-start.15
  119.5 2.9 %collective-permute-start.16 = (f32[296,128]{1,0:T(8,128)S(1)}, f32[296,128]{1,0:T(8,128)S(1)}, u32[]{:S(2)}, u32[]{:S(2)}) collective-permute-start(f32[296,128]{1,0:T(8,128)S(1)} %get-tuple-element.27), channel_id=1, source_target_pairs={{0,8},{1,9},{2,10},{3,11},{4,12},{5,13},{6,14},{7,15},{8,0},{9,1},... | collective-permute-start | bytes 454664 | tf_op jit(solution)/shard_map/ppermute | solution.py:49
  122.4 1.5 %collective-permute-done.15 = f32[296,128]{1,0:T(8,128)S(1)} collective-permute-done((f32[296,128]{1,0:T(8,128)S(1)}, f32[296,128]{1,0:T(8,128)S(1)}, u32[]{:S(2)}, u32[]{:S(2)}) %collective-permute-start.15) | collective-permute-done | bytes 151584 | tf_op jit(solution)/shard_map/ppermute | solution.py:49
  124.0 2.7 %collective-permute-done.16 = f32[296,128]{1,0:T(8,128)S(1)} collective-permute-done((f32[296,128]{1,0:T(8,128)S(1)}, f32[296,128]{1,0:T(8,128)S(1)}, u32[]{:S(2)}, u32[]{:S(2)}) %collective-permute-start.16) | collective-permute-done | bytes 151584 | tf_op jit(solution)/shard_map/ppermute | solution.py:49
  126.8 4.8 %collective-permute-start.18 = (f32[1184,128]{1,0:T(8,128)S(1)}, f32[1184,128]{1,0:T(8,128)S(1)}, u32[]{:S(2)}, u32[]{:S(2)}) collective-permute-start(f32[1184,128]{1,0:T(8,128)S(1)} %bitcast.60), channel_id=1, source_target_pairs={{0,1},{1,0},{2,3},{3,2},{4,5},{5,4},{6,7},{7,6},{8,9},{9,8},{10,11... | collective-permute-start | bytes 1818632 | tf_op jit(solution)/shard_map/ppermute | solution.py:49
  132.4 0.8 collective-permute-done.18
  133.3 1.1 fusion.13
  (48 shorter events, 6.1 us)
Async XLA Ops:
  1.3 5.6 %collective-permute-start = (s32[4]{0:T(128)S(1)}, s32[4]{0:T(128)S(1)}, u32[]{:S(2)}, u32[]{:S(2)}) collective-permute-start(s32[4]{0:T(128)S(1)} %compare_select_fusion), channel_id=1, source_target_pairs={{0,1},{1,0},{2,3},{3,2},{4,5},{5,4},{6,7},{7,6},{8,9},{9,8},{10,11... | collective-permute-start | bytes 56 | tf_op jit(solution)/shard_map/ppermute | solution.py:49
  3.4 15.1 %copy-start.1 = (bf16[3,3,128,128]{3,2,1,0:T(8,128)(2,1)S(1)}, bf16[3,3,128,128]{3,2,1,0:T(8,128)(2,1)}, u32[]{:S(2)}) copy-start(bf16[3,3,128,128]{3,2,1,0:T(8,128)(2,1)} %param.12) | copy-start | bytes 884740
  6.9 25.9 %collective-permute-start.2 = (bf16[4,752,128]{2,1,0:T(8,128)(2,1)}, bf16[4,752,128]{2,1,0:T(8,128)(2,1)S(1)}, u32[]{:S(2)}, u32[]{:S(2)}) collective-permute-start(bf16[4,752,128]{2,1,0:T(8,128)(2,1)} %get-tuple-element.20), channel_id=1, source_target_pairs={{0,4},{1,125},{2,6},{3,127},{4,8},{5,1},{6,10},{7,3},{8,12},{9,5},... | collective-permute-start | bytes 2310152 | tf_op jit(solution)/shard_map/ppermute | solution.py:460
  13.3 4.6 %collective-permute-start.1 = (s32[4]{0:T(128)S(1)}, s32[4]{0:T(128)S(1)}, u32[]{:S(2)}, u32[]{:S(2)}) collective-permute-start(s32[4]{0:T(128)S(1)} %fusion.15), channel_id=1, source_target_pairs={{0,2},{1,3},{2,0},{3,1},{4,6},{5,7},{6,4},{7,5},{8,10},{9,11},{10,... | collective-permute-start | bytes 56 | tf_op jit(solution)/shard_map/ppermute | solution.py:49
  18.4 12.9 %collective-permute-start.3 = (bf16[2,752,128]{2,1,0:T(8,128)(2,1)}, bf16[2,752,128]{2,1,0:T(8,128)(2,1)S(1)}, u32[]{:S(2)}, u32[]{:S(2)}) collective-permute-start(bf16[2,752,128]{2,1,0:T(8,128)(2,1)} %get-tuple-element.22), channel_id=1, source_target_pairs={{0,8},{1,121},{2,10},{3,123},{4,12},{5,125},{6,14},{7,127},{8,16},... | collective-permute-start | bytes 1155080 | tf_op jit(solution)/shard_map/ppermute | solution.py:460
  18.7 12.6 %collective-permute-start.4 = (bf16[1,752,128]{2,1,0:T(8,128)(2,1)}, bf16[1,752,128]{2,1,0:T(8,128)(2,1)S(1)}, u32[]{:S(2)}, u32[]{:S(2)}) collective-permute-start(bf16[1,752,128]{2,1,0:T(8,128)(2,1)} %get-tuple-element.23), channel_id=1, source_target_pairs={{0,12},{1,117},{2,14},{3,119},{4,16},{5,121},{6,18},{7,123},{8,20}... | collective-permute-start | bytes 577544 | tf_op jit(solution)/shard_map/ppermute | solution.py:460
  32.9 4.6 %copy-start.3 = (bf16[3,3,128,128]{3,2,1,0:T(8,128)(2,1)S(1)}, bf16[3,3,128,128]{3,2,1,0:T(8,128)(2,1)}, u32[]{:S(2)}) copy-start(bf16[3,3,128,128]{3,2,1,0:T(8,128)(2,1)} %param.11) | copy-start | bytes 884740
  33.8 5.0 %collective-permute-start.5 = (bf16[4,384,128]{2,1,0:T(8,128)(2,1)S(1)}, bf16[4,384,128]{2,1,0:T(8,128)(2,1)S(1)}, u32[]{:S(2)}, u32[]{:S(2)}) collective-permute-start(bf16[4,384,128]{2,1,0:T(8,128)(2,1)S(1)} %get-tuple-element.32), channel_id=1, source_target_pairs={{0,1},{1,0},{2,3},{3,2},{4,5},{5,4},{6,7},{7,6},{8,9},{9,8},{10,11... | collective-permute-start | bytes 1179656 | tf_op jit(solution)/shard_map/ppermute | solution.py:49
  38.8 0.7 copy-start.2
  84.0 3.3 %copy-start = (f32[2368,128]{1,0:T(8,128)S(1)}, f32[2368,128]{1,0:T(8,128)}, u32[]{:S(2)}) copy-start(f32[2368,128]{1,0:T(8,128)} %get-tuple-element.25) | copy-start | bytes 3637252
  85.2 2.1 %collective-permute-start.6 = (f32[1184,128]{1,0:T(8,128)S(1)}, f32[1184,128]{1,0:T(8,128)S(1)}, u32[]{:S(2)}, u32[]{:S(2)}) collective-permute-start(f32[1184,128]{1,0:T(8,128)S(1)} %dynamic-slice_bitcast_fusion), channel_id=1, source_target_pairs={{0,1},{1,0},{2,3},{3,2},{4,5},{5,4},{6,7},{7,6},{8,9},{9,8},{10,11... | collective-permute-start | bytes 1818632 | tf_op jit(solution)/shard_map/ppermute | solution.py:49
  87.4 9.9 %collective-permute-start.7 = (f32[296,128]{1,0:T(8,128)S(1)}, f32[296,128]{1,0:T(8,128)S(1)}, u32[]{:S(2)}, u32[]{:S(2)}) collective-permute-start(f32[296,128]{1,0:T(8,128)S(1)} %get-tuple-element.38), channel_id=1, source_target_pairs={{0,4},{1,5},{2,6},{3,7},{4,8},{5,9},{6,10},{7,11},{8,12},{9,13},{1... | collective-permute-start | bytes 454664 | tf_op jit(solution)/shard_map/ppermute | solution.py:49
  87.5 9.8 %collective-permute-start.8 = (f32[296,128]{1,0:T(8,128)S(1)}, f32[296,128]{1,0:T(8,128)S(1)}, u32[]{:S(2)}, u32[]{:S(2)}) collective-permute-start(f32[296,128]{1,0:T(8,128)S(1)} %get-tuple-element.40), channel_id=1, source_target_pairs={{0,8},{1,9},{2,10},{3,11},{4,12},{5,13},{6,14},{7,15},{8,0},{9,1},... | collective-permute-start | bytes 454664 | tf_op jit(solution)/shard_map/ppermute | solution.py:49
  89.3 8.4 %collective-permute-start.9 = (f32[296,128]{1,0:T(8,128)S(1)}, f32[296,128]{1,0:T(8,128)S(1)}, u32[]{:S(2)}, u32[]{:S(2)}) collective-permute-start(f32[296,128]{1,0:T(8,128)S(1)} %get-tuple-element.39), channel_id=1, source_target_pairs={{0,12},{1,13},{2,14},{3,15},{4,0},{5,1},{6,2},{7,3},{8,4},{9,5},{1... | collective-permute-start | bytes 454664 | tf_op jit(solution)/shard_map/ppermute | solution.py:49
  97.7 5.3 %collective-permute-start.10 = (f32[296,128]{1,0:T(8,128)S(1)}, f32[296,128]{1,0:T(8,128)S(1)}, u32[]{:S(2)}, u32[]{:S(2)}) collective-permute-start(f32[296,128]{1,0:T(8,128)S(1)} %fusion.12), channel_id=1, source_target_pairs={{0,16},{1,17},{2,18},{3,19},{4,20},{5,21},{6,22},{7,23},{8,24},{9,... | collective-permute-start | bytes 454664 | tf_op jit(solution)/shard_map/ppermute | solution.py:49
  97.8 8.7 %collective-permute-start.11 = (f32[296,128]{1,0:T(8,128)S(1)}, f32[296,128]{1,0:T(8,128)S(1)}, u32[]{:S(2)}, u32[]{:S(2)}) collective-permute-start(f32[296,128]{1,0:T(8,128)S(1)} %fusion.12), channel_id=1, source_target_pairs={{0,32},{1,33},{2,34},{3,35},{4,36},{5,37},{6,38},{7,39},{8,40},{9,... | collective-permute-start | bytes 454664 | tf_op jit(solution)/shard_map/ppermute | solution.py:49
  100.7 6.4 %collective-permute-start.12 = (f32[296,128]{1,0:T(8,128)S(1)}, f32[296,128]{1,0:T(8,128)S(1)}, u32[]{:S(2)}, u32[]{:S(2)}) collective-permute-start(f32[296,128]{1,0:T(8,128)S(1)} %fusion.12), channel_id=1, source_target_pairs={{0,48},{1,49},{2,50},{3,51},{4,52},{5,53},{6,54},{7,55},{8,56},{9,... | collective-permute-start | bytes 454664 | tf_op jit(solution)/shard_map/ppermute | solution.py:49
  107.2 24.5 %copy-start.4 = (f32[4,1,384]{2,1,0:T(1,128)S(1)}, f32[4,1,384]{2,1,0:T(1,128)}, u32[]{:S(2)}) copy-start(f32[4,1,384]{2,1,0:T(1,128)} %get-tuple-element.24) | copy-start | bytes 18436
  107.2 5.6 %collective-permute-start.13 = (f32[296,128]{1,0:T(8,128)S(1)}, f32[296,128]{1,0:T(8,128)S(1)}, u32[]{:S(2)}, u32[]{:S(2)}) collective-permute-start(f32[296,128]{1,0:T(8,128)S(1)} %add_add_fusion), channel_id=1, source_target_pairs={{0,2},{1,3},{2,0},{3,1},{4,6},{5,7},{6,4},{7,5},{8,10},{9,11},{10,... | collective-permute-start | bytes 454664 | tf_op jit(solution)/shard_map/ppermute | solution.py:49
  112.8 5.7 %collective-permute-start.14 = (f32[296,128]{1,0:T(8,128)S(1)}, f32[296,128]{1,0:T(8,128)S(1)}, u32[]{:S(2)}, u32[]{:S(2)}) collective-permute-start(f32[296,128]{1,0:T(8,128)S(1)} %add.161), channel_id=1, source_target_pairs={{0,64},{1,65},{2,66},{3,67},{4,68},{5,69},{6,70},{7,71},{8,72},{9,... | collective-permute-start | bytes 454664 | tf_op jit(solution)/shard_map/ppermute | solution.py:49
  118.6 5.3 %collective-permute-start.15 = (f32[296,128]{1,0:T(8,128)S(1)}, f32[296,128]{1,0:T(8,128)S(1)}, u32[]{:S(2)}, u32[]{:S(2)}) collective-permute-start(f32[296,128]{1,0:T(8,128)S(1)} %get-tuple-element.27), channel_id=1, source_target_pairs={{0,4},{1,5},{2,6},{3,7},{4,8},{5,9},{6,10},{7,11},{8,12},{9,13},{1... | collective-permute-start | bytes 454664 | tf_op jit(solution)/shard_map/ppermute | solution.py:49
  119.5 7.2 %collective-permute-start.16 = (f32[296,128]{1,0:T(8,128)S(1)}, f32[296,128]{1,0:T(8,128)S(1)}, u32[]{:S(2)}, u32[]{:S(2)}) collective-permute-start(f32[296,128]{1,0:T(8,128)S(1)} %get-tuple-element.27), channel_id=1, source_target_pairs={{0,8},{1,9},{2,10},{3,11},{4,12},{5,13},{6,14},{7,15},{8,0},{9,1},... | collective-permute-start | bytes 454664 | tf_op jit(solution)/shard_map/ppermute | solution.py:49
  122.4 4.3 %collective-permute-start.17 = (f32[296,128]{1,0:T(8,128)S(1)}, f32[296,128]{1,0:T(8,128)S(1)}, u32[]{:S(2)}, u32[]{:S(2)}) collective-permute-start(f32[296,128]{1,0:T(8,128)S(1)} %get-tuple-element.27), channel_id=1, source_target_pairs={{0,12},{1,13},{2,14},{3,15},{4,0},{5,1},{6,2},{7,3},{8,4},{9,5},{1... | collective-permute-start | bytes 454664 | tf_op jit(solution)/shard_map/ppermute | solution.py:49
  126.8 6.5 %collective-permute-start.18 = (f32[1184,128]{1,0:T(8,128)S(1)}, f32[1184,128]{1,0:T(8,128)S(1)}, u32[]{:S(2)}, u32[]{:S(2)}) collective-permute-start(f32[1184,128]{1,0:T(8,128)S(1)} %bitcast.60), channel_id=1, source_target_pairs={{0,1},{1,0},{2,3},{3,2},{4,5},{5,4},{6,7},{7,6},{8,9},{9,8},{10,11... | collective-permute-start | bytes 1818632 | tf_op jit(solution)/shard_map/ppermute | solution.py:49

commit v3 on v2

--- a/solution.py
+++ b/solution.py
@@ -77,10 +77,6 @@
     for d, g in enumerate(got, 1):
         out = lax.dynamic_update_index_in_dim(out, g, (place - d) % n, 0)
     return out.reshape(n * value.shape[0], C)
-
-
-def sigmoid(a):
-    return 0.5 * jnp.tanh(0.5 * a) + 0.5
 
 
 def chip_row(half, src, r, dst, sem):
@@ -184,8 +180,8 @@
     state_ref, target_ref, mine_ref, other_ref,
     amp_ref, w1_ref, w2_ref, wt_ref,
     grads_ref, cells_ref,
-    state_s, tgt_s, hash_s, buf_s, cbuf_s, crps_s,
-    in3_s, hid3_s, cot3_s, pre_s, fc_s, ya_s, yb_s, acc_s, sem,
+    state_s, tgt_s, hash_s, bufs, cbuf_s, crps_s,
+    in3, hid3, cot3_s, pre_s, fc_s, ya_s, yb_s, acc_s, sem,
 ):
     band = place_ref[0]
     quarter = place_ref[1]
@@ -197,15 +193,15 @@
     copies += own_window(quarter, target_ref, tgt_s.at[pl.ds(1, SLOTS)], sem.at[1])
     start(copies)
 
-    buf_s[0:PAD] = jnp.zeros((PAD, C), F32)
-    buf_s[PAD + J :] = jnp.zeros((PAD, C), F32)
+    for buf in bufs:
+        buf[0:PAD] = jnp.zeros((PAD, C), F32)
+        buf[PAD + J :] = jnp.zeros((PAD, C), F32)
 
     cols = lax.broadcasted_iota(jnp.int32, (J, C), 0)
     chan = lax.broadcasted_iota(jnp.int32, (J, C), 1)
     lon = quarter * OWN - LEFT + cols
     lon = jnp.where(lon < 0, lon + LON, jnp.where(lon >= LON, lon - LON, lon))
     hash_s[...] = lon * 668265263 + chan * 1274126177
-    own_col = ((cols >= LEFT) & (cols < LEFT + OWN)).astype(F32)
 
     wait(copies)
 
@@ -225,73 +221,90 @@
     def _():
         put_edges(other_ref, mine_ref)
 
-    def valid(e):
+    def outside(e):
         g = offset - DEPTH + e
-        return ((g >= 0) & (g < ROWS_TOTAL)).astype(F32)
-
-    def put3(ref, m, e, v):
-        buf_s[PAD : PAD + J] = v
-        ref[m, e, :, C : 2 * C] = v.astype(BF)
-        ref[m, e, :, 0:C] = buf_s[PAD - 1 : PAD - 1 + J].astype(BF)
-        ref[m, e, :, 2 * C :] = buf_s[PAD + 1 : PAD + 1 + J].astype(BF)
+        return (g < 0) | (g >= ROWS_TOTAL)
+
+    def trim(ref, m, slot):
+        ref[m, slot, 0:LEFT] = jnp.zeros((LEFT, C), BF)
+        ref[m, slot, LEFT + OWN :] = jnp.zeros((J - OWN - LEFT, C), BF)
+
+    for e in (0, 1, 2):
+
+        @pl.when(outside(e))
+        def _():
+            state_s[e] = jnp.zeros((J, C), BF)
+
+    for e in range(DEPTH + 1, EXT):
+
+        @pl.when(outside(e))
+        def _():
+            state_s[e] = jnp.zeros((J, C), BF)
+
+    turn = [0]
+
+    def put3(ref, m, slot, v):
+        buf = bufs[turn[0] % len(bufs)]
+        turn[0] += 1
+        buf[PAD : PAD + J] = v
+        ref[m, slot, :, C : 2 * C] = v.astype(BF)
+        ref[m, slot, :, 0:C] = buf[PAD - 1 : PAD - 1 + J].astype(BF)
+        ref[m, slot, :, 2 * C :] = buf[PAD + 1 : PAD + 1 + J].astype(BF)
 
     amp = amp_ref[...]
-
     amp_step = amp * (1.0 / 32768.0)
     amp_base = amp * (0.5 / 32768.0 - 1.0)
 
-    def make_inputs(i, _):
-        e, m = i // MEM, i % MEM
-        g = offset - DEPTH + e
-        inside = (g >= 0) & (g < ROWS_TOTAL)
-
-        @pl.when(inside)
-        def _():
-            h = hash_s[...] + (g * 374761393 + seeds_ref[m] * 1103515245)
+    def make_inputs(m, k):
+        seed = seeds_ref[jnp.minimum(m, MEM - 1)] * 1103515245
+        for j in range(2):
+            e = 2 * k + j
+            live = jnp.where(outside(e), 0.0, 1.0)
+            h = hash_s[...] + ((offset - DEPTH + e) * 374761393 + seed)
             h = h ^ (h >> 13)
             h = h * 1274126177
             h = h ^ (h >> 16)
-            v = (state_s[e].astype(F32) + amp_base) + (h & 65535).astype(F32) * amp_step
-            put3(in3_s, m, e, v)
-
-        @pl.when(jnp.logical_not(inside))
-        def _():
-            in3_s[m, e] = jnp.zeros((J, 3 * C), BF)
-
+            v = (state_s[e].astype(F32) + amp_base * live) + (h & 65535).astype(F32) * (
+                amp_step * live
+            )
+            put3(in3[k], m, j, v)
+
+    def conv_pair(top, bottom, m, w):
+        lhs = jnp.concatenate([top[m, 0], top[m, 1], bottom[m, 0], bottom[m, 1]], axis=1)
+        return jnp.dot(lhs, w[...], preferred_element_type=F32)
+
+    def make_hidden(m, p):
+        out = conv_pair(in3[p], in3[p + 1], m, w1_ref)
+        for j in range(2):
+            e = 1 + 2 * p + j
+            a = out[:, j * C : (j + 1) * C]
+            if DEPTH <= e < DEPTH + SLOTS:
+                pre_s[m, e - DEPTH] = a
+            half = jnp.where(outside(e), 0.0, 0.5)
+            put3(hid3[p], m, j, (a * half) * (1.0 + jnp.tanh(0.5 * a)))
+
+    def make_forecast(m, p):
+        out = conv_pair(hid3[p], hid3[p + 1], m, w2_ref)
+        for j in range(2):
+            v = in3[p + 1][m, j, :, C : 2 * C].astype(F32) + out[:, j * C : (j + 1) * C]
+            fc_s[m, 2 * p + j] = v.astype(BF)
+
+    def member(m, _):
+        make_inputs(m, 0)
+        make_inputs(m, 1)
+        make_inputs(m, 2)
+        make_hidden(m, 0)
+        make_inputs(m, 3)
+        make_hidden(m, 1)
+        make_inputs(m, 4)
+        make_forecast(m, 0)
+        make_hidden(m, 2)
+        make_forecast(m, 1)
+        make_hidden(m, 3)
+        make_forecast(m, 2)
         return 0
 
-    lax.fori_loop(0, EXT * MEM, make_inputs, 0)
-
-    def conv_pair(ref, m, e, w):
-        lhs = jnp.concatenate([ref[m, e + s] for s in range(4)], axis=1)
-        return jnp.dot(lhs, w[...], preferred_element_type=F32)
-
-    def make_hidden(i, _):
-        p, m = i // MEM, i % MEM
-        out = conv_pair(in3_s, m, 2 * p, w1_ref)
-        for k in range(2):
-            e = 1 + 2 * p + k
-            a = out[:, k * C : (k + 1) * C]
-
-            @pl.when((e >= DEPTH) & (e < DEPTH + SLOTS))
-            def _():
-                pre_s[m, e - DEPTH] = a
-
-            put3(hid3_s, m, e - 1, a * sigmoid(a) * valid(e))
-        return 0
-
-    lax.fori_loop(0, 4 * MEM, make_hidden, 0)
-
-    def make_forecast(i, _):
-        p, m = i // MEM, i % MEM
-        out = conv_pair(hid3_s, m, 2 * p, w2_ref)
-        for k in range(2):
-            e = 2 + 2 * p + k
-            v = (in3_s[m, e, :, C : 2 * C].astype(F32) + out[:, k * C : (k + 1) * C]) * valid(e)
-            fc_s[m, e - 2] = v.astype(BF)
-        return 0
-
-    lax.fori_loop(0, 3 * MEM, make_forecast, 0)
+    lax.fori_loop(0, MEM, member, 0)
 
     pair_scale = 1.0 / (MEM * (MEM - 1))
     factor = 1.0 / math.sqrt(ROWS_TOTAL * LON)
@@ -301,7 +314,7 @@
     def make_crps(r, loss):
         e = r + 2
         g = jnp.clip(offset - DEPTH + e, 0, ROWS_TOTAL - 1)
-        weight = weight_ref[g] * valid(e)
+        weight = jnp.where(outside(e), 0.0, weight_ref[g])
         mine = ((r >= 1) & (r < 1 + n)).astype(F32)
         scale = weight * (factor * pair_scale)
         slot = jnp.clip(r - 1, 0, SLOTS - 1)
@@ -343,7 +356,12 @@
         @pl.when((r >= 1) & (r < 1 + SLOTS))
         def _():
             for m in range(MEM):
-                ya_s[m, slot] = (cbuf_s[m, PAD : PAD + J] * (own_col * mine)).astype(BF)
+                ya_s[m, slot] = cot3_s[m, r, :, C : 2 * C]
+                trim(ya_s, m, slot)
+            @pl.when(r > n)
+            def _():
+                ya_s[:, slot] = jnp.zeros((MEM, J, C), BF)
+
             cells_ref[slot] = jnp.sum(jnp.transpose(crps_s[...]), axis=0, keepdims=True) * (
                 weight * mine * (1.0 / C)
             )
@@ -360,19 +378,21 @@
 
     def make_pre_cot(i, _):
         p, m = i // MEM, i % MEM
-        out = conv_pair(cot3_s, m, 2 * p, wt_ref)
+        lhs = jnp.concatenate([cot3_s[m, 2 * p + r] for r in range(4)], axis=1)
+        out = jnp.dot(lhs, wt_ref[...], preferred_element_type=F32)
         for k in range(2):
             s = 2 * p + k
             a = pre_s[m, s]
-            sig = sigmoid(a)
-            mine = (s < n).astype(F32)
-            v = out[:, k * C : (k + 1) * C] * (sig * (1.0 + a * (1.0 - sig))) * (own_col * mine)
+            t = jnp.tanh(0.5 * a)
+            mine = jnp.where(s < n, 0.25, 0.0)
+            v = out[:, k * C : (k + 1) * C] * (((1.0 + t) * mine) * (2.0 + a * (1.0 - t)))
             yb_s[m, s] = v.astype(BF)
+            trim(yb_s, m, s)
         return 0
 
     lax.fori_loop(0, 2 * MEM, make_pre_cot, 0)
 
-    def weight_grad(x3, first, y, row0):
+    def weight_grad(rows, y, row0):
         acc_s[...] = jnp.zeros_like(acc_s)
 
         def step(m, _):
@@ -383,11 +403,16 @@
                 ],
                 axis=0,
             )
-            for s in range(4):
-                xs = jnp.concatenate([x3[m, first + s], x3[m, first + 2 + s]], axis=0)
-                acc_s[:, s * 384 : (s + 1) * 384] += lax.dot_general(
-                    ys, xs, (((0,), (0,)), ((), ())), preferred_element_type=F32
-                )
+            xs = jnp.concatenate(
+                [
+                    jnp.concatenate([ref[m, j] for ref, j in rows[a : a + 4]], axis=1)
+                    for a in (0, 2)
+                ],
+                axis=0,
+            )
+            acc_s[...] += lax.dot_general(
+                ys, xs, (((0,), (0,)), ((), ())), preferred_element_type=F32
+            )
             return 0
 
         lax.fori_loop(0, MEM, step, 0)
@@ -395,8 +420,8 @@
             blk = acc_s[0:C, k * C : (k + 1) * C] + acc_s[C:, 384 + k * C : 384 + (k + 1) * C]
             grads_ref[row0 + k * C : row0 + (k + 1) * C] = jnp.transpose(blk)
 
-    weight_grad(in3_s, 2, yb_s, 0)
-    weight_grad(hid3_s, 1, ya_s, 1152)
+    weight_grad([(in3[e // 2], e % 2) for e in range(2, 8)], yb_s, 0)
+    weight_grad([(hid3[(e - 1) // 2], (e - 1) % 2) for e in range(2, 8)], ya_s, 1152)
     total = jnp.sum(loss, axis=1, keepdims=True) * (1.0 / (ROWS_TOTAL * LON))
     grads_ref[2304:R] = jnp.broadcast_to(total, (R - 2304, C))
 
@@ -417,11 +442,11 @@
             pltpu.VMEM((EXT, J, C), BF),
             pltpu.VMEM((SLOTS + 2, J, C), BF),
             pltpu.VMEM((J, C), jnp.int32),
-            pltpu.VMEM((J + 2 * PAD, C), F32),
+            [pltpu.VMEM((J + 2 * PAD, C), F32) for _ in range(6)],
             pltpu.VMEM((MEM, J + 2 * PAD, C), F32),
             pltpu.VMEM((J, C), F32),
-            pltpu.VMEM((MEM, EXT, J, 3 * C), BF),
-            pltpu.VMEM((MEM, EXT - 2, J, 3 * C), BF),
+            [pltpu.VMEM((MEM + (k < 3), 2, J, 3 * C), BF) for k in range(5)],
+            [pltpu.VMEM((MEM, 2, J, 3 * C), BF) for _ in range(4)],
             pltpu.VMEM((MEM, EXT - 4, J, 3 * C), BF),
             pltpu.VMEM((MEM, SLOTS, J, C), F32),
             pltpu.VMEM((MEM, EXT - 4, J, C), BF),

time: 135 us -> 125 us (0.926)
  Pallas kernels: 47.9 us -> 38.2 us
    pallas_call x1, Pallas kernels: 44.4 us -> 34.7 us  [local_step(): pl.pallas_call(kernel, out_shape=(jax.ShapeDtypeStruct((R, C), F32), jax....]
  transfers between devices with their start and end apart: 19 -> 19, of which waited for: 15 -> 13; matrix products, arithmetic and copies ran while one was open for 4% -> 4% of each run, Pallas kernels for 3% -> 3%
where the time goes in v3:
time: 125 us
  waiting for transfers between devices  41.5 us (33%)
  Pallas kernels  38.2 us (31%)
  starting transfers between devices  33.8 us (27%)
  local copies, waits for them, and re-layouts  5.64 us (5%)
  other arithmetic  4.64 us (4%)
  between operations  1.51 us (1%)
    pallas_call x1, Pallas kernels, local_step(): pl.pallas_call(kernel, out_shape=(jax.ShapeDtypeStruct((R, C), F32), jax....  34.7 us
    ppermute x16, waiting for transfers between devices, shift(): return lax.ppermute(value, BM, pairs)  29 us
    ppermute x16, starting transfers between devices, shift(): return lax.ppermute(value, BM, pairs)  26.6 us
    ppermute x3, waiting for transfers between devices, send(): return lax.ppermute(value, BM, pairs)  12.5 us
    ppermute x3, starting transfers between devices, send(): return lax.ppermute(value, BM, pairs)  7.17 us
    pallas_call x1, Pallas kernels, edges(): pl.pallas_call(edge_kernel, out_shape=(rows(4), rows(2), rows(1), jax.Sha...  3.45 us
  transfers between devices with their start and end apart: 19, of which 13 were waited for; matrix products, arithmetic and copies ran while one was open for 4% of the time, Pallas kernels for 3%

profile of v3, /device:TPU:1, one launch (start us, length us, event | category | flops | bytes accessed | tf_op | source)
XLA Modules:
  0.0 125.2 jit_solution(8494934018282815905)
XLA Ops:
  1.3 1.5 %collective-permute-start = (s32[4]{0:T(128)S(1)}, s32[4]{0:T(128)S(1)}, u32[]{:S(2)}, u32[]{:S(2)}) collective-permute-start(s32[4]{0:T(128)S(1)} %compare_select_fusion), channel_id=1, source_target_pairs={{0,1},{1,0},{2,3},{3,2},{4,5},{5,4},{6,7},{7,6},{8,9},{9,8},{10,11... | collective-permute-start | bytes 56 | tf_op jit(solution)/shard_map/ppermute | solution.py:49
  3.4 3.5 %edge_rows.1 = (bf16[4,752,128]{2,1,0:T(8,128)(2,1)}, bf16[2,752,128]{2,1,0:T(8,128)(2,1)}, bf16[1,752,128]{2,1,0:T(8,128)(2,1)}, f32[8,128]{1,0:T(8,128)}) custom-call(s32[32]{0:T(128)} %counts_ref.3, s32[2]{0:T(128)} %pad_add_fusion.place_ref, bf16[4,1440,128]{2,1,0:T(8,128)(2,1)} %state_ref.3, bf16[4,1440,128]{2,1,0:T(8,128)(2,1)} %target_ref.3), custom_call_target="tpu_custom_call" | custom-call | tf_op jit(solution)/shard_map/edge_rows/pallas_call | solution.py:168
  6.9 6.5 %collective-permute-start.2 = (bf16[4,752,128]{2,1,0:T(8,128)(2,1)}, bf16[4,752,128]{2,1,0:T(8,128)(2,1)S(1)}, u32[]{:S(2)}, u32[]{:S(2)}) collective-permute-start(bf16[4,752,128]{2,1,0:T(8,128)(2,1)} %get-tuple-element.20), channel_id=1, source_target_pairs={{0,4},{1,125},{2,6},{3,127},{4,8},{5,1},{6,10},{7,3},{8,12},{9,5},... | collective-permute-start | bytes 2310152 | tf_op jit(solution)/shard_map/ppermute | solution.py:485
  13.3 3.3 %collective-permute-start.1 = (s32[4]{0:T(128)S(1)}, s32[4]{0:T(128)S(1)}, u32[]{:S(2)}, u32[]{:S(2)}) collective-permute-start(s32[4]{0:T(128)S(1)} %fusion.15), channel_id=1, source_target_pairs={{0,2},{1,3},{2,0},{3,1},{4,6},{5,7},{6,4},{7,5},{8,10},{9,11},{10,... | collective-permute-start | bytes 56 | tf_op jit(solution)/shard_map/ppermute | solution.py:49
  16.7 1.3 collective-permute-done.1
  19.4 0.8 compare_bitcast_fusion.3
  20.2 11.0 %collective-permute-done.4 = bf16[1,752,128]{2,1,0:T(8,128)(2,1)S(1)} collective-permute-done((bf16[1,752,128]{2,1,0:T(8,128)(2,1)}, bf16[1,752,128]{2,1,0:T(8,128)(2,1)S(1)}, u32[]{:S(2)}, u32[]{:S(2)}) %collective-permute-start.4) | collective-permute-done | bytes 192544 | tf_op jit(solution)/shard_map/ppermute | solution.py:485
  31.3 1.4 %collective-permute-done.2 = bf16[4,752,128]{2,1,0:T(8,128)(2,1)S(1)} collective-permute-done((bf16[4,752,128]{2,1,0:T(8,128)(2,1)}, bf16[4,752,128]{2,1,0:T(8,128)(2,1)S(1)}, u32[]{:S(2)}, u32[]{:S(2)}) %collective-permute-start.2) | collective-permute-done | bytes 770080 | tf_op jit(solution)/shard_map/ppermute | solution.py:485
  32.9 0.8 constant_dynamic-slice_fusion
  33.8 2.7 %collective-permute-start.5 = (bf16[4,384,128]{2,1,0:T(8,128)(2,1)S(1)}, bf16[4,384,128]{2,1,0:T(8,128)(2,1)S(1)}, u32[]{:S(2)}, u32[]{:S(2)}) collective-permute-start(bf16[4,384,128]{2,1,0:T(8,128)(2,1)S(1)} %get-tuple-element.32), channel_id=1, source_target_pairs={{0,1},{1,0},{2,3},{3,2},{4,5},{5,4},{6,7},{7,6},{8,9},{9,8},{10,11... | collective-permute-start | bytes 1179656 | tf_op jit(solution)/shard_map/ppermute | solution.py:49
  36.5 1.0 fusion.8.wt_ref
  37.4 1.3 %fusion.6 = (bf16[1536,256]{1,0:T(8,128)(2,1)}, bf16[1536,256]{1,0:T(8,128)(2,1)}) fusion(bf16[1152,128]{1,0:T(8,128)(2,1)S(1)} %bitcast.70, bf16[1152,128]{1,0:T(8,128)(2,1)S(1)} %bitcast.66), kind=kLoop, calls=%fused_computation.8 | loop fusion | flops 5505024 | bytes 2162688 | tf_op jit(solution)/shard_map/concatenate | solution.py:465
  38.7 0.7 copy-done.2
  39.5 34.7 %ensemble_step.1 = (f32[2368,128]{1,0:T(8,128)}, f32[4,1,384]{2,1,0:T(1,128)}) custom-call(s32[32]{0:T(128)} %counts_ref.3, s32[4]{0:T(128)} %add.135.seeds_ref, s32[2]{0:T(128)} %pad_add_fusion.place_ref, f32[96]{0:T(128)} %constant.119.clone.weight_ref, bf16[4,1440,128]{2,1,0:T(8,128)(2,1)} %state_ref.3, bf16[4,1440,128]{2,1,0:T(8,128)(2,1)} %target_ref.3, ...), custom_call_target="tpu_custom_call" | custom-call | tf_op jit(solution)/shard_map/ensemble_step/pallas_call | solution.py:433
  74.2 1.2 dynamic-slice_bitcast_fusion
  75.6 1.9 %collective-permute-done.6 = f32[1184,128]{1,0:T(8,128)S(1)} collective-permute-done((f32[1184,128]{1,0:T(8,128)S(1)}, f32[1184,128]{1,0:T(8,128)S(1)}, u32[]{:S(2)}, u32[]{:S(2)}) %collective-permute-start.6) | collective-permute-done | bytes 606240 | tf_op jit(solution)/shard_map/ppermute | solution.py:49
  78.2 2.2 %collective-permute-start.9 = (f32[296,128]{1,0:T(8,128)S(1)}, f32[296,128]{1,0:T(8,128)S(1)}, u32[]{:S(2)}, u32[]{:S(2)}) collective-permute-start(f32[296,128]{1,0:T(8,128)S(1)} %get-tuple-element.39), channel_id=1, source_target_pairs={{0,12},{1,13},{2,14},{3,15},{4,0},{5,1},{6,2},{7,3},{8,4},{9,5},{1... | collective-permute-start | bytes 454664 | tf_op jit(solution)/shard_map/ppermute | solution.py:49
  80.4 7.2 %collective-permute-done.7 = f32[296,128]{1,0:T(8,128)S(1)} collective-permute-done((f32[296,128]{1,0:T(8,128)S(1)}, f32[296,128]{1,0:T(8,128)S(1)}, u32[]{:S(2)}, u32[]{:S(2)}) %collective-permute-start.7) | collective-permute-done | bytes 151584 | tf_op jit(solution)/shard_map/ppermute | solution.py:49
  88.0 1.7 %collective-permute-start.11 = (f32[296,128]{1,0:T(8,128)S(1)}, f32[296,128]{1,0:T(8,128)S(1)}, u32[]{:S(2)}, u32[]{:S(2)}) collective-permute-start(f32[296,128]{1,0:T(8,128)S(1)} %fusion.12), channel_id=1, source_target_pairs={{0,32},{1,33},{2,34},{3,35},{4,36},{5,37},{6,38},{7,39},{8,40},{9,... | collective-permute-start | bytes 454664 | tf_op jit(solution)/shard_map/ppermute | solution.py:49
  89.7 1.0 collective-permute-start.12
  90.7 4.8 %collective-permute-done.10 = f32[296,128]{1,0:T(8,128)S(1)} collective-permute-done((f32[296,128]{1,0:T(8,128)S(1)}, f32[296,128]{1,0:T(8,128)S(1)}, u32[]{:S(2)}, u32[]{:S(2)}) %collective-permute-start.10) | collective-permute-done | bytes 151584 | tf_op jit(solution)/shard_map/ppermute | solution.py:49
  95.5 1.7 %collective-permute-done.12 = f32[296,128]{1,0:T(8,128)S(1)} collective-permute-done((f32[296,128]{1,0:T(8,128)S(1)}, f32[296,128]{1,0:T(8,128)S(1)}, u32[]{:S(2)}, u32[]{:S(2)}) %collective-permute-start.12) | collective-permute-done | bytes 151584 | tf_op jit(solution)/shard_map/ppermute | solution.py:49
  97.2 3.5 %collective-permute-start.13 = (f32[296,128]{1,0:T(8,128)S(1)}, f32[296,128]{1,0:T(8,128)S(1)}, u32[]{:S(2)}, u32[]{:S(2)}) collective-permute-start(f32[296,128]{1,0:T(8,128)S(1)} %add_add_fusion), channel_id=1, source_target_pairs={{0,2},{1,3},{2,0},{3,1},{4,6},{5,7},{6,4},{7,5},{8,10},{9,11},{10,... | collective-permute-start | bytes 454664 | tf_op jit(solution)/shard_map/ppermute | solution.py:49
  100.7 2.6 %collective-permute-done.13 = f32[296,128]{1,0:T(8,128)S(1)} collective-permute-done((f32[296,128]{1,0:T(8,128)S(1)}, f32[296,128]{1,0:T(8,128)S(1)}, u32[]{:S(2)}, u32[]{:S(2)}) %collective-permute-start.13) | collective-permute-done | bytes 151584 | tf_op jit(solution)/shard_map/ppermute | solution.py:49
  103.7 4.3 %collective-permute-done.14 = f32[296,128]{1,0:T(8,128)S(1)} collective-permute-done((f32[296,128]{1,0:T(8,128)S(1)}, f32[296,128]{1,0:T(8,128)S(1)}, u32[]{:S(2)}, u32[]{:S(2)}) %collective-permute-start.14) | collective-permute-done | bytes 151584 | tf_op jit(solution)/shard_map/ppermute | solution.py:49
  108.1 1.0 collective-permute-start.15
  109.0 2.8 %collective-permute-start.16 = (f32[296,128]{1,0:T(8,128)S(1)}, f32[296,128]{1,0:T(8,128)S(1)}, u32[]{:S(2)}, u32[]{:S(2)}) collective-permute-start(f32[296,128]{1,0:T(8,128)S(1)} %get-tuple-element.27), channel_id=1, source_target_pairs={{0,8},{1,9},{2,10},{3,11},{4,12},{5,13},{6,14},{7,15},{8,0},{9,1},... | collective-permute-start | bytes 454664 | tf_op jit(solution)/shard_map/ppermute | solution.py:49
  111.9 1.5 %collective-permute-done.15 = f32[296,128]{1,0:T(8,128)S(1)} collective-permute-done((f32[296,128]{1,0:T(8,128)S(1)}, f32[296,128]{1,0:T(8,128)S(1)}, u32[]{:S(2)}, u32[]{:S(2)}) %collective-permute-start.15) | collective-permute-done | bytes 151584 | tf_op jit(solution)/shard_map/ppermute | solution.py:49
  113.4 2.7 %collective-permute-done.16 = f32[296,128]{1,0:T(8,128)S(1)} collective-permute-done((f32[296,128]{1,0:T(8,128)S(1)}, f32[296,128]{1,0:T(8,128)S(1)}, u32[]{:S(2)}, u32[]{:S(2)}) %collective-permute-start.16) | collective-permute-done | bytes 151584 | tf_op jit(solution)/shard_map/ppermute | solution.py:49
  116.1 5.8 %collective-permute-start.18 = (f32[1184,128]{1,0:T(8,128)S(1)}, f32[1184,128]{1,0:T(8,128)S(1)}, u32[]{:S(2)}, u32[]{:S(2)}) collective-permute-start(f32[1184,128]{1,0:T(8,128)S(1)} %bitcast.60), channel_id=1, source_target_pairs={{0,1},{1,0},{2,3},{3,2},{4,5},{5,4},{6,7},{7,6},{8,9},{9,8},{10,11... | collective-permute-start | bytes 1818632 | tf_op jit(solution)/shard_map/ppermute | solution.py:49
  122.8 0.8 collective-permute-done.18
  123.6 1.1 fusion.13
  (48 shorter events, 5.4 us)
Async XLA Ops:
  1.3 5.6 %collective-permute-start = (s32[4]{0:T(128)S(1)}, s32[4]{0:T(128)S(1)}, u32[]{:S(2)}, u32[]{:S(2)}) collective-permute-start(s32[4]{0:T(128)S(1)} %compare_select_fusion), channel_id=1, source_target_pairs={{0,1},{1,0},{2,3},{3,2},{4,5},{5,4},{6,7},{7,6},{8,9},{9,8},{10,11... | collective-permute-start | bytes 56 | tf_op jit(solution)/shard_map/ppermute | solution.py:49
  3.4 15.1 %copy-start.1 = (bf16[3,3,128,128]{3,2,1,0:T(8,128)(2,1)S(1)}, bf16[3,3,128,128]{3,2,1,0:T(8,128)(2,1)}, u32[]{:S(2)}) copy-start(bf16[3,3,128,128]{3,2,1,0:T(8,128)(2,1)} %param.12) | copy-start | bytes 884740
  6.9 25.9 %collective-permute-start.2 = (bf16[4,752,128]{2,1,0:T(8,128)(2,1)}, bf16[4,752,128]{2,1,0:T(8,128)(2,1)S(1)}, u32[]{:S(2)}, u32[]{:S(2)}) collective-permute-start(bf16[4,752,128]{2,1,0:T(8,128)(2,1)} %get-tuple-element.20), channel_id=1, source_target_pairs={{0,4},{1,125},{2,6},{3,127},{4,8},{5,1},{6,10},{7,3},{8,12},{9,5},... | collective-permute-start | bytes 2310152 | tf_op jit(solution)/shard_map/ppermute | solution.py:485
  13.3 4.6 %collective-permute-start.1 = (s32[4]{0:T(128)S(1)}, s32[4]{0:T(128)S(1)}, u32[]{:S(2)}, u32[]{:S(2)}) collective-permute-start(s32[4]{0:T(128)S(1)} %fusion.15), channel_id=1, source_target_pairs={{0,2},{1,3},{2,0},{3,1},{4,6},{5,7},{6,4},{7,5},{8,10},{9,11},{10,... | collective-permute-start | bytes 56 | tf_op jit(solution)/shard_map/ppermute | solution.py:49
  18.4 12.9 %collective-permute-start.3 = (bf16[2,752,128]{2,1,0:T(8,128)(2,1)}, bf16[2,752,128]{2,1,0:T(8,128)(2,1)S(1)}, u32[]{:S(2)}, u32[]{:S(2)}) collective-permute-start(bf16[2,752,128]{2,1,0:T(8,128)(2,1)} %get-tuple-element.22), channel_id=1, source_target_pairs={{0,8},{1,121},{2,10},{3,123},{4,12},{5,125},{6,14},{7,127},{8,16},... | collective-permute-start | bytes 1155080 | tf_op jit(solution)/shard_map/ppermute | solution.py:485
  18.7 12.6 %collective-permute-start.4 = (bf16[1,752,128]{2,1,0:T(8,128)(2,1)}, bf16[1,752,128]{2,1,0:T(8,128)(2,1)S(1)}, u32[]{:S(2)}, u32[]{:S(2)}) collective-permute-start(bf16[1,752,128]{2,1,0:T(8,128)(2,1)} %get-tuple-element.23), channel_id=1, source_target_pairs={{0,12},{1,117},{2,14},{3,119},{4,16},{5,121},{6,18},{7,123},{8,20}... | collective-permute-start | bytes 577544 | tf_op jit(solution)/shard_map/ppermute | solution.py:485
  32.9 4.5 %copy-start.3 = (bf16[3,3,128,128]{3,2,1,0:T(8,128)(2,1)S(1)}, bf16[3,3,128,128]{3,2,1,0:T(8,128)(2,1)}, u32[]{:S(2)}) copy-start(bf16[3,3,128,128]{3,2,1,0:T(8,128)(2,1)} %param.11) | copy-start | bytes 884740
  33.8 5.0 %collective-permute-start.5 = (bf16[4,384,128]{2,1,0:T(8,128)(2,1)S(1)}, bf16[4,384,128]{2,1,0:T(8,128)(2,1)S(1)}, u32[]{:S(2)}, u32[]{:S(2)}) collective-permute-start(bf16[4,384,128]{2,1,0:T(8,128)(2,1)S(1)} %get-tuple-element.32), channel_id=1, source_target_pairs={{0,1},{1,0},{2,3},{3,2},{4,5},{5,4},{6,7},{7,6},{8,9},{9,8},{10,11... | collective-permute-start | bytes 1179656 | tf_op jit(solution)/shard_map/ppermute | solution.py:49
  38.7 0.7 copy-start.2
  74.2 3.3 %copy-start = (f32[2368,128]{1,0:T(8,128)S(1)}, f32[2368,128]{1,0:T(8,128)}, u32[]{:S(2)}) copy-start(f32[2368,128]{1,0:T(8,128)} %get-tuple-element.25) | copy-start | bytes 3637252
  75.4 2.1 %collective-permute-start.6 = (f32[1184,128]{1,0:T(8,128)S(1)}, f32[1184,128]{1,0:T(8,128)S(1)}, u32[]{:S(2)}, u32[]{:S(2)}) collective-permute-start(f32[1184,128]{1,0:T(8,128)S(1)} %dynamic-slice_bitcast_fusion), channel_id=1, source_target_pairs={{0,1},{1,0},{2,3},{3,2},{4,5},{5,4},{6,7},{7,6},{8,9},{9,8},{10,11... | collective-permute-start | bytes 1818632 | tf_op jit(solution)/shard_map/ppermute | solution.py:49
  77.7 9.9 %collective-permute-start.7 = (f32[296,128]{1,0:T(8,128)S(1)}, f32[296,128]{1,0:T(8,128)S(1)}, u32[]{:S(2)}, u32[]{:S(2)}) collective-permute-start(f32[296,128]{1,0:T(8,128)S(1)} %get-tuple-element.38), channel_id=1, source_target_pairs={{0,4},{1,5},{2,6},{3,7},{4,8},{5,9},{6,10},{7,11},{8,12},{9,13},{1... | collective-permute-start | bytes 454664 | tf_op jit(solution)/shard_map/ppermute | solution.py:49
  77.7 9.9 %collective-permute-start.8 = (f32[296,128]{1,0:T(8,128)S(1)}, f32[296,128]{1,0:T(8,128)S(1)}, u32[]{:S(2)}, u32[]{:S(2)}) collective-permute-start(f32[296,128]{1,0:T(8,128)S(1)} %get-tuple-element.40), channel_id=1, source_target_pairs={{0,8},{1,9},{2,10},{3,11},{4,12},{5,13},{6,14},{7,15},{8,0},{9,1},... | collective-permute-start | bytes 454664 | tf_op jit(solution)/shard_map/ppermute | solution.py:49
  78.2 9.7 %collective-permute-start.9 = (f32[296,128]{1,0:T(8,128)S(1)}, f32[296,128]{1,0:T(8,128)S(1)}, u32[]{:S(2)}, u32[]{:S(2)}) collective-permute-start(f32[296,128]{1,0:T(8,128)S(1)} %get-tuple-element.39), channel_id=1, source_target_pairs={{0,12},{1,13},{2,14},{3,15},{4,0},{5,1},{6,2},{7,3},{8,4},{9,5},{1... | collective-permute-start | bytes 454664 | tf_op jit(solution)/shard_map/ppermute | solution.py:49
  87.9 7.6 %collective-permute-start.10 = (f32[296,128]{1,0:T(8,128)S(1)}, f32[296,128]{1,0:T(8,128)S(1)}, u32[]{:S(2)}, u32[]{:S(2)}) collective-permute-start(f32[296,128]{1,0:T(8,128)S(1)} %fusion.12), channel_id=1, source_target_pairs={{0,16},{1,17},{2,18},{3,19},{4,20},{5,21},{6,22},{7,23},{8,24},{9,... | collective-permute-start | bytes 454664 | tf_op jit(solution)/shard_map/ppermute | solution.py:49
  88.0 7.5 %collective-permute-start.11 = (f32[296,128]{1,0:T(8,128)S(1)}, f32[296,128]{1,0:T(8,128)S(1)}, u32[]{:S(2)}, u32[]{:S(2)}) collective-permute-start(f32[296,128]{1,0:T(8,128)S(1)} %fusion.12), channel_id=1, source_target_pairs={{0,32},{1,33},{2,34},{3,35},{4,36},{5,37},{6,38},{7,39},{8,40},{9,... | collective-permute-start | bytes 454664 | tf_op jit(solution)/shard_map/ppermute | solution.py:49
  89.7 7.4 %collective-permute-start.12 = (f32[296,128]{1,0:T(8,128)S(1)}, f32[296,128]{1,0:T(8,128)S(1)}, u32[]{:S(2)}, u32[]{:S(2)}) collective-permute-start(f32[296,128]{1,0:T(8,128)S(1)} %fusion.12), channel_id=1, source_target_pairs={{0,48},{1,49},{2,50},{3,51},{4,52},{5,53},{6,54},{7,55},{8,56},{9,... | collective-permute-start | bytes 454664 | tf_op jit(solution)/shard_map/ppermute | solution.py:49
  97.2 24.7 %copy-start.4 = (f32[4,1,384]{2,1,0:T(1,128)S(1)}, f32[4,1,384]{2,1,0:T(1,128)}, u32[]{:S(2)}) copy-start(f32[4,1,384]{2,1,0:T(1,128)} %get-tuple-element.24) | copy-start | bytes 18436
  97.2 6.1 %collective-permute-start.13 = (f32[296,128]{1,0:T(8,128)S(1)}, f32[296,128]{1,0:T(8,128)S(1)}, u32[]{:S(2)}, u32[]{:S(2)}) collective-permute-start(f32[296,128]{1,0:T(8,128)S(1)} %add_add_fusion), channel_id=1, source_target_pairs={{0,2},{1,3},{2,0},{3,1},{4,6},{5,7},{6,4},{7,5},{8,10},{9,11},{10,... | collective-permute-start | bytes 454664 | tf_op jit(solution)/shard_map/ppermute | solution.py:49
  103.3 4.7 %collective-permute-start.14 = (f32[296,128]{1,0:T(8,128)S(1)}, f32[296,128]{1,0:T(8,128)S(1)}, u32[]{:S(2)}, u32[]{:S(2)}) collective-permute-start(f32[296,128]{1,0:T(8,128)S(1)} %add.161), channel_id=1, source_target_pairs={{0,64},{1,65},{2,66},{3,67},{4,68},{5,69},{6,70},{7,71},{8,72},{9,... | collective-permute-start | bytes 454664 | tf_op jit(solution)/shard_map/ppermute | solution.py:49
  108.1 5.3 %collective-permute-start.15 = (f32[296,128]{1,0:T(8,128)S(1)}, f32[296,128]{1,0:T(8,128)S(1)}, u32[]{:S(2)}, u32[]{:S(2)}) collective-permute-start(f32[296,128]{1,0:T(8,128)S(1)} %get-tuple-element.27), channel_id=1, source_target_pairs={{0,4},{1,5},{2,6},{3,7},{4,8},{5,9},{6,10},{7,11},{8,12},{9,13},{1... | collective-permute-start | bytes 454664 | tf_op jit(solution)/shard_map/ppermute | solution.py:49
  109.0 7.0 %collective-permute-start.16 = (f32[296,128]{1,0:T(8,128)S(1)}, f32[296,128]{1,0:T(8,128)S(1)}, u32[]{:S(2)}, u32[]{:S(2)}) collective-permute-start(f32[296,128]{1,0:T(8,128)S(1)} %get-tuple-element.27), channel_id=1, source_target_pairs={{0,8},{1,9},{2,10},{3,11},{4,12},{5,13},{6,14},{7,15},{8,0},{9,1},... | collective-permute-start | bytes 454664 | tf_op jit(solution)/shard_map/ppermute | solution.py:49
  111.9 4.2 %collective-permute-start.17 = (f32[296,128]{1,0:T(8,128)S(1)}, f32[296,128]{1,0:T(8,128)S(1)}, u32[]{:S(2)}, u32[]{:S(2)}) collective-permute-start(f32[296,128]{1,0:T(8,128)S(1)} %get-tuple-element.27), channel_id=1, source_target_pairs={{0,12},{1,13},{2,14},{3,15},{4,0},{5,1},{6,2},{7,3},{8,4},{9,5},{1... | collective-permute-start | bytes 454664 | tf_op jit(solution)/shard_map/ppermute | solution.py:49
  116.1 7.5 %collective-permute-start.18 = (f32[1184,128]{1,0:T(8,128)S(1)}, f32[1184,128]{1,0:T(8,128)S(1)}, u32[]{:S(2)}, u32[]{:S(2)}) collective-permute-start(f32[1184,128]{1,0:T(8,128)S(1)} %bitcast.60), channel_id=1, source_target_pairs={{0,1},{1,0},{2,3},{3,2},{4,5},{5,4},{6,7},{7,6},{8,9},{9,8},{10,11... | collective-permute-start | bytes 1818632 | tf_op jit(solution)/shard_map/ppermute | solution.py:49

commit v4 on v3

--- a/solution.py
+++ b/solution.py
@@ -23,7 +23,8 @@
 EXT = SLOTS + 2 * DEPTH
 PAD = 8
 W = 752
-R = 2368
+G = 1152
+TAIL = 16
 BF = jnp.bfloat16
 F32 = jnp.float32
 BM = ("band", "member")
@@ -40,43 +41,100 @@
 SIZES = [2, 4, 4, 2, 2]
 
 
+def permute(value, move):
+    return lax.ppermute(value, BM, [(i, index(move(coords(i)))) for i in range(128)])
+
+
 def shift(value, dim, by):
-    pairs = []
-    for i in range(128):
-        v = coords(i)
+    def move(v):
         v[dim] = (v[dim] + by) % SIZES[dim]
-        pairs.append((i, index(v)))
-    return lax.ppermute(value, BM, pairs)
-
-
-def scatter_sum(value, dim, place):
-    n = SIZES[dim]
-    parts = value.reshape(n, value.shape[0] // n, C)
-    total = lax.dynamic_index_in_dim(parts, place, 0, keepdims=False)
-    got = [
-        shift(lax.dynamic_index_in_dim(parts, (place + d) % n, 0, keepdims=False), dim, d)
-        for d in range(1, n)
-    ]
-    for g in got:
-        total = total + g
-    return total
-
-
-def exchange_sum(value, dim):
-    got = [shift(value, dim, d) for d in range(1, SIZES[dim])]
-    for g in got:
-        value = value + g
-    return value
-
-
-def gather(value, dim, place):
-    n = SIZES[dim]
-    got = [shift(value, dim, d) for d in range(1, n)]
-    out = jnp.zeros((n,) + value.shape, value.dtype)
-    out = lax.dynamic_update_index_in_dim(out, value, place, 0)
+        return v
+
+    return permute(value, move)
+
+
+def shift_z(value, by):
+    def move(v):
+        z = (2 * v[3] + v[0] + by) % 4
+        v[3], v[0] = z // 2, z % 2
+        return v
+
+    return permute(value, move)
+
+
+def root(bound):
+    return half(jnp.sqrt(jnp.maximum(bound, 2.0**-24)) * 1.001)
+
+
+def half(value):
+    return lax.reduce_precision(value, exponent_bits=5, mantissa_bits=10)
+
+
+def encode(value, bound, loss):
+    r = root(bound)
+    q = (value * (1.0 / (r * r))).astype(jnp.float16)
+    rl = root(jnp.abs(loss))
+    share = loss * (1.0 / (rl * rl))
+    high = half(share)
+    low = (share - high) * 1024.0
+    tail = jnp.concatenate([r, rl, high, low, jnp.zeros((TAIL - 4, C), F32)], axis=0)
+    return q, tail.astype(jnp.float16)
+
+
+def decode(message):
+    q, tail = message[:-TAIL].astype(F32), message[-TAIL:].astype(F32)
+    r, rl = tail[0:1], tail[1:2]
+    scale = r * r
+    return q * scale, scale, (tail[2:3] + tail[3:4] * (1.0 / 1024.0)) * (rl * rl)
+
+
+def ordered(own, got, place):
+    out = jnp.zeros((len(got) + 1,) + own.shape, own.dtype)
+    out = lax.dynamic_update_index_in_dim(out, own, place, 0)
     for d, g in enumerate(got, 1):
-        out = lax.dynamic_update_index_in_dim(out, g, (place - d) % n, 0)
-    return out.reshape(n * value.shape[0], C)
+        out = lax.dynamic_update_index_in_dim(out, g, (place - d) % (len(got) + 1), 0)
+    return out
+
+
+def total(messages):
+    parts = [decode(messages[k]) for k in range(messages.shape[0])]
+    value, bound, loss = parts[0]
+    for v, b, l in parts[1:]:
+        value, bound, loss = value + v, bound + b, loss + l
+    return value, bound, loss
+
+
+def reduce_all(kept, sent, band, member):
+    core = member % 2
+    x, y = band % 4, band // 4 % 4
+    z = 2 * (member // 2) + band // 16
+    got = shift(sent, 4, 1)
+    value = kept[:G] + got[:G]
+    bound = kept[G : G + 1] + got[G : G + 1]
+    loss = kept[G + 1 : G + 2] + got[G + 1 : G + 2]
+
+    q, tail = encode(value, bound, loss)
+    parts = q.reshape(4, G // 4, C)
+
+    def part(k):
+        return jnp.concatenate([lax.dynamic_index_in_dim(parts, k, 0, keepdims=False), tail], axis=0)
+
+    got = [shift(part((x + d) % 4), 2, d) for d in range(1, 4)]
+    value, bound, loss = total(ordered(part(x), got, x))
+
+    message = jnp.concatenate(encode(value, bound, loss), axis=0)
+    value, bound, loss = total(ordered(message, [shift(message, 1, d) for d in range(1, 4)], y))
+
+    message = jnp.concatenate(encode(value, bound, loss), axis=0)
+    value, bound, loss = total(ordered(message, [shift_z(message, d) for d in range(1, 4)], z))
+
+    message = jnp.concatenate(encode(value, bound, loss), axis=0)
+    messages = ordered(message, [shift(message, 2, d) for d in range(1, 4)], x)
+    value = jnp.concatenate([decode(messages[k])[0] for k in range(4)], axis=0)
+    other = shift(value, 4, 1)
+    first = jnp.where(core == 0, value, other)
+    second = jnp.where(core == 0, other, value)
+    return loss[0, 0], first.reshape(3, 3, C, C), second.reshape(3, 3, C, C)
 
 
 def chip_row(half, src, r, dst, sem):
@@ -392,7 +450,7 @@
 
     lax.fori_loop(0, 2 * MEM, make_pre_cot, 0)
 
-    def weight_grad(rows, y, row0):
+    def weight_grad(rows, y, slot):
         acc_s[...] = jnp.zeros_like(acc_s)
 
         def step(m, _):
@@ -416,14 +474,21 @@
             return 0
 
         lax.fori_loop(0, MEM, step, 0)
+        biggest = jnp.zeros((C, C), F32)
         for k in range(9):
             blk = acc_s[0:C, k * C : (k + 1) * C] + acc_s[C:, 384 + k * C : 384 + (k + 1) * C]
-            grads_ref[row0 + k * C : row0 + (k + 1) * C] = jnp.transpose(blk)
-
-    weight_grad([(in3[e // 2], e % 2) for e in range(2, 8)], yb_s, 0)
-    weight_grad([(hid3[(e - 1) // 2], (e - 1) % 2) for e in range(2, 8)], ya_s, 1152)
-    total = jnp.sum(loss, axis=1, keepdims=True) * (1.0 / (ROWS_TOTAL * LON))
-    grads_ref[2304:R] = jnp.broadcast_to(total, (R - 2304, C))
+            biggest = jnp.maximum(biggest, jnp.abs(blk))
+            grads_ref[slot, k * C : (k + 1) * C] = jnp.transpose(blk)
+        return biggest
+
+    top1 = weight_grad([(in3[e // 2], e % 2) for e in range(2, 8)], yb_s, core)
+    top2 = weight_grad([(hid3[(e - 1) // 2], (e - 1) % 2) for e in range(2, 8)], ya_s, 1 - core)
+    biggest = jnp.max(jnp.max(jnp.maximum(top1, top2), axis=0, keepdims=True), axis=1, keepdims=True)
+    loss = jnp.sum(loss, axis=1, keepdims=True) * (1.0 / (ROWS_TOTAL * LON))
+    for slot in range(2):
+        grads_ref[slot, G : G + 1] = jnp.broadcast_to(biggest, (1, C))
+        grads_ref[slot, G + 1 : G + 2] = jnp.broadcast_to(loss, (1, C))
+        grads_ref[slot, G + 2 :] = jnp.zeros((6, C), F32)
 
 
 def local_step(counts, seeds, place, weights, state, target, mine, other, amp, w1, w2, wt):
@@ -433,7 +498,7 @@
     return pl.pallas_call(
         kernel,
         out_shape=(
-            jax.ShapeDtypeStruct((R, C), F32),
+            jax.ShapeDtypeStruct((2, G + 8, C), F32),
             jax.ShapeDtypeStruct((SLOTS, 1, J), F32),
         ),
         in_specs=[smem] * 4 + [hbm] * 2 + [vmem] * 6,
@@ -470,7 +535,6 @@
 def body(state, target, amp, filt1, filt2, counts, seed):
     band = lax.axis_index("band")
     member = lax.axis_index("member")
-    x = band % 4
     core = member % 2
     weights = jnp.asarray(
         np.cos(np.pi * ((np.arange(ROWS_TOTAL) + 0.5) / GRID_ROWS - 0.5)).astype(np.float32)
@@ -508,20 +572,8 @@
         counts, seeds, place, weights, state, target, mine, other, amp[None], w1, w2, wt
     )
 
-    part = scatter_sum(grads, 4, core)
-    part = scatter_sum(part, 2, x)
-    part = exchange_sum(part, 1)
-    part = exchange_sum(part, 3)
-    part = exchange_sum(part, 0)
-    part = gather(part, 2, x)
-    full = gather(part, 4, core)
-
-    return (
-        cells[:, 0, LEFT : LEFT + OWN],
-        full[2304, 0],
-        full[:1152].reshape(3, 3, C, C),
-        full[1152:2304].reshape(3, 3, C, C),
-    )
+    mean_loss, grad_one, grad_two = reduce_all(grads[0], grads[1], band, member)
+    return cells[:, 0, LEFT : LEFT + OWN], mean_loss, grad_one, grad_two
 
 
 def solution(mesh):

time: 125 us -> 118 us (0.944)
  waiting for transfers between devices: 41.5 us -> 28.8 us
  other arithmetic: 4.64 us -> 8.16 us
  starting transfers between devices: 33.8 us -> 35.2 us
    ppermute x16 -> x17, waiting for transfers between devices: 29 us -> 16.3 us  [permute(): lax.ppermute(value, BM, [(i, index(move(coords(i)))) for i in range(128)])]
    slice x3 -> x1, local copies, waits for them, and re-layouts: 1.67 us -> 0.07 us  [body(): return (cells[:, 0, LEFT:LEFT + OWN], mean_loss, grad_one, grad_two)]
    convert_element_type x0 -> x7, other arithmetic: none -> 1.43 us  [the longest x4 1.41 us: encode(): q = (value * (1.0 / (r * r))).astype(jnp.float16)]
    ppermute x16 -> x17, starting transfers between devices: 26.6 us -> 28 us  [permute(): lax.ppermute(value, BM, [(i, index(move(coords(i)))) for i in range(128)])]
    concatenate x0 -> x7, local copies, waits for them, and re-layouts: none -> 1.31 us  [the longest x4 0.75 us: part(): jnp.concatenate([lax.dynamic_index_in_dim(parts, k, 0, keepdims=False), t...]
  transfers between devices with their start and end apart: 19 -> 20, of which waited for: 13 -> 14; matrix products, arithmetic and copies ran while one was open for 4% -> 5% of each run, Pallas kernels for 3% -> 3%
where the time goes in v4:
time: 118 us
  Pallas kernels  38.3 us (32%)
  starting transfers between devices  35.2 us (30%)
  waiting for transfers between devices  28.8 us (24%)
  other arithmetic  8.16 us (7%)
  local copies, waits for them, and re-layouts  5.73 us (5%)
  between operations  1.99 us (2%)
    pallas_call x1, Pallas kernels, local_step(): pl.pallas_call(kernel, out_shape=(jax.ShapeDtypeStruct((2, G + 8, C), F32...  34.8 us
    ppermute x17, starting transfers between devices, permute(): lax.ppermute(value, BM, [(i, index(move(coords(i)))) for i in range(128)])  28 us
    ppermute x17, waiting for transfers between devices, permute(): lax.ppermute(value, BM, [(i, index(move(coords(i)))) for i in range(128)])  16.3 us
    ppermute x3, waiting for transfers between devices, send(): return lax.ppermute(value, BM, pairs)  12.5 us
    ppermute x3, starting transfers between devices, send(): return lax.ppermute(value, BM, pairs)  7.17 us
    pallas_call x1, Pallas kernels, edges(): pl.pallas_call(edge_kernel, out_shape=(rows(4), rows(2), rows(1), jax.Sha...  3.45 us
  transfers between devices with their start and end apart: 20, of which 14 were waited for; matrix products, arithmetic and copies ran while one was open for 5% of the time, Pallas kernels for 3%

profile of v4, /device:TPU:1, one launch (start us, length us, event | category | flops | bytes accessed | tf_op | source)
XLA Modules:
  0.0 118.1 jit_solution(15655876825672971021)
XLA Ops:
  1.3 1.5 %collective-permute-start = (s32[4]{0:T(128)S(1)}, s32[4]{0:T(128)S(1)}, u32[]{:S(2)}, u32[]{:S(2)}) collective-permute-start(s32[4]{0:T(128)S(1)} %compare_select_fusion), channel_id=1, source_target_pairs={{0,1},{1,0},{2,3},{3,2},{4,5},{5,4},{6,7},{7,6},{8,9},{9,8},{10,11... | collective-permute-start | bytes 56 | tf_op jit(solution)/shard_map/ppermute | solution.py:45
  3.4 3.5 %edge_rows.1 = (bf16[4,752,128]{2,1,0:T(8,128)(2,1)}, bf16[2,752,128]{2,1,0:T(8,128)(2,1)}, bf16[1,752,128]{2,1,0:T(8,128)(2,1)}, f32[8,128]{1,0:T(8,128)}) custom-call(s32[32]{0:T(128)} %counts_ref.3, s32[2]{0:T(128)} %pad_add_fusion.place_ref, bf16[4,1440,128]{2,1,0:T(8,128)(2,1)} %state_ref.3, bf16[4,1440,128]{2,1,0:T(8,128)(2,1)} %target_ref.3), custom_call_target="tpu_custom_call" | custom-call | tf_op jit(solution)/shard_map/edge_rows/pallas_call | solution.py:226
  6.9 6.5 %collective-permute-start.2 = (bf16[4,752,128]{2,1,0:T(8,128)(2,1)}, bf16[4,752,128]{2,1,0:T(8,128)(2,1)S(1)}, u32[]{:S(2)}, u32[]{:S(2)}) collective-permute-start(bf16[4,752,128]{2,1,0:T(8,128)(2,1)} %get-tuple-element.20), channel_id=1, source_target_pairs={{0,4},{1,125},{2,6},{3,127},{4,8},{5,1},{6,10},{7,3},{8,12},{9,5},... | collective-permute-start | bytes 2310152 | tf_op jit(solution)/shard_map/ppermute | solution.py:549
  13.3 3.3 %collective-permute-start.1 = (s32[4]{0:T(128)S(1)}, s32[4]{0:T(128)S(1)}, u32[]{:S(2)}, u32[]{:S(2)}) collective-permute-start(s32[4]{0:T(128)S(1)} %fusion.108), channel_id=1, source_target_pairs={{0,2},{1,3},{2,0},{3,1},{4,6},{5,7},{6,4},{7,5},{8,10},{9,11},{10,... | collective-permute-start | bytes 56 | tf_op jit(solution)/shard_map/ppermute | solution.py:45
  16.7 1.3 %collective-permute-done.1 = s32[4]{0:T(128)S(1)} collective-permute-done((s32[4]{0:T(128)S(1)}, s32[4]{0:T(128)S(1)}, u32[]{:S(2)}, u32[]{:S(2)}) %collective-permute-start.1) | collective-permute-done | bytes 48 | tf_op jit(solution)/shard_map/ppermute | solution.py:45
  19.4 0.8 compare_bitcast_fusion.3
  20.2 11.2 %collective-permute-done.4 = bf16[1,752,128]{2,1,0:T(8,128)(2,1)S(1)} collective-permute-done((bf16[1,752,128]{2,1,0:T(8,128)(2,1)}, bf16[1,752,128]{2,1,0:T(8,128)(2,1)S(1)}, u32[]{:S(2)}, u32[]{:S(2)}) %collective-permute-start.4) | collective-permute-done | bytes 192544 | tf_op jit(solution)/shard_map/ppermute | solution.py:549
  31.4 1.3 %collective-permute-done.2 = bf16[4,752,128]{2,1,0:T(8,128)(2,1)S(1)} collective-permute-done((bf16[4,752,128]{2,1,0:T(8,128)(2,1)}, bf16[4,752,128]{2,1,0:T(8,128)(2,1)S(1)}, u32[]{:S(2)}, u32[]{:S(2)}) %collective-permute-start.2) | collective-permute-done | bytes 770080 | tf_op jit(solution)/shard_map/ppermute | solution.py:549
  32.9 0.8 constant_dynamic-slice_fusion
  33.7 2.8 %collective-permute-start.5 = (bf16[4,384,128]{2,1,0:T(8,128)(2,1)S(1)}, bf16[4,384,128]{2,1,0:T(8,128)(2,1)S(1)}, u32[]{:S(2)}, u32[]{:S(2)}) collective-permute-start(bf16[4,384,128]{2,1,0:T(8,128)(2,1)S(1)} %get-tuple-element.52), channel_id=1, source_target_pairs={{0,1},{1,0},{2,3},{3,2},{4,5},{5,4},{6,7},{7,6},{8,9},{9,8},{10,11... | collective-permute-start | bytes 1179656 | tf_op jit(solution)/shard_map/ppermute | solution.py:45
  36.5 0.9 fusion.8.wt_ref
  37.5 1.3 %fusion.6 = (bf16[1536,256]{1,0:T(8,128)(2,1)}, bf16[1536,256]{1,0:T(8,128)(2,1)}) fusion(bf16[1152,128]{1,0:T(8,128)(2,1)S(1)} %bitcast.249, bf16[1152,128]{1,0:T(8,128)(2,1)S(1)} %bitcast.244), kind=kLoop, calls=%fused_computation.8 | loop fusion | flops 5505024 | bytes 2162688 | tf_op jit(solution)/shard_map/concatenate | solution.py:530
  39.5 34.8 %ensemble_step.1 = (f32[2,1160,128]{2,1,0:T(8,128)}, f32[4,1,384]{2,1,0:T(1,128)}) custom-call(s32[32]{0:T(128)} %counts_ref.3, s32[4]{0:T(128)} %add.301.seeds_ref, s32[2]{0:T(128)} %pad_add_fusion.place_ref, f32[96]{0:T(128)} %constant.203.clone.weight_ref, bf16[4,1440,128]{2,1,0:T(8,128)(2,1)} %state_ref.3, bf16[4,1440,128]{2,1,0:T(8,128)(2,1)} %target_ref.3, ...), custom_call_target="tpu_custom_call" | custom-call | tf_op jit(solution)/shard_map/ensemble_step/pallas_call | solution.py:498
  74.4 1.1 slice_bitcast_fusion
  75.9 1.7 %collective-permute-done.6 = f32[1160,128]{1,0:T(8,128)S(1)} collective-permute-done((f32[1160,128]{1,0:T(8,128)S(1)}, f32[1160,128]{1,0:T(8,128)S(1)}, u32[]{:S(2)}, u32[]{:S(2)}) %collective-permute-start.6) | collective-permute-done | bytes 593952 | tf_op jit(solution)/shard_map/ppermute | solution.py:45
  78.4 1.2 %fusion.10 = f16[1152,128]{1,0:T(8,128)(2,1)S(1)} fusion(f32[1160,128]{1,0:T(8,128)S(1)} %collective-permute-done.6, f32[2,1160,128]{2,1,0:T(8,128)} %get-tuple-element.25, f32[128]{0:T(128)S(1)} %divide_bitcast_fusion.3), kind=kLoop, calls=%fused_computation.15 | loop fusion | flops 442368 | bytes 1475072 | tf_op jit(solution)/shard_map/convert_element_type | solution.py:75
  81.3 2.0 %collective-permute-start.9 = (f16[304,128]{1,0:T(8,128)(2,1)S(1)}, f16[304,128]{1,0:T(8,128)(2,1)S(1)}, u32[]{:S(2)}, u32[]{:S(2)}) collective-permute-start(f16[304,128]{1,0:T(8,128)(2,1)S(1)} %concatenate.58), channel_id=1, source_target_pairs={{0,12},{1,13},{2,14},{3,15},{4,0},{5,1},{6,2},{7,3},{8,4},{9,5},{1... | collective-permute-start | bytes 233480 | tf_op jit(solution)/shard_map/ppermute | solution.py:45
  83.4 3.4 %collective-permute-done.7 = f16[304,128]{1,0:T(8,128)(2,1)S(1)} collective-permute-done((f16[304,128]{1,0:T(8,128)(2,1)S(1)}, f16[304,128]{1,0:T(8,128)(2,1)S(1)}, u32[]{:S(2)}, u32[]{:S(2)}) %collective-permute-start.7) | collective-permute-done | bytes 77856 | tf_op jit(solution)/shard_map/ppermute | solution.py:45
  87.9 1.6 %collective-permute-start.11 = (f16[304,128]{1,0:T(8,128)(2,1)S(1)}, f16[304,128]{1,0:T(8,128)(2,1)S(1)}, u32[]{:S(2)}, u32[]{:S(2)}) collective-permute-start(f16[304,128]{1,0:T(8,128)(2,1)S(1)} %concatenate.59), channel_id=1, source_target_pairs={{0,32},{1,33},{2,34},{3,35},{4,36},{5,37},{6,38},{7,39},{8,40},{9,... | collective-permute-start | bytes 233480 | tf_op jit(solution)/shard_map/ppermute | solution.py:45
  89.5 1.1 collective-permute-start.12
  90.6 2.5 %collective-permute-done.10 = f16[304,128]{1,0:T(8,128)(2,1)S(1)} collective-permute-done((f16[304,128]{1,0:T(8,128)(2,1)S(1)}, f16[304,128]{1,0:T(8,128)(2,1)S(1)}, u32[]{:S(2)}, u32[]{:S(2)}) %collective-permute-start.10) | collective-permute-done | bytes 77856 | tf_op jit(solution)/shard_map/ppermute | solution.py:45
  93.2 0.8 collective-permute-done.12
  94.5 1.0 collective-permute-start.13
  95.5 3.1 %collective-permute-start.14 = (f16[304,128]{1,0:T(8,128)(2,1)S(1)}, f16[304,128]{1,0:T(8,128)(2,1)S(1)}, u32[]{:S(2)}, u32[]{:S(2)}) collective-permute-start(f16[304,128]{1,0:T(8,128)(2,1)S(1)} %concatenate.60), channel_id=1, source_target_pairs={{0,2},{1,3},{2,0},{3,1},{4,6},{5,7},{6,4},{7,5},{8,10},{9,11},{10,... | collective-permute-start | bytes 233480 | tf_op jit(solution)/shard_map/ppermute | solution.py:45
  98.6 1.2 %collective-permute-start.15 = (f16[304,128]{1,0:T(8,128)(2,1)S(1)}, f16[304,128]{1,0:T(8,128)(2,1)S(1)}, u32[]{:S(2)}, u32[]{:S(2)}) collective-permute-start(f16[304,128]{1,0:T(8,128)(2,1)S(1)} %concatenate.60), channel_id=1, source_target_pairs={{0,66},{1,67},{2,64},{3,65},{4,70},{5,71},{6,68},{7,69},{8,74},{9,... | collective-permute-start | bytes 233480 | tf_op jit(solution)/shard_map/ppermute | solution.py:45
  99.9 1.3 %collective-permute-done.14 = f16[304,128]{1,0:T(8,128)(2,1)S(1)} collective-permute-done((f16[304,128]{1,0:T(8,128)(2,1)S(1)}, f16[304,128]{1,0:T(8,128)(2,1)S(1)}, u32[]{:S(2)}, u32[]{:S(2)}) %collective-permute-start.14) | collective-permute-done | bytes 77856 | tf_op jit(solution)/shard_map/ppermute | solution.py:45
  101.2 0.9 collective-permute-done.15
  102.7 4.7 %collective-permute-start.17 = (f16[304,128]{1,0:T(8,128)(2,1)S(1)}, f16[304,128]{1,0:T(8,128)(2,1)S(1)}, u32[]{:S(2)}, u32[]{:S(2)}) collective-permute-start(f16[304,128]{1,0:T(8,128)(2,1)S(1)} %concatenate.61), channel_id=1, source_target_pairs={{0,8},{1,9},{2,10},{3,11},{4,12},{5,13},{6,14},{7,15},{8,0},{9,1},... | collective-permute-start | bytes 233480 | tf_op jit(solution)/shard_map/ppermute | solution.py:45
  108.0 2.0 %collective-permute-done.17 = f16[304,128]{1,0:T(8,128)(2,1)S(1)} collective-permute-done((f16[304,128]{1,0:T(8,128)(2,1)S(1)}, f16[304,128]{1,0:T(8,128)(2,1)S(1)}, u32[]{:S(2)}, u32[]{:S(2)}) %collective-permute-start.17) | collective-permute-done | bytes 77856 | tf_op jit(solution)/shard_map/ppermute | solution.py:45
  110.7 4.6 %collective-permute-start.19 = (f32[1152,128]{1,0:T(8,128)S(1)}, f32[1152,128]{1,0:T(8,128)S(1)}, u32[]{:S(2)}, u32[]{:S(2)}) collective-permute-start(f32[1152,128]{1,0:T(8,128)S(1)} %pad_maximum_fusion.1), channel_id=1, source_target_pairs={{0,1},{1,0},{2,3},{3,2},{4,5},{5,4},{6,7},{7,6},{8,9},{9,8},{10,11... | collective-permute-start | bytes 1769480 | tf_op jit(solution)/shard_map/ppermute | solution.py:45
  116.1 0.9 collective-permute-done.19
  117.0 1.1 broadcast_select_fusion
  (93 shorter events, 10.0 us)
Async XLA Ops:
  1.3 5.5 %collective-permute-start = (s32[4]{0:T(128)S(1)}, s32[4]{0:T(128)S(1)}, u32[]{:S(2)}, u32[]{:S(2)}) collective-permute-start(s32[4]{0:T(128)S(1)} %compare_select_fusion), channel_id=1, source_target_pairs={{0,1},{1,0},{2,3},{3,2},{4,5},{5,4},{6,7},{7,6},{8,9},{9,8},{10,11... | collective-permute-start | bytes 56 | tf_op jit(solution)/shard_map/ppermute | solution.py:45
  3.4 15.1 %copy-start = (bf16[3,3,128,128]{3,2,1,0:T(8,128)(2,1)S(1)}, bf16[3,3,128,128]{3,2,1,0:T(8,128)(2,1)}, u32[]{:S(2)}) copy-start(bf16[3,3,128,128]{3,2,1,0:T(8,128)(2,1)} %param.12) | copy-start | bytes 884740
  6.9 25.9 %collective-permute-start.2 = (bf16[4,752,128]{2,1,0:T(8,128)(2,1)}, bf16[4,752,128]{2,1,0:T(8,128)(2,1)S(1)}, u32[]{:S(2)}, u32[]{:S(2)}) collective-permute-start(bf16[4,752,128]{2,1,0:T(8,128)(2,1)} %get-tuple-element.20), channel_id=1, source_target_pairs={{0,4},{1,125},{2,6},{3,127},{4,8},{5,1},{6,10},{7,3},{8,12},{9,5},... | collective-permute-start | bytes 2310152 | tf_op jit(solution)/shard_map/ppermute | solution.py:549
  13.3 4.6 %collective-permute-start.1 = (s32[4]{0:T(128)S(1)}, s32[4]{0:T(128)S(1)}, u32[]{:S(2)}, u32[]{:S(2)}) collective-permute-start(s32[4]{0:T(128)S(1)} %fusion.108), channel_id=1, source_target_pairs={{0,2},{1,3},{2,0},{3,1},{4,6},{5,7},{6,4},{7,5},{8,10},{9,11},{10,... | collective-permute-start | bytes 56 | tf_op jit(solution)/shard_map/ppermute | solution.py:45
  18.4 13.0 %collective-permute-start.3 = (bf16[2,752,128]{2,1,0:T(8,128)(2,1)}, bf16[2,752,128]{2,1,0:T(8,128)(2,1)S(1)}, u32[]{:S(2)}, u32[]{:S(2)}) collective-permute-start(bf16[2,752,128]{2,1,0:T(8,128)(2,1)} %get-tuple-element.22), channel_id=1, source_target_pairs={{0,8},{1,121},{2,10},{3,123},{4,12},{5,125},{6,14},{7,127},{8,16},... | collective-permute-start | bytes 1155080 | tf_op jit(solution)/shard_map/ppermute | solution.py:549
  18.7 12.8 %collective-permute-start.4 = (bf16[1,752,128]{2,1,0:T(8,128)(2,1)}, bf16[1,752,128]{2,1,0:T(8,128)(2,1)S(1)}, u32[]{:S(2)}, u32[]{:S(2)}) collective-permute-start(bf16[1,752,128]{2,1,0:T(8,128)(2,1)} %get-tuple-element.23), channel_id=1, source_target_pairs={{0,12},{1,117},{2,14},{3,119},{4,16},{5,121},{6,18},{7,123},{8,20}... | collective-permute-start | bytes 577544 | tf_op jit(solution)/shard_map/ppermute | solution.py:549
  32.9 4.6 %copy-start.2 = (bf16[3,3,128,128]{3,2,1,0:T(8,128)(2,1)S(1)}, bf16[3,3,128,128]{3,2,1,0:T(8,128)(2,1)}, u32[]{:S(2)}) copy-start(bf16[3,3,128,128]{3,2,1,0:T(8,128)(2,1)} %param.11) | copy-start | bytes 884740
  33.7 5.0 %collective-permute-start.5 = (bf16[4,384,128]{2,1,0:T(8,128)(2,1)S(1)}, bf16[4,384,128]{2,1,0:T(8,128)(2,1)S(1)}, u32[]{:S(2)}, u32[]{:S(2)}) collective-permute-start(bf16[4,384,128]{2,1,0:T(8,128)(2,1)S(1)} %get-tuple-element.52), channel_id=1, source_target_pairs={{0,1},{1,0},{2,3},{3,2},{4,5},{5,4},{6,7},{7,6},{8,9},{9,8},{10,11... | collective-permute-start | bytes 1179656 | tf_op jit(solution)/shard_map/ppermute | solution.py:45
  38.8 0.7 copy-start.1
  75.5 2.1 %collective-permute-start.6 = (f32[1160,128]{1,0:T(8,128)S(1)}, f32[1160,128]{1,0:T(8,128)S(1)}, u32[]{:S(2)}, u32[]{:S(2)}) collective-permute-start(f32[1160,128]{1,0:T(8,128)S(1)} %slice_bitcast_fusion), channel_id=1, source_target_pairs={{0,1},{1,0},{2,3},{3,2},{4,5},{5,4},{6,7},{7,6},{8,9},{9,8},{10,11... | collective-permute-start | bytes 1781768 | tf_op jit(solution)/shard_map/ppermute | solution.py:45
  80.1 6.7 %collective-permute-start.7 = (f16[304,128]{1,0:T(8,128)(2,1)S(1)}, f16[304,128]{1,0:T(8,128)(2,1)S(1)}, u32[]{:S(2)}, u32[]{:S(2)}) collective-permute-start(f16[304,128]{1,0:T(8,128)(2,1)S(1)} %concatenate.56), channel_id=1, source_target_pairs={{0,4},{1,5},{2,6},{3,7},{4,8},{5,9},{6,10},{7,11},{8,12},{9,13},{1... | collective-permute-start | bytes 233480 | tf_op jit(solution)/shard_map/ppermute | solution.py:45
  80.3 6.5 %collective-permute-start.8 = (f16[304,128]{1,0:T(8,128)(2,1)S(1)}, f16[304,128]{1,0:T(8,128)(2,1)S(1)}, u32[]{:S(2)}, u32[]{:S(2)}) collective-permute-start(f16[304,128]{1,0:T(8,128)(2,1)S(1)} %concatenate.57), channel_id=1, source_target_pairs={{0,8},{1,9},{2,10},{3,11},{4,12},{5,13},{6,14},{7,15},{8,0},{9,1},... | collective-permute-start | bytes 233480 | tf_op jit(solution)/shard_map/ppermute | solution.py:45
  81.3 6.0 %collective-permute-start.9 = (f16[304,128]{1,0:T(8,128)(2,1)S(1)}, f16[304,128]{1,0:T(8,128)(2,1)S(1)}, u32[]{:S(2)}, u32[]{:S(2)}) collective-permute-start(f16[304,128]{1,0:T(8,128)(2,1)S(1)} %concatenate.58), channel_id=1, source_target_pairs={{0,12},{1,13},{2,14},{3,15},{4,0},{5,1},{6,2},{7,3},{8,4},{9,5},{1... | collective-permute-start | bytes 233480 | tf_op jit(solution)/shard_map/ppermute | solution.py:45
  87.8 5.4 %collective-permute-start.10 = (f16[304,128]{1,0:T(8,128)(2,1)S(1)}, f16[304,128]{1,0:T(8,128)(2,1)S(1)}, u32[]{:S(2)}, u32[]{:S(2)}) collective-permute-start(f16[304,128]{1,0:T(8,128)(2,1)S(1)} %concatenate.59), channel_id=1, source_target_pairs={{0,16},{1,17},{2,18},{3,19},{4,20},{5,21},{6,22},{7,23},{8,24},{9,... | collective-permute-start | bytes 233480 | tf_op jit(solution)/shard_map/ppermute | solution.py:45
  87.9 5.3 %collective-permute-start.11 = (f16[304,128]{1,0:T(8,128)(2,1)S(1)}, f16[304,128]{1,0:T(8,128)(2,1)S(1)}, u32[]{:S(2)}, u32[]{:S(2)}) collective-permute-start(f16[304,128]{1,0:T(8,128)(2,1)S(1)} %concatenate.59), channel_id=1, source_target_pairs={{0,32},{1,33},{2,34},{3,35},{4,36},{5,37},{6,38},{7,39},{8,40},{9,... | collective-permute-start | bytes 233480 | tf_op jit(solution)/shard_map/ppermute | solution.py:45
  89.5 4.6 %collective-permute-start.12 = (f16[304,128]{1,0:T(8,128)(2,1)S(1)}, f16[304,128]{1,0:T(8,128)(2,1)S(1)}, u32[]{:S(2)}, u32[]{:S(2)}) collective-permute-start(f16[304,128]{1,0:T(8,128)(2,1)S(1)} %concatenate.59), channel_id=1, source_target_pairs={{0,48},{1,49},{2,50},{3,51},{4,52},{5,53},{6,54},{7,55},{8,56},{9,... | collective-permute-start | bytes 233480 | tf_op jit(solution)/shard_map/ppermute | solution.py:45
  94.5 5.4 %collective-permute-start.13 = (f16[304,128]{1,0:T(8,128)(2,1)S(1)}, f16[304,128]{1,0:T(8,128)(2,1)S(1)}, u32[]{:S(2)}, u32[]{:S(2)}) collective-permute-start(f16[304,128]{1,0:T(8,128)(2,1)S(1)} %concatenate.60), channel_id=1, source_target_pairs={{0,64},{1,65},{2,66},{3,67},{4,68},{5,69},{6,70},{7,71},{8,72},{9,... | collective-permute-start | bytes 233480 | tf_op jit(solution)/shard_map/ppermute | solution.py:45
  95.5 5.7 %collective-permute-start.14 = (f16[304,128]{1,0:T(8,128)(2,1)S(1)}, f16[304,128]{1,0:T(8,128)(2,1)S(1)}, u32[]{:S(2)}, u32[]{:S(2)}) collective-permute-start(f16[304,128]{1,0:T(8,128)(2,1)S(1)} %concatenate.60), channel_id=1, source_target_pairs={{0,2},{1,3},{2,0},{3,1},{4,6},{5,7},{6,4},{7,5},{8,10},{9,11},{10,... | collective-permute-start | bytes 233480 | tf_op jit(solution)/shard_map/ppermute | solution.py:45
  98.6 3.5 %collective-permute-start.15 = (f16[304,128]{1,0:T(8,128)(2,1)S(1)}, f16[304,128]{1,0:T(8,128)(2,1)S(1)}, u32[]{:S(2)}, u32[]{:S(2)}) collective-permute-start(f16[304,128]{1,0:T(8,128)(2,1)S(1)} %concatenate.60), channel_id=1, source_target_pairs={{0,66},{1,67},{2,64},{3,65},{4,70},{5,71},{6,68},{7,69},{8,74},{9,... | collective-permute-start | bytes 233480 | tf_op jit(solution)/shard_map/ppermute | solution.py:45
  102.2 8.5 %copy-start.4 = (f32[1,128]{1,0:T(1,128)}, f32[1,128]{1,0:T(1,128)S(1)}, u32[]{:S(2)}) copy-start(f32[1,128]{1,0:T(1,128)S(1)} %get-tuple-element.28) | copy-start | bytes 1540
  102.6 12.8 %copy-start.3 = (f32[4,1,384]{2,1,0:T(1,128)S(1)}, f32[4,1,384]{2,1,0:T(1,128)}, u32[]{:S(2)}) copy-start(f32[4,1,384]{2,1,0:T(1,128)} %get-tuple-element.24) | copy-start | bytes 18436
  102.6 5.3 %collective-permute-start.16 = (f16[304,128]{1,0:T(8,128)(2,1)S(1)}, f16[304,128]{1,0:T(8,128)(2,1)S(1)}, u32[]{:S(2)}, u32[]{:S(2)}) collective-permute-start(f16[304,128]{1,0:T(8,128)(2,1)S(1)} %concatenate.61), channel_id=1, source_target_pairs={{0,4},{1,5},{2,6},{3,7},{4,8},{5,9},{6,10},{7,11},{8,12},{9,13},{1... | collective-permute-start | bytes 233480 | tf_op jit(solution)/shard_map/ppermute | solution.py:45
  102.7 7.3 %collective-permute-start.17 = (f16[304,128]{1,0:T(8,128)(2,1)S(1)}, f16[304,128]{1,0:T(8,128)(2,1)S(1)}, u32[]{:S(2)}, u32[]{:S(2)}) collective-permute-start(f16[304,128]{1,0:T(8,128)(2,1)S(1)} %concatenate.61), channel_id=1, source_target_pairs={{0,8},{1,9},{2,10},{3,11},{4,12},{5,13},{6,14},{7,15},{8,0},{9,1},... | collective-permute-start | bytes 233480 | tf_op jit(solution)/shard_map/ppermute | solution.py:45
  107.3 3.2 %collective-permute-start.18 = (f16[304,128]{1,0:T(8,128)(2,1)S(1)}, f16[304,128]{1,0:T(8,128)(2,1)S(1)}, u32[]{:S(2)}, u32[]{:S(2)}) collective-permute-start(f16[304,128]{1,0:T(8,128)(2,1)S(1)} %concatenate.61), channel_id=1, source_target_pairs={{0,12},{1,13},{2,14},{3,15},{4,0},{5,1},{6,2},{7,3},{8,4},{9,5},{1... | collective-permute-start | bytes 233480 | tf_op jit(solution)/shard_map/ppermute | solution.py:45
  110.7 6.3 %collective-permute-start.19 = (f32[1152,128]{1,0:T(8,128)S(1)}, f32[1152,128]{1,0:T(8,128)S(1)}, u32[]{:S(2)}, u32[]{:S(2)}) collective-permute-start(f32[1152,128]{1,0:T(8,128)S(1)} %pad_maximum_fusion.1), channel_id=1, source_target_pairs={{0,1},{1,0},{2,3},{3,2},{4,5},{5,4},{6,7},{7,6},{8,9},{9,8},{10,11... | collective-permute-start | bytes 1769480 | tf_op jit(solution)/shard_map/ppermute | solution.py:45

commit v5 on v4

--- a/solution.py
+++ b/solution.py
@@ -239,7 +239,7 @@
     amp_ref, w1_ref, w2_ref, wt_ref,
     grads_ref, cells_ref,
     state_s, tgt_s, hash_s, bufs, cbuf_s, crps_s,
-    in3, hid3, cot3_s, pre_s, fc_s, ya_s, yb_s, acc_s, sem,
+    in3, hid3, cot3_s, pre_s, fc_s, ya_s, yb_s, acc_s, acc2_s, sem,
 ):
     band = place_ref[0]
     quarter = place_ref[1]
@@ -314,7 +314,7 @@
     amp_base = amp * (0.5 / 32768.0 - 1.0)
 
     def make_inputs(m, k):
-        seed = seeds_ref[jnp.minimum(m, MEM - 1)] * 1103515245
+        seed = seeds_ref[m] * 1103515245
         for j in range(2):
             e = 2 * k + j
             live = jnp.where(outside(e), 0.0, 1.0)
@@ -369,73 +369,85 @@
 
     step = 32
 
-    def make_crps(r, loss):
-        e = r + 2
-        g = jnp.clip(offset - DEPTH + e, 0, ROWS_TOTAL - 1)
-        weight = jnp.where(outside(e), 0.0, weight_ref[g])
-        mine = ((r >= 1) & (r < 1 + n)).astype(F32)
-        scale = weight * (factor * pair_scale)
-        slot = jnp.clip(r - 1, 0, SLOTS - 1)
-
-        def chunk(k, _):
+    def crps_chunk(r, k, scale):
+        at = pl.ds(k * step, step)
+        if not isinstance(k, int):
             at = pl.ds(pl.multiple_of(k * step, step), step)
-            t = tgt_s[r, at].astype(F32)
-            f = [fc_s[m, r, at].astype(F32) for m in range(MEM)]
-            skill = None
-            spread = None
-            slopes = []
-            for m in range(MEM):
-                d = f[m] - t
+        t = tgt_s[r, at].astype(F32)
+        f = [fc_s[m, r, at].astype(F32) for m in range(MEM)]
+        skill = None
+        spread = None
+        slopes = []
+        for m in range(MEM):
+            d = f[m] - t
+            q = d * d + SMOOTH
+            inv = lax.rsqrt(q)
+            skill = q * inv if skill is None else skill + q * inv
+            slopes.append(d * inv * (MEM - 1.0))
+        for a in range(MEM):
+            for b in range(a + 1, MEM):
+                d = f[a] - f[b]
                 q = d * d + SMOOTH
                 inv = lax.rsqrt(q)
-                skill = q * inv if skill is None else skill + q * inv
-                slopes.append(d * inv * (MEM - 1.0))
-            for a in range(MEM):
-                for b in range(a + 1, MEM):
-                    d = f[a] - f[b]
-                    q = d * d + SMOOTH
-                    inv = lax.rsqrt(q)
-                    spread = q * inv if spread is None else spread + q * inv
-                    tilt = d * inv
-                    slopes[a] = slopes[a] - tilt
-                    slopes[b] = slopes[b] + tilt
-            crps_s[at] = (skill * (MEM - 1.0) - spread) * pair_scale
-            for m in range(MEM):
-                cbuf_s[m, pl.ds(pl.multiple_of(PAD + k * step, 8), step)] = slopes[m] * scale
-            return 0
-
-        lax.fori_loop(0, J // step, chunk, 0)
+                spread = q * inv if spread is None else spread + q * inv
+                tilt = d * inv
+                slopes[a] = slopes[a] - tilt
+                slopes[b] = slopes[b] + tilt
+        crps_s[at] = (skill * (MEM - 1.0) - spread) * pair_scale
         for m in range(MEM):
-            mid = cbuf_s[m, PAD : PAD + J]
-            cot3_s[m, r, :, C : 2 * C] = mid.astype(BF)
+            start_at = PAD + k * step
+            if not isinstance(k, int):
+                start_at = pl.multiple_of(start_at, 8)
+            cbuf_s[m, pl.ds(start_at, step)] = slopes[m] * scale
+
+    def crps_weight(r):
+        g = jnp.clip(offset - DEPTH + 2 + r, 0, ROWS_TOTAL - 1)
+        return jnp.where(outside(r + 2), 0.0, weight_ref[g])
+
+    def spread_out(r):
+        for m in range(MEM):
+            cot3_s[m, r, :, C : 2 * C] = cbuf_s[m, PAD : PAD + J].astype(BF)
             cot3_s[m, r, :, 0:C] = cbuf_s[m, PAD - 1 : PAD - 1 + J].astype(BF)
             cot3_s[m, r, :, 2 * C :] = cbuf_s[m, PAD + 1 : PAD + 1 + J].astype(BF)
 
-        @pl.when((r >= 1) & (r < 1 + SLOTS))
-        def _():
-            for m in range(MEM):
-                ya_s[m, slot] = cot3_s[m, r, :, C : 2 * C]
-                trim(ya_s, m, slot)
-            @pl.when(r > n)
-            def _():
-                ya_s[:, slot] = jnp.zeros((MEM, J, C), BF)
-
-            cells_ref[slot] = jnp.sum(jnp.transpose(crps_s[...]), axis=0, keepdims=True) * (
-                weight * mine * (1.0 / C)
-            )
-
-        return loss
+    def keep_own(r, weight):
+        for m in range(MEM):
+            ya_s[m, r - 1] = jnp.where(r > n, 0.0, cbuf_s[m, PAD : PAD + J]).astype(BF)
+            trim(ya_s, m, r - 1)
+        mine = jnp.where(r > n, 0.0, weight * (1.0 / C))
+        cells_ref[r - 1] = jnp.sum(jnp.transpose(crps_s[...]), axis=0, keepdims=True) * mine
+
+    def crps_row(r):
+        weight = crps_weight(r)
+        for k in range(J // step):
+            crps_chunk(r, k, weight * (factor * pair_scale))
+        spread_out(r)
+        if 1 <= r <= SLOTS:
+            keep_own(r, weight)
 
     for m in range(MEM):
         cbuf_s[m, 0:PAD] = jnp.zeros((PAD, C), F32)
         cbuf_s[m, PAD + J :] = jnp.zeros((PAD, C), F32)
-    lax.fori_loop(0, SLOTS + 2, make_crps, 0)
-    loss = cells_ref[0] + cells_ref[1] + cells_ref[2] + cells_ref[3]
-    lane = lax.broadcasted_iota(jnp.int32, (1, J), 1)
-    loss = jnp.where((lane >= LEFT) & (lane < LEFT + OWN), loss, 0.0)
-
-    def make_pre_cot(i, _):
-        p, m = i // MEM, i % MEM
+
+    def crps_looped(r, _):
+        weight = crps_weight(r)
+
+        def chunk(k, _):
+            crps_chunk(r, k, weight * (factor * pair_scale))
+            return 0
+
+        lax.fori_loop(0, J // step, chunk, 0)
+        spread_out(r)
+
+        @pl.when(r >= 1)
+        def _():
+            keep_own(r, weight)
+
+        return 0
+
+    lax.fori_loop(0, 3, crps_looped, 0)
+
+    def make_pre_cot(m, p):
         lhs = jnp.concatenate([cot3_s[m, 2 * p + r] for r in range(4)], axis=1)
         out = jnp.dot(lhs, wt_ref[...], preferred_element_type=F32)
         for k in range(2):
@@ -446,11 +458,42 @@
             v = out[:, k * C : (k + 1) * C] * (((1.0 + t) * mine) * (2.0 + a * (1.0 - t)))
             yb_s[m, s] = v.astype(BF)
             trim(yb_s, m, s)
-        return 0
-
-    lax.fori_loop(0, 2 * MEM, make_pre_cot, 0)
-
-    def weight_grad(rows, y, slot):
+
+    hidden_rows = [(hid3[(e - 1) // 2], (e - 1) % 2) for e in range(2, 8)]
+
+    def grad_two(p):
+        for g in (0, 2):
+            ys = jnp.concatenate(
+                [jnp.concatenate([ya_s[m, 2 * p], ya_s[m, 2 * p + 1]], axis=1) for m in (g, g + 1)],
+                axis=0,
+            )
+            xs = jnp.concatenate(
+                [
+                    jnp.concatenate([ref[m, j] for ref, j in hidden_rows[2 * p : 2 * p + 4]], axis=1)
+                    for m in (g, g + 1)
+                ],
+                axis=0,
+            )
+            part = lax.dot_general(ys, xs, (((0,), (0,)), ((), ())), preferred_element_type=F32)
+            if p == 0 and g == 0:
+                acc2_s[...] = part
+            else:
+                acc2_s[...] += part
+
+    crps_row(3)
+    grad_two(0)
+    crps_row(4)
+    for m in range(MEM):
+        make_pre_cot(m, 0)
+    crps_row(5)
+    grad_two(1)
+    for m in range(MEM):
+        make_pre_cot(m, 1)
+    loss = cells_ref[0] + cells_ref[1] + cells_ref[2] + cells_ref[3]
+    lane = lax.broadcasted_iota(jnp.int32, (1, J), 1)
+    loss = jnp.where((lane >= LEFT) & (lane < LEFT + OWN), loss, 0.0)
+
+    def accumulate(rows, y):
         acc_s[...] = jnp.zeros_like(acc_s)
 
         def step(m, _):
@@ -474,15 +517,18 @@
             return 0
 
         lax.fori_loop(0, MEM, step, 0)
+
+    def finish(acc, slot):
         biggest = jnp.zeros((C, C), F32)
         for k in range(9):
-            blk = acc_s[0:C, k * C : (k + 1) * C] + acc_s[C:, 384 + k * C : 384 + (k + 1) * C]
+            blk = acc[0:C, k * C : (k + 1) * C] + acc[C:, 384 + k * C : 384 + (k + 1) * C]
             biggest = jnp.maximum(biggest, jnp.abs(blk))
             grads_ref[slot, k * C : (k + 1) * C] = jnp.transpose(blk)
         return biggest
 
-    top1 = weight_grad([(in3[e // 2], e % 2) for e in range(2, 8)], yb_s, core)
-    top2 = weight_grad([(hid3[(e - 1) // 2], (e - 1) % 2) for e in range(2, 8)], ya_s, 1 - core)
+    top2 = finish(acc2_s, 1 - core)
+    accumulate([(in3[e // 2], e % 2) for e in range(2, 8)], yb_s)
+    top1 = finish(acc_s, core)
     biggest = jnp.max(jnp.max(jnp.maximum(top1, top2), axis=0, keepdims=True), axis=1, keepdims=True)
     loss = jnp.sum(loss, axis=1, keepdims=True) * (1.0 / (ROWS_TOTAL * LON))
     for slot in range(2):
@@ -510,13 +556,14 @@
             [pltpu.VMEM((J + 2 * PAD, C), F32) for _ in range(6)],
             pltpu.VMEM((MEM, J + 2 * PAD, C), F32),
             pltpu.VMEM((J, C), F32),
-            [pltpu.VMEM((MEM + (k < 3), 2, J, 3 * C), BF) for k in range(5)],
+            [pltpu.VMEM((MEM, 2, J, 3 * C), BF) for _ in range(5)],
             [pltpu.VMEM((MEM, 2, J, 3 * C), BF) for _ in range(4)],
             pltpu.VMEM((MEM, EXT - 4, J, 3 * C), BF),
             pltpu.VMEM((MEM, SLOTS, J, C), F32),
             pltpu.VMEM((MEM, EXT - 4, J, C), BF),
             pltpu.VMEM((MEM, SLOTS, J, C), BF),
             pltpu.VMEM((MEM, SLOTS, J, C), BF),
+            pltpu.VMEM((2 * C, 4 * 384), F32),
             pltpu.VMEM((2 * C, 4 * 384), F32),
             pltpu.SemaphoreType.DMA((2, 2)),
         ],

time: 118 us -> 115 us (0.975)
  Pallas kernels: 38.3 us -> 35.1 us
    pallas_call x1, Pallas kernels: 34.8 us -> 31.6 us  [local_step(): pl.pallas_call(kernel, out_shape=(jax.ShapeDtypeStruct((2, G + 8, C), F32...]
where the time goes in v5:
time: 115 us
  Pallas kernels  35.1 us (31%)
  starting transfers between devices  35 us (30%)
  waiting for transfers between devices  28.9 us (25%)
  other arithmetic  8.16 us (7%)
  local copies, waits for them, and re-layouts  5.73 us (5%)
  between operations  1.99 us (2%)
    pallas_call x1, Pallas kernels, local_step(): pl.pallas_call(kernel, out_shape=(jax.ShapeDtypeStruct((2, G + 8, C), F32...  31.6 us
    ppermute x17, starting transfers between devices, permute(): lax.ppermute(value, BM, [(i, index(move(coords(i)))) for i in range(128)])  27.8 us
    ppermute x17, waiting for transfers between devices, permute(): lax.ppermute(value, BM, [(i, index(move(coords(i)))) for i in range(128)])  16.4 us
    ppermute x3, waiting for transfers between devices, send(): return lax.ppermute(value, BM, pairs)  12.5 us
    ppermute x3, starting transfers between devices, send(): return lax.ppermute(value, BM, pairs)  7.21 us
    pallas_call x1, Pallas kernels, edges(): pl.pallas_call(edge_kernel, out_shape=(rows(4), rows(2), rows(1), jax.Sha...  3.45 us
  transfers between devices with their start and end apart: 20, of which 14 were waited for; matrix products, arithmetic and copies ran while one was open for 5% of the time, Pallas kernels for 3%

profile of v5, /device:TPU:1, one launch (start us, length us, event | category | flops | bytes accessed | tf_op | source)
XLA Modules:
  0.0 114.9 jit_solution(4567005518196575637)
XLA Ops:
  1.3 1.5 %collective-permute-start = (s32[4]{0:T(128)S(1)}, s32[4]{0:T(128)S(1)}, u32[]{:S(2)}, u32[]{:S(2)}) collective-permute-start(s32[4]{0:T(128)S(1)} %compare_select_fusion), channel_id=1, source_target_pairs={{0,1},{1,0},{2,3},{3,2},{4,5},{5,4},{6,7},{7,6},{8,9},{9,8},{10,11... | collective-permute-start | bytes 56 | tf_op jit(solution)/shard_map/ppermute | solution.py:45
  3.4 3.5 %edge_rows.1 = (bf16[4,752,128]{2,1,0:T(8,128)(2,1)}, bf16[2,752,128]{2,1,0:T(8,128)(2,1)}, bf16[1,752,128]{2,1,0:T(8,128)(2,1)}, f32[8,128]{1,0:T(8,128)}) custom-call(s32[32]{0:T(128)} %counts_ref.3, s32[2]{0:T(128)} %pad_add_fusion.place_ref, bf16[4,1440,128]{2,1,0:T(8,128)(2,1)} %state_ref.3, bf16[4,1440,128]{2,1,0:T(8,128)(2,1)} %target_ref.3), custom_call_target="tpu_custom_call" | custom-call | tf_op jit(solution)/shard_map/edge_rows/pallas_call | solution.py:226
  6.9 6.5 %collective-permute-start.2 = (bf16[4,752,128]{2,1,0:T(8,128)(2,1)}, bf16[4,752,128]{2,1,0:T(8,128)(2,1)S(1)}, u32[]{:S(2)}, u32[]{:S(2)}) collective-permute-start(bf16[4,752,128]{2,1,0:T(8,128)(2,1)} %get-tuple-element.20), channel_id=1, source_target_pairs={{0,4},{1,125},{2,6},{3,127},{4,8},{5,1},{6,10},{7,3},{8,12},{9,5},... | collective-permute-start | bytes 2310152 | tf_op jit(solution)/shard_map/ppermute | solution.py:596
  13.3 3.3 %collective-permute-start.1 = (s32[4]{0:T(128)S(1)}, s32[4]{0:T(128)S(1)}, u32[]{:S(2)}, u32[]{:S(2)}) collective-permute-start(s32[4]{0:T(128)S(1)} %fusion.108), channel_id=1, source_target_pairs={{0,2},{1,3},{2,0},{3,1},{4,6},{5,7},{6,4},{7,5},{8,10},{9,11},{10,... | collective-permute-start | bytes 56 | tf_op jit(solution)/shard_map/ppermute | solution.py:45
  16.6 1.3 %collective-permute-done.1 = s32[4]{0:T(128)S(1)} collective-permute-done((s32[4]{0:T(128)S(1)}, s32[4]{0:T(128)S(1)}, u32[]{:S(2)}, u32[]{:S(2)}) %collective-permute-start.1) | collective-permute-done | bytes 48 | tf_op jit(solution)/shard_map/ppermute | solution.py:45
  19.4 0.8 compare_bitcast_fusion.3
  20.2 11.2 %collective-permute-done.4 = bf16[1,752,128]{2,1,0:T(8,128)(2,1)S(1)} collective-permute-done((bf16[1,752,128]{2,1,0:T(8,128)(2,1)}, bf16[1,752,128]{2,1,0:T(8,128)(2,1)S(1)}, u32[]{:S(2)}, u32[]{:S(2)}) %collective-permute-start.4) | collective-permute-done | bytes 192544 | tf_op jit(solution)/shard_map/ppermute | solution.py:596
  31.4 1.3 %collective-permute-done.2 = bf16[4,752,128]{2,1,0:T(8,128)(2,1)S(1)} collective-permute-done((bf16[4,752,128]{2,1,0:T(8,128)(2,1)}, bf16[4,752,128]{2,1,0:T(8,128)(2,1)S(1)}, u32[]{:S(2)}, u32[]{:S(2)}) %collective-permute-start.2) | collective-permute-done | bytes 770080 | tf_op jit(solution)/shard_map/ppermute | solution.py:596
  32.9 0.8 constant_dynamic-slice_fusion
  33.7 2.7 %collective-permute-start.5 = (bf16[4,384,128]{2,1,0:T(8,128)(2,1)S(1)}, bf16[4,384,128]{2,1,0:T(8,128)(2,1)S(1)}, u32[]{:S(2)}, u32[]{:S(2)}) collective-permute-start(bf16[4,384,128]{2,1,0:T(8,128)(2,1)S(1)} %get-tuple-element.52), channel_id=1, source_target_pairs={{0,1},{1,0},{2,3},{3,2},{4,5},{5,4},{6,7},{7,6},{8,9},{9,8},{10,11... | collective-permute-start | bytes 1179656 | tf_op jit(solution)/shard_map/ppermute | solution.py:45
  36.4 0.9 fusion.8.wt_ref
  37.4 1.3 %fusion.6 = (bf16[1536,256]{1,0:T(8,128)(2,1)}, bf16[1536,256]{1,0:T(8,128)(2,1)}) fusion(bf16[1152,128]{1,0:T(8,128)(2,1)S(1)} %bitcast.249, bf16[1152,128]{1,0:T(8,128)(2,1)S(1)} %bitcast.244), kind=kLoop, calls=%fused_computation.8 | loop fusion | flops 5505024 | bytes 2162688 | tf_op jit(solution)/shard_map/concatenate | solution.py:577
  39.4 31.6 %ensemble_step.1 = (f32[2,1160,128]{2,1,0:T(8,128)}, f32[4,1,384]{2,1,0:T(1,128)}) custom-call(s32[32]{0:T(128)} %counts_ref.3, s32[4]{0:T(128)} %add.301.seeds_ref, s32[2]{0:T(128)} %pad_add_fusion.place_ref, f32[96]{0:T(128)} %constant.203.clone.weight_ref, bf16[4,1440,128]{2,1,0:T(8,128)(2,1)} %state_ref.3, bf16[4,1440,128]{2,1,0:T(8,128)(2,1)} %target_ref.3, ...), custom_call_target="tpu_custom_call" | custom-call | tf_op jit(solution)/shard_map/ensemble_step/pallas_call | solution.py:544
  71.1 1.1 slice_bitcast_fusion
  72.6 1.7 %collective-permute-done.6 = f32[1160,128]{1,0:T(8,128)S(1)} collective-permute-done((f32[1160,128]{1,0:T(8,128)S(1)}, f32[1160,128]{1,0:T(8,128)S(1)}, u32[]{:S(2)}, u32[]{:S(2)}) %collective-permute-start.6) | collective-permute-done | bytes 593952 | tf_op jit(solution)/shard_map/ppermute | solution.py:45
  75.1 1.2 %fusion.10 = f16[1152,128]{1,0:T(8,128)(2,1)S(1)} fusion(f32[1160,128]{1,0:T(8,128)S(1)} %collective-permute-done.6, f32[2,1160,128]{2,1,0:T(8,128)} %get-tuple-element.25, f32[128]{0:T(128)S(1)} %divide_bitcast_fusion.3), kind=kLoop, calls=%fused_computation.15 | loop fusion | flops 442368 | bytes 1475072 | tf_op jit(solution)/shard_map/convert_element_type | solution.py:75
  77.9 2.4 %collective-permute-start.9 = (f16[304,128]{1,0:T(8,128)(2,1)S(1)}, f16[304,128]{1,0:T(8,128)(2,1)S(1)}, u32[]{:S(2)}, u32[]{:S(2)}) collective-permute-start(f16[304,128]{1,0:T(8,128)(2,1)S(1)} %concatenate.58), channel_id=1, source_target_pairs={{0,12},{1,13},{2,14},{3,15},{4,0},{5,1},{6,2},{7,3},{8,4},{9,5},{1... | collective-permute-start | bytes 233480 | tf_op jit(solution)/shard_map/ppermute | solution.py:45
  80.4 3.1 %collective-permute-done.7 = f16[304,128]{1,0:T(8,128)(2,1)S(1)} collective-permute-done((f16[304,128]{1,0:T(8,128)(2,1)S(1)}, f16[304,128]{1,0:T(8,128)(2,1)S(1)}, u32[]{:S(2)}, u32[]{:S(2)}) %collective-permute-start.7) | collective-permute-done | bytes 77856 | tf_op jit(solution)/shard_map/ppermute | solution.py:45
  84.6 1.8 %collective-permute-start.11 = (f16[304,128]{1,0:T(8,128)(2,1)S(1)}, f16[304,128]{1,0:T(8,128)(2,1)S(1)}, u32[]{:S(2)}, u32[]{:S(2)}) collective-permute-start(f16[304,128]{1,0:T(8,128)(2,1)S(1)} %concatenate.59), channel_id=1, source_target_pairs={{0,32},{1,33},{2,34},{3,35},{4,36},{5,37},{6,38},{7,39},{8,40},{9,... | collective-permute-start | bytes 233480 | tf_op jit(solution)/shard_map/ppermute | solution.py:45
  86.5 0.8 collective-permute-start.12
  87.4 2.5 %collective-permute-done.10 = f16[304,128]{1,0:T(8,128)(2,1)S(1)} collective-permute-done((f16[304,128]{1,0:T(8,128)(2,1)S(1)}, f16[304,128]{1,0:T(8,128)(2,1)S(1)}, u32[]{:S(2)}, u32[]{:S(2)}) %collective-permute-start.10) | collective-permute-done | bytes 77856 | tf_op jit(solution)/shard_map/ppermute | solution.py:45
  90.0 0.8 collective-permute-done.12
  91.2 1.3 %collective-permute-start.13 = (f16[304,128]{1,0:T(8,128)(2,1)S(1)}, f16[304,128]{1,0:T(8,128)(2,1)S(1)}, u32[]{:S(2)}, u32[]{:S(2)}) collective-permute-start(f16[304,128]{1,0:T(8,128)(2,1)S(1)} %concatenate.60), channel_id=1, source_target_pairs={{0,64},{1,65},{2,66},{3,67},{4,68},{5,69},{6,70},{7,71},{8,72},{9,... | collective-permute-start | bytes 233480 | tf_op jit(solution)/shard_map/ppermute | solution.py:45
  92.5 3.2 %collective-permute-start.14 = (f16[304,128]{1,0:T(8,128)(2,1)S(1)}, f16[304,128]{1,0:T(8,128)(2,1)S(1)}, u32[]{:S(2)}, u32[]{:S(2)}) collective-permute-start(f16[304,128]{1,0:T(8,128)(2,1)S(1)} %concatenate.60), channel_id=1, source_target_pairs={{0,2},{1,3},{2,0},{3,1},{4,6},{5,7},{6,4},{7,5},{8,10},{9,11},{10,... | collective-permute-start | bytes 233480 | tf_op jit(solution)/shard_map/ppermute | solution.py:45
  95.7 0.9 collective-permute-start.15
  96.8 1.6 %collective-permute-done.14 = f16[304,128]{1,0:T(8,128)(2,1)S(1)} collective-permute-done((f16[304,128]{1,0:T(8,128)(2,1)S(1)}, f16[304,128]{1,0:T(8,128)(2,1)S(1)}, u32[]{:S(2)}, u32[]{:S(2)}) %collective-permute-start.14) | collective-permute-done | bytes 77856 | tf_op jit(solution)/shard_map/ppermute | solution.py:45
  98.4 0.9 collective-permute-done.15
  99.8 4.3 %collective-permute-start.17 = (f16[304,128]{1,0:T(8,128)(2,1)S(1)}, f16[304,128]{1,0:T(8,128)(2,1)S(1)}, u32[]{:S(2)}, u32[]{:S(2)}) collective-permute-start(f16[304,128]{1,0:T(8,128)(2,1)S(1)} %concatenate.61), channel_id=1, source_target_pairs={{0,8},{1,9},{2,10},{3,11},{4,12},{5,13},{6,14},{7,15},{8,0},{9,1},... | collective-permute-start | bytes 233480 | tf_op jit(solution)/shard_map/ppermute | solution.py:45
  104.8 2.0 %collective-permute-done.17 = f16[304,128]{1,0:T(8,128)(2,1)S(1)} collective-permute-done((f16[304,128]{1,0:T(8,128)(2,1)S(1)}, f16[304,128]{1,0:T(8,128)(2,1)S(1)}, u32[]{:S(2)}, u32[]{:S(2)}) %collective-permute-start.17) | collective-permute-done | bytes 77856 | tf_op jit(solution)/shard_map/ppermute | solution.py:45
  107.6 4.6 %collective-permute-start.19 = (f32[1152,128]{1,0:T(8,128)S(1)}, f32[1152,128]{1,0:T(8,128)S(1)}, u32[]{:S(2)}, u32[]{:S(2)}) collective-permute-start(f32[1152,128]{1,0:T(8,128)S(1)} %pad_maximum_fusion.1), channel_id=1, source_target_pairs={{0,1},{1,0},{2,3},{3,2},{4,5},{5,4},{6,7},{7,6},{8,9},{9,8},{10,11... | collective-permute-start | bytes 1769480 | tf_op jit(solution)/shard_map/ppermute | solution.py:45
  112.8 0.9 collective-permute-done.19
  113.8 1.1 broadcast_select_fusion
  (93 shorter events, 9.9 us)
Async XLA Ops:
  1.3 5.5 %collective-permute-start = (s32[4]{0:T(128)S(1)}, s32[4]{0:T(128)S(1)}, u32[]{:S(2)}, u32[]{:S(2)}) collective-permute-start(s32[4]{0:T(128)S(1)} %compare_select_fusion), channel_id=1, source_target_pairs={{0,1},{1,0},{2,3},{3,2},{4,5},{5,4},{6,7},{7,6},{8,9},{9,8},{10,11... | collective-permute-start | bytes 56 | tf_op jit(solution)/shard_map/ppermute | solution.py:45
  3.4 15.0 %copy-start = (bf16[3,3,128,128]{3,2,1,0:T(8,128)(2,1)S(1)}, bf16[3,3,128,128]{3,2,1,0:T(8,128)(2,1)}, u32[]{:S(2)}) copy-start(bf16[3,3,128,128]{3,2,1,0:T(8,128)(2,1)} %param.12) | copy-start | bytes 884740
  6.9 25.9 %collective-permute-start.2 = (bf16[4,752,128]{2,1,0:T(8,128)(2,1)}, bf16[4,752,128]{2,1,0:T(8,128)(2,1)S(1)}, u32[]{:S(2)}, u32[]{:S(2)}) collective-permute-start(bf16[4,752,128]{2,1,0:T(8,128)(2,1)} %get-tuple-element.20), channel_id=1, source_target_pairs={{0,4},{1,125},{2,6},{3,127},{4,8},{5,1},{6,10},{7,3},{8,12},{9,5},... | collective-permute-start | bytes 2310152 | tf_op jit(solution)/shard_map/ppermute | solution.py:596
  13.3 4.5 %collective-permute-start.1 = (s32[4]{0:T(128)S(1)}, s32[4]{0:T(128)S(1)}, u32[]{:S(2)}, u32[]{:S(2)}) collective-permute-start(s32[4]{0:T(128)S(1)} %fusion.108), channel_id=1, source_target_pairs={{0,2},{1,3},{2,0},{3,1},{4,6},{5,7},{6,4},{7,5},{8,10},{9,11},{10,... | collective-permute-start | bytes 56 | tf_op jit(solution)/shard_map/ppermute | solution.py:45
  18.4 13.0 %collective-permute-start.3 = (bf16[2,752,128]{2,1,0:T(8,128)(2,1)}, bf16[2,752,128]{2,1,0:T(8,128)(2,1)S(1)}, u32[]{:S(2)}, u32[]{:S(2)}) collective-permute-start(bf16[2,752,128]{2,1,0:T(8,128)(2,1)} %get-tuple-element.22), channel_id=1, source_target_pairs={{0,8},{1,121},{2,10},{3,123},{4,12},{5,125},{6,14},{7,127},{8,16},... | collective-permute-start | bytes 1155080 | tf_op jit(solution)/shard_map/ppermute | solution.py:596
  18.6 12.8 %collective-permute-start.4 = (bf16[1,752,128]{2,1,0:T(8,128)(2,1)}, bf16[1,752,128]{2,1,0:T(8,128)(2,1)S(1)}, u32[]{:S(2)}, u32[]{:S(2)}) collective-permute-start(bf16[1,752,128]{2,1,0:T(8,128)(2,1)} %get-tuple-element.23), channel_id=1, source_target_pairs={{0,12},{1,117},{2,14},{3,119},{4,16},{5,121},{6,18},{7,123},{8,20}... | collective-permute-start | bytes 577544 | tf_op jit(solution)/shard_map/ppermute | solution.py:596
  32.9 4.5 %copy-start.2 = (bf16[3,3,128,128]{3,2,1,0:T(8,128)(2,1)S(1)}, bf16[3,3,128,128]{3,2,1,0:T(8,128)(2,1)}, u32[]{:S(2)}) copy-start(bf16[3,3,128,128]{3,2,1,0:T(8,128)(2,1)} %param.11) | copy-start | bytes 884740
  33.7 5.0 %collective-permute-start.5 = (bf16[4,384,128]{2,1,0:T(8,128)(2,1)S(1)}, bf16[4,384,128]{2,1,0:T(8,128)(2,1)S(1)}, u32[]{:S(2)}, u32[]{:S(2)}) collective-permute-start(bf16[4,384,128]{2,1,0:T(8,128)(2,1)S(1)} %get-tuple-element.52), channel_id=1, source_target_pairs={{0,1},{1,0},{2,3},{3,2},{4,5},{5,4},{6,7},{7,6},{8,9},{9,8},{10,11... | collective-permute-start | bytes 1179656 | tf_op jit(solution)/shard_map/ppermute | solution.py:45
  38.7 0.7 copy-start.1
  72.2 2.1 %collective-permute-start.6 = (f32[1160,128]{1,0:T(8,128)S(1)}, f32[1160,128]{1,0:T(8,128)S(1)}, u32[]{:S(2)}, u32[]{:S(2)}) collective-permute-start(f32[1160,128]{1,0:T(8,128)S(1)} %slice_bitcast_fusion), channel_id=1, source_target_pairs={{0,1},{1,0},{2,3},{3,2},{4,5},{5,4},{6,7},{7,6},{8,9},{9,8},{10,11... | collective-permute-start | bytes 1781768 | tf_op jit(solution)/shard_map/ppermute | solution.py:45
  76.8 6.7 %collective-permute-start.7 = (f16[304,128]{1,0:T(8,128)(2,1)S(1)}, f16[304,128]{1,0:T(8,128)(2,1)S(1)}, u32[]{:S(2)}, u32[]{:S(2)}) collective-permute-start(f16[304,128]{1,0:T(8,128)(2,1)S(1)} %concatenate.56), channel_id=1, source_target_pairs={{0,4},{1,5},{2,6},{3,7},{4,8},{5,9},{6,10},{7,11},{8,12},{9,13},{1... | collective-permute-start | bytes 233480 | tf_op jit(solution)/shard_map/ppermute | solution.py:45
  77.1 6.5 %collective-permute-start.8 = (f16[304,128]{1,0:T(8,128)(2,1)S(1)}, f16[304,128]{1,0:T(8,128)(2,1)S(1)}, u32[]{:S(2)}, u32[]{:S(2)}) collective-permute-start(f16[304,128]{1,0:T(8,128)(2,1)S(1)} %concatenate.57), channel_id=1, source_target_pairs={{0,8},{1,9},{2,10},{3,11},{4,12},{5,13},{6,14},{7,15},{8,0},{9,1},... | collective-permute-start | bytes 233480 | tf_op jit(solution)/shard_map/ppermute | solution.py:45
  77.9 6.2 %collective-permute-start.9 = (f16[304,128]{1,0:T(8,128)(2,1)S(1)}, f16[304,128]{1,0:T(8,128)(2,1)S(1)}, u32[]{:S(2)}, u32[]{:S(2)}) collective-permute-start(f16[304,128]{1,0:T(8,128)(2,1)S(1)} %concatenate.58), channel_id=1, source_target_pairs={{0,12},{1,13},{2,14},{3,15},{4,0},{5,1},{6,2},{7,3},{8,4},{9,5},{1... | collective-permute-start | bytes 233480 | tf_op jit(solution)/shard_map/ppermute | solution.py:45
  84.5 5.4 %collective-permute-start.10 = (f16[304,128]{1,0:T(8,128)(2,1)S(1)}, f16[304,128]{1,0:T(8,128)(2,1)S(1)}, u32[]{:S(2)}, u32[]{:S(2)}) collective-permute-start(f16[304,128]{1,0:T(8,128)(2,1)S(1)} %concatenate.59), channel_id=1, source_target_pairs={{0,16},{1,17},{2,18},{3,19},{4,20},{5,21},{6,22},{7,23},{8,24},{9,... | collective-permute-start | bytes 233480 | tf_op jit(solution)/shard_map/ppermute | solution.py:45
  84.6 5.3 %collective-permute-start.11 = (f16[304,128]{1,0:T(8,128)(2,1)S(1)}, f16[304,128]{1,0:T(8,128)(2,1)S(1)}, u32[]{:S(2)}, u32[]{:S(2)}) collective-permute-start(f16[304,128]{1,0:T(8,128)(2,1)S(1)} %concatenate.59), channel_id=1, source_target_pairs={{0,32},{1,33},{2,34},{3,35},{4,36},{5,37},{6,38},{7,39},{8,40},{9,... | collective-permute-start | bytes 233480 | tf_op jit(solution)/shard_map/ppermute | solution.py:45
  86.5 4.3 %collective-permute-start.12 = (f16[304,128]{1,0:T(8,128)(2,1)S(1)}, f16[304,128]{1,0:T(8,128)(2,1)S(1)}, u32[]{:S(2)}, u32[]{:S(2)}) collective-permute-start(f16[304,128]{1,0:T(8,128)(2,1)S(1)} %concatenate.59), channel_id=1, source_target_pairs={{0,48},{1,49},{2,50},{3,51},{4,52},{5,53},{6,54},{7,55},{8,56},{9,... | collective-permute-start | bytes 233480 | tf_op jit(solution)/shard_map/ppermute | solution.py:45
  91.2 5.5 %collective-permute-start.13 = (f16[304,128]{1,0:T(8,128)(2,1)S(1)}, f16[304,128]{1,0:T(8,128)(2,1)S(1)}, u32[]{:S(2)}, u32[]{:S(2)}) collective-permute-start(f16[304,128]{1,0:T(8,128)(2,1)S(1)} %concatenate.60), channel_id=1, source_target_pairs={{0,64},{1,65},{2,66},{3,67},{4,68},{5,69},{6,70},{7,71},{8,72},{9,... | collective-permute-start | bytes 233480 | tf_op jit(solution)/shard_map/ppermute | solution.py:45
  92.5 5.8 %collective-permute-start.14 = (f16[304,128]{1,0:T(8,128)(2,1)S(1)}, f16[304,128]{1,0:T(8,128)(2,1)S(1)}, u32[]{:S(2)}, u32[]{:S(2)}) collective-permute-start(f16[304,128]{1,0:T(8,128)(2,1)S(1)} %concatenate.60), channel_id=1, source_target_pairs={{0,2},{1,3},{2,0},{3,1},{4,6},{5,7},{6,4},{7,5},{8,10},{9,11},{10,... | collective-permute-start | bytes 233480 | tf_op jit(solution)/shard_map/ppermute | solution.py:45
  95.7 3.5 %collective-permute-start.15 = (f16[304,128]{1,0:T(8,128)(2,1)S(1)}, f16[304,128]{1,0:T(8,128)(2,1)S(1)}, u32[]{:S(2)}, u32[]{:S(2)}) collective-permute-start(f16[304,128]{1,0:T(8,128)(2,1)S(1)} %concatenate.60), channel_id=1, source_target_pairs={{0,66},{1,67},{2,64},{3,65},{4,70},{5,71},{6,68},{7,69},{8,74},{9,... | collective-permute-start | bytes 233480 | tf_op jit(solution)/shard_map/ppermute | solution.py:45
  99.4 8.2 %copy-start.4 = (f32[1,128]{1,0:T(1,128)}, f32[1,128]{1,0:T(1,128)S(1)}, u32[]{:S(2)}) copy-start(f32[1,128]{1,0:T(1,128)S(1)} %get-tuple-element.28) | copy-start | bytes 1540
  99.7 12.4 %copy-start.3 = (f32[4,1,384]{2,1,0:T(1,128)S(1)}, f32[4,1,384]{2,1,0:T(1,128)}, u32[]{:S(2)}) copy-start(f32[4,1,384]{2,1,0:T(1,128)} %get-tuple-element.24) | copy-start | bytes 18436
  99.8 5.0 %collective-permute-start.16 = (f16[304,128]{1,0:T(8,128)(2,1)S(1)}, f16[304,128]{1,0:T(8,128)(2,1)S(1)}, u32[]{:S(2)}, u32[]{:S(2)}) collective-permute-start(f16[304,128]{1,0:T(8,128)(2,1)S(1)} %concatenate.61), channel_id=1, source_target_pairs={{0,4},{1,5},{2,6},{3,7},{4,8},{5,9},{6,10},{7,11},{8,12},{9,13},{1... | collective-permute-start | bytes 233480 | tf_op jit(solution)/shard_map/ppermute | solution.py:45
  99.8 7.0 %collective-permute-start.17 = (f16[304,128]{1,0:T(8,128)(2,1)S(1)}, f16[304,128]{1,0:T(8,128)(2,1)S(1)}, u32[]{:S(2)}, u32[]{:S(2)}) collective-permute-start(f16[304,128]{1,0:T(8,128)(2,1)S(1)} %concatenate.61), channel_id=1, source_target_pairs={{0,8},{1,9},{2,10},{3,11},{4,12},{5,13},{6,14},{7,15},{8,0},{9,1},... | collective-permute-start | bytes 233480 | tf_op jit(solution)/shard_map/ppermute | solution.py:45
  104.2 3.2 %collective-permute-start.18 = (f16[304,128]{1,0:T(8,128)(2,1)S(1)}, f16[304,128]{1,0:T(8,128)(2,1)S(1)}, u32[]{:S(2)}, u32[]{:S(2)}) collective-permute-start(f16[304,128]{1,0:T(8,128)(2,1)S(1)} %concatenate.61), channel_id=1, source_target_pairs={{0,12},{1,13},{2,14},{3,15},{4,0},{5,1},{6,2},{7,3},{8,4},{9,5},{1... | collective-permute-start | bytes 233480 | tf_op jit(solution)/shard_map/ppermute | solution.py:45
  107.6 6.2 %collective-permute-start.19 = (f32[1152,128]{1,0:T(8,128)S(1)}, f32[1152,128]{1,0:T(8,128)S(1)}, u32[]{:S(2)}, u32[]{:S(2)}) collective-permute-start(f32[1152,128]{1,0:T(8,128)S(1)} %pad_maximum_fusion.1), channel_id=1, source_target_pairs={{0,1},{1,0},{2,3},{3,2},{4,5},{5,4},{6,7},{7,6},{8,9},{9,8},{10,11... | collective-permute-start | bytes 1769480 | tf_op jit(solution)/shard_map/ppermute | solution.py:45

commit v6 on v5

--- a/solution.py
+++ b/solution.py
@@ -227,7 +227,7 @@
         edge_kernel,
         out_shape=(rows(4), rows(2), rows(1), jax.ShapeDtypeStruct((8, C), F32)),
         in_specs=[smem, smem, hbm, hbm],
-        out_specs=(vmem,) * 4,
+        out_specs=(hbm, hbm, hbm, vmem),
         scratch_shapes=[pltpu.SemaphoreType.DMA((7, 2))],
         name="edge_rows",
     )(counts, place, state, target)
@@ -601,9 +601,13 @@
     one, seeds = lax.optimization_barrier((one, seeds))
     g1 = send(one, 1)
     seeds = seeds + shift(seeds, 3, 1)
-    two, three, seeds = lax.optimization_barrier((two, three, seeds))
+    two, three, seeds, filt1, filt2 = lax.optimization_barrier((two, three, seeds, filt1, filt2))
     g2 = send(two, 2)
     g3 = send(three, 3)
+    w1 = paired(filt1)
+    w2 = paired(filt2)
+    wt = paired(jnp.transpose(filt2[::-1, ::-1], (0, 1, 3, 2)))
+    g3, w1, w2, wt = lax.optimization_barrier((g3, w1, w2, wt))
     row2 = jnp.where(flag(0), g1[1:2], g2[:1])
     row3 = jnp.where(
         flag(1), g1[2:3], jnp.where(flag(2), g2[:1], jnp.where(flag(3), g2[1:], g3))
@@ -612,9 +616,6 @@
     mine = lax.dynamic_slice_in_dim(halo, OWN * core, J, 1)
     other = shift(lax.dynamic_slice_in_dim(halo, OWN * (1 - core), J, 1), 4, 1)
 
-    w1 = paired(filt1)
-    w2 = paired(filt2)
-    wt = paired(jnp.transpose(filt2[::-1, ::-1], (0, 1, 3, 2)))
     grads, cells = local_step(
         counts, seeds, place, weights, state, target, mine, other, amp[None], w1, w2, wt
     )

time: 115 us -> 154 us (1.34)
  Pallas kernels: 35.1 us -> 75.1 us
    pallas_call x1, Pallas kernels: 3.45 us -> 43.5 us  [edges(): pl.pallas_call(edge_kernel, out_shape=(rows(4), rows(2), rows(1), jax.Sha...]
    ppermute x17, waiting for transfers between devices: 16.4 us -> 18.4 us  [permute(): lax.ppermute(value, BM, [(i, index(move(coords(i)))) for i in range(128)])]
    ppermute x3, waiting for transfers between devices: 12.5 us -> 10.7 us  [send(): return lax.ppermute(value, BM, pairs)]
  transfers between devices with their start and end apart: 20 -> 20, of which waited for: 14 -> 15; matrix products, arithmetic and copies ran while one was open for 5% -> 4% of each run, Pallas kernels for 3% -> 28%
where the time goes in v6:
time: 154 us
  Pallas kernels  75.1 us (49%)
  starting transfers between devices  34 us (22%)
  waiting for transfers between devices  29.2 us (19%)
  other arithmetic  8.15 us (5%)
  local copies, waits for them, and re-layouts  5.72 us (4%)
  between operations  1.65 us (1%)
    pallas_call x1, Pallas kernels, edges(): pl.pallas_call(edge_kernel, out_shape=(rows(4), rows(2), rows(1), jax.Sha...  43.5 us
    pallas_call x1, Pallas kernels, local_step(): pl.pallas_call(kernel, out_shape=(jax.ShapeDtypeStruct((2, G + 8, C), F32...  31.6 us
    ppermute x17, starting transfers between devices, permute(): lax.ppermute(value, BM, [(i, index(move(coords(i)))) for i in range(128)])  26.3 us
    ppermute x17, waiting for transfers between devices, permute(): lax.ppermute(value, BM, [(i, index(move(coords(i)))) for i in range(128)])  18.4 us
    ppermute x3, waiting for transfers between devices, send(): return lax.ppermute(value, BM, pairs)  10.7 us
    ppermute x3, starting transfers between devices, send(): return lax.ppermute(value, BM, pairs)  7.68 us
  transfers between devices with their start and end apart: 20, of which 15 were waited for; matrix products, arithmetic and copies ran while one was open for 4% of the time, Pallas kernels for 28%

profile of v6, /device:TPU:1, one launch (start us, length us, event | category | flops | bytes accessed | tf_op | source)
XLA Modules:
  0.0 153.7 jit_solution(5492064076512326491)
XLA Ops:
  1.3 1.5 collective-permute-start
  3.4 43.5 %edge_rows.1 = (bf16[4,752,128]{2,1,0:T(8,128)(2,1)}, bf16[2,752,128]{2,1,0:T(8,128)(2,1)}, bf16[1,752,128]{2,1,0:T(8,128)(2,1)}, f32[8,128]{1,0:T(8,128)}) custom-call(s32[32]{0:T(128)} %counts_ref.3, s32[2]{0:T(128)} %pad_add_fusion.place_ref, bf16[4,1440,128]{2,1,0:T(8,128)(2,1)} %state_ref.3, bf16[4,1440,128]{2,1,0:T(8,128)(2,1)} %target_ref.3), custom_call_target="tpu_custom_call" | custom-call | tf_op jit(solution)/shard_map/edge_rows/pallas_call | solution.py:226
  46.9 6.5 %collective-permute-start.2 = (bf16[4,752,128]{2,1,0:T(8,128)(2,1)}, bf16[4,752,128]{2,1,0:T(8,128)(2,1)S(1)}, u32[]{:S(2)}, u32[]{:S(2)}) collective-permute-start(bf16[4,752,128]{2,1,0:T(8,128)(2,1)} %get-tuple-element.26), channel_id=1, source_target_pairs={{0,4},{1,125},{2,6},{3,127},{4,8},{5,1},{6,10},{7,3},{8,12},{9,5},... | collective-permute-start | bytes 2310152 | tf_op jit(solution)/shard_map/ppermute | solution.py:596
  53.3 0.8 compare_bitcast_fusion.3
  54.2 3.3 %collective-permute-start.1 = (s32[4]{0:T(128)S(1)}, s32[4]{0:T(128)S(1)}, u32[]{:S(2)}, u32[]{:S(2)}) collective-permute-start(s32[4]{0:T(128)S(1)} %fusion.108), channel_id=1, source_target_pairs={{0,2},{1,3},{2,0},{3,1},{4,6},{5,7},{6,4},{7,5},{8,10},{9,11},{10,... | collective-permute-start | bytes 56 | tf_op jit(solution)/shard_map/ppermute | solution.py:45
  57.5 1.3 collective-permute-done.1
  59.3 1.2 collective-permute-start.3
  60.5 1.3 fusion.6
  62.1 1.0 fusion.8.wt_ref
  63.0 10.7 %collective-permute-done.4 = bf16[1,752,128]{2,1,0:T(8,128)(2,1)S(1)} collective-permute-done((bf16[1,752,128]{2,1,0:T(8,128)(2,1)}, bf16[1,752,128]{2,1,0:T(8,128)(2,1)S(1)}, u32[]{:S(2)}, u32[]{:S(2)}) %collective-permute-start.4) | collective-permute-done | bytes 192544 | tf_op jit(solution)/shard_map/ppermute | solution.py:596
  74.0 0.8 constant_dynamic-slice_fusion
  74.8 1.7 %collective-permute-start.5 = (bf16[4,384,128]{2,1,0:T(8,128)(2,1)S(1)}, bf16[4,384,128]{2,1,0:T(8,128)(2,1)S(1)}, u32[]{:S(2)}, u32[]{:S(2)}) collective-permute-start(bf16[4,384,128]{2,1,0:T(8,128)(2,1)S(1)} %get-tuple-element.64), channel_id=1, source_target_pairs={{0,1},{1,0},{2,3},{3,2},{4,5},{5,4},{6,7},{7,6},{8,9},{9,8},{10,11... | collective-permute-start | bytes 1179656 | tf_op jit(solution)/shard_map/ppermute | solution.py:45
  76.5 1.3 collective-permute-done.5.other_ref
  78.6 31.6 %ensemble_step.1 = (f32[2,1160,128]{2,1,0:T(8,128)}, f32[4,1,384]{2,1,0:T(1,128)}) custom-call(s32[32]{0:T(128)} %counts_ref.3, s32[4]{0:T(128)} %add.301.seeds_ref, s32[2]{0:T(128)} %pad_add_fusion.place_ref, f32[96]{0:T(128)} %constant.203.clone.weight_ref, bf16[4,1440,128]{2,1,0:T(8,128)(2,1)} %state_ref.3, bf16[4,1440,128]{2,1,0:T(8,128)(2,1)} %target_ref.3, ...), custom_call_target="tpu_custom_call" | custom-call | tf_op jit(solution)/shard_map/ensemble_step/pallas_call | solution.py:544
  110.2 1.1 slice_bitcast_fusion
  111.8 1.6 %collective-permute-done.6 = f32[1160,128]{1,0:T(8,128)S(1)} collective-permute-done((f32[1160,128]{1,0:T(8,128)S(1)}, f32[1160,128]{1,0:T(8,128)S(1)}, u32[]{:S(2)}, u32[]{:S(2)}) %collective-permute-start.6) | collective-permute-done | bytes 593952 | tf_op jit(solution)/shard_map/ppermute | solution.py:45
  114.2 1.2 fusion.10
  116.2 1.0 collective-permute-start.8
  117.4 2.0 %collective-permute-start.9 = (f16[304,128]{1,0:T(8,128)(2,1)S(1)}, f16[304,128]{1,0:T(8,128)(2,1)S(1)}, u32[]{:S(2)}, u32[]{:S(2)}) collective-permute-start(f16[304,128]{1,0:T(8,128)(2,1)S(1)} %concatenate.58), channel_id=1, source_target_pairs={{0,12},{1,13},{2,14},{3,15},{4,0},{5,1},{6,2},{7,3},{8,4},{9,5},{1... | collective-permute-start | bytes 233480 | tf_op jit(solution)/shard_map/ppermute | solution.py:45
  119.5 3.0 %collective-permute-done.7 = f16[304,128]{1,0:T(8,128)(2,1)S(1)} collective-permute-done((f16[304,128]{1,0:T(8,128)(2,1)S(1)}, f16[304,128]{1,0:T(8,128)(2,1)S(1)}, u32[]{:S(2)}, u32[]{:S(2)}) %collective-permute-start.7) | collective-permute-done | bytes 77856 | tf_op jit(solution)/shard_map/ppermute | solution.py:45
  123.5 2.0 %collective-permute-start.11 = (f16[304,128]{1,0:T(8,128)(2,1)S(1)}, f16[304,128]{1,0:T(8,128)(2,1)S(1)}, u32[]{:S(2)}, u32[]{:S(2)}) collective-permute-start(f16[304,128]{1,0:T(8,128)(2,1)S(1)} %concatenate.59), channel_id=1, source_target_pairs={{0,32},{1,33},{2,34},{3,35},{4,36},{5,37},{6,38},{7,39},{8,40},{9,... | collective-permute-start | bytes 233480 | tf_op jit(solution)/shard_map/ppermute | solution.py:45
  126.3 2.5 %collective-permute-done.10 = f16[304,128]{1,0:T(8,128)(2,1)S(1)} collective-permute-done((f16[304,128]{1,0:T(8,128)(2,1)S(1)}, f16[304,128]{1,0:T(8,128)(2,1)S(1)}, u32[]{:S(2)}, u32[]{:S(2)}) %collective-permute-start.10) | collective-permute-done | bytes 77856 | tf_op jit(solution)/shard_map/ppermute | solution.py:45
  130.1 2.2 %collective-permute-start.13 = (f16[304,128]{1,0:T(8,128)(2,1)S(1)}, f16[304,128]{1,0:T(8,128)(2,1)S(1)}, u32[]{:S(2)}, u32[]{:S(2)}) collective-permute-start(f16[304,128]{1,0:T(8,128)(2,1)S(1)} %concatenate.60), channel_id=1, source_target_pairs={{0,64},{1,65},{2,66},{3,67},{4,68},{5,69},{6,70},{7,71},{8,72},{9,... | collective-permute-start | bytes 233480 | tf_op jit(solution)/shard_map/ppermute | solution.py:45
  132.4 3.3 %collective-permute-start.14 = (f16[304,128]{1,0:T(8,128)(2,1)S(1)}, f16[304,128]{1,0:T(8,128)(2,1)S(1)}, u32[]{:S(2)}, u32[]{:S(2)}) collective-permute-start(f16[304,128]{1,0:T(8,128)(2,1)S(1)} %concatenate.60), channel_id=1, source_target_pairs={{0,2},{1,3},{2,0},{3,1},{4,6},{5,7},{6,4},{7,5},{8,10},{9,11},{10,... | collective-permute-start | bytes 233480 | tf_op jit(solution)/shard_map/ppermute | solution.py:45
  136.2 2.0 %collective-permute-done.14 = f16[304,128]{1,0:T(8,128)(2,1)S(1)} collective-permute-done((f16[304,128]{1,0:T(8,128)(2,1)S(1)}, f16[304,128]{1,0:T(8,128)(2,1)S(1)}, u32[]{:S(2)}, u32[]{:S(2)}) %collective-permute-start.14) | collective-permute-done | bytes 77856 | tf_op jit(solution)/shard_map/ppermute | solution.py:45
  138.3 0.9 collective-permute-done.15
  139.7 3.3 %collective-permute-start.17 = (f16[304,128]{1,0:T(8,128)(2,1)S(1)}, f16[304,128]{1,0:T(8,128)(2,1)S(1)}, u32[]{:S(2)}, u32[]{:S(2)}) collective-permute-start(f16[304,128]{1,0:T(8,128)(2,1)S(1)} %concatenate.61), channel_id=1, source_target_pairs={{0,8},{1,9},{2,10},{3,11},{4,12},{5,13},{6,14},{7,15},{8,0},{9,1},... | collective-permute-start | bytes 233480 | tf_op jit(solution)/shard_map/ppermute | solution.py:45
  143.1 1.1 collective-permute-done.16
  144.2 1.4 collective-permute-done.17
  146.4 4.6 %collective-permute-start.19 = (f32[1152,128]{1,0:T(8,128)S(1)}, f32[1152,128]{1,0:T(8,128)S(1)}, u32[]{:S(2)}, u32[]{:S(2)}) collective-permute-start(f32[1152,128]{1,0:T(8,128)S(1)} %pad_maximum_fusion.1), channel_id=1, source_target_pairs={{0,1},{1,0},{2,3},{3,2},{4,5},{5,4},{6,7},{7,6},{8,9},{9,8},{10,11... | collective-permute-start | bytes 1769480 | tf_op jit(solution)/shard_map/ppermute | solution.py:45
  151.7 0.9 collective-permute-done.19
  152.6 1.1 broadcast_select_fusion
  (93 shorter events, 10.2 us)
Async XLA Ops:
  1.3 45.6 %collective-permute-start = (s32[4]{0:T(128)S(1)}, s32[4]{0:T(128)S(1)}, u32[]{:S(2)}, u32[]{:S(2)}) collective-permute-start(s32[4]{0:T(128)S(1)} %compare_select_fusion), channel_id=1, source_target_pairs={{0,1},{1,0},{2,3},{3,2},{4,5},{5,4},{6,7},{7,6},{8,9},{9,8},{10,11... | collective-permute-start | bytes 56 | tf_op jit(solution)/shard_map/ppermute | solution.py:45
  3.4 57.2 %copy-start = (bf16[3,3,128,128]{3,2,1,0:T(8,128)(2,1)S(1)}, bf16[3,3,128,128]{3,2,1,0:T(8,128)(2,1)}, u32[]{:S(2)}) copy-start(bf16[3,3,128,128]{3,2,1,0:T(8,128)(2,1)} %param.12) | copy-start | bytes 884740
  3.4 57.2 %copy-start.2 = (bf16[3,3,128,128]{3,2,1,0:T(8,128)(2,1)S(1)}, bf16[3,3,128,128]{3,2,1,0:T(8,128)(2,1)}, u32[]{:S(2)}) copy-start(bf16[3,3,128,128]{3,2,1,0:T(8,128)(2,1)} %param.11) | copy-start | bytes 884740
  46.9 26.9 %collective-permute-start.2 = (bf16[4,752,128]{2,1,0:T(8,128)(2,1)}, bf16[4,752,128]{2,1,0:T(8,128)(2,1)S(1)}, u32[]{:S(2)}, u32[]{:S(2)}) collective-permute-start(bf16[4,752,128]{2,1,0:T(8,128)(2,1)} %get-tuple-element.26), channel_id=1, source_target_pairs={{0,4},{1,125},{2,6},{3,127},{4,8},{5,1},{6,10},{7,3},{8,12},{9,5},... | collective-permute-start | bytes 2310152 | tf_op jit(solution)/shard_map/ppermute | solution.py:596
  54.2 4.6 %collective-permute-start.1 = (s32[4]{0:T(128)S(1)}, s32[4]{0:T(128)S(1)}, u32[]{:S(2)}, u32[]{:S(2)}) collective-permute-start(s32[4]{0:T(128)S(1)} %fusion.108), channel_id=1, source_target_pairs={{0,2},{1,3},{2,0},{3,1},{4,6},{5,7},{6,4},{7,5},{8,10},{9,11},{10,... | collective-permute-start | bytes 56 | tf_op jit(solution)/shard_map/ppermute | solution.py:45
  59.3 14.4 %collective-permute-start.4 = (bf16[1,752,128]{2,1,0:T(8,128)(2,1)}, bf16[1,752,128]{2,1,0:T(8,128)(2,1)S(1)}, u32[]{:S(2)}, u32[]{:S(2)}) collective-permute-start(bf16[1,752,128]{2,1,0:T(8,128)(2,1)} %get-tuple-element.29), channel_id=1, source_target_pairs={{0,12},{1,117},{2,14},{3,119},{4,16},{5,121},{6,18},{7,123},{8,20}... | collective-permute-start | bytes 577544 | tf_op jit(solution)/shard_map/ppermute | solution.py:596
  59.3 14.4 %collective-permute-start.3 = (bf16[2,752,128]{2,1,0:T(8,128)(2,1)}, bf16[2,752,128]{2,1,0:T(8,128)(2,1)S(1)}, u32[]{:S(2)}, u32[]{:S(2)}) collective-permute-start(bf16[2,752,128]{2,1,0:T(8,128)(2,1)} %get-tuple-element.28), channel_id=1, source_target_pairs={{0,8},{1,121},{2,10},{3,123},{4,12},{5,125},{6,14},{7,127},{8,16},... | collective-permute-start | bytes 1155080 | tf_op jit(solution)/shard_map/ppermute | solution.py:596
  74.8 3.1 %collective-permute-start.5 = (bf16[4,384,128]{2,1,0:T(8,128)(2,1)S(1)}, bf16[4,384,128]{2,1,0:T(8,128)(2,1)S(1)}, u32[]{:S(2)}, u32[]{:S(2)}) collective-permute-start(bf16[4,384,128]{2,1,0:T(8,128)(2,1)S(1)} %get-tuple-element.64), channel_id=1, source_target_pairs={{0,1},{1,0},{2,3},{3,2},{4,5},{5,4},{6,7},{7,6},{8,9},{9,8},{10,11... | collective-permute-start | bytes 1179656 | tf_op jit(solution)/shard_map/ppermute | solution.py:45
  77.9 0.7 copy-start.1
  111.3 2.1 %collective-permute-start.6 = (f32[1160,128]{1,0:T(8,128)S(1)}, f32[1160,128]{1,0:T(8,128)S(1)}, u32[]{:S(2)}, u32[]{:S(2)}) collective-permute-start(f32[1160,128]{1,0:T(8,128)S(1)} %slice_bitcast_fusion), channel_id=1, source_target_pairs={{0,1},{1,0},{2,3},{3,2},{4,5},{5,4},{6,7},{7,6},{8,9},{9,8},{10,11... | collective-permute-start | bytes 1781768 | tf_op jit(solution)/shard_map/ppermute | solution.py:45
  115.9 6.6 %collective-permute-start.7 = (f16[304,128]{1,0:T(8,128)(2,1)S(1)}, f16[304,128]{1,0:T(8,128)(2,1)S(1)}, u32[]{:S(2)}, u32[]{:S(2)}) collective-permute-start(f16[304,128]{1,0:T(8,128)(2,1)S(1)} %concatenate.56), channel_id=1, source_target_pairs={{0,4},{1,5},{2,6},{3,7},{4,8},{5,9},{6,10},{7,11},{8,12},{9,13},{1... | collective-permute-start | bytes 233480 | tf_op jit(solution)/shard_map/ppermute | solution.py:45
  116.2 6.4 %collective-permute-start.8 = (f16[304,128]{1,0:T(8,128)(2,1)S(1)}, f16[304,128]{1,0:T(8,128)(2,1)S(1)}, u32[]{:S(2)}, u32[]{:S(2)}) collective-permute-start(f16[304,128]{1,0:T(8,128)(2,1)S(1)} %concatenate.57), channel_id=1, source_target_pairs={{0,8},{1,9},{2,10},{3,11},{4,12},{5,13},{6,14},{7,15},{8,0},{9,1},... | collective-permute-start | bytes 233480 | tf_op jit(solution)/shard_map/ppermute | solution.py:45
  117.4 5.6 %collective-permute-start.9 = (f16[304,128]{1,0:T(8,128)(2,1)S(1)}, f16[304,128]{1,0:T(8,128)(2,1)S(1)}, u32[]{:S(2)}, u32[]{:S(2)}) collective-permute-start(f16[304,128]{1,0:T(8,128)(2,1)S(1)} %concatenate.58), channel_id=1, source_target_pairs={{0,12},{1,13},{2,14},{3,15},{4,0},{5,1},{6,2},{7,3},{8,4},{9,5},{1... | collective-permute-start | bytes 233480 | tf_op jit(solution)/shard_map/ppermute | solution.py:45
  123.4 5.4 %collective-permute-start.10 = (f16[304,128]{1,0:T(8,128)(2,1)S(1)}, f16[304,128]{1,0:T(8,128)(2,1)S(1)}, u32[]{:S(2)}, u32[]{:S(2)}) collective-permute-start(f16[304,128]{1,0:T(8,128)(2,1)S(1)} %concatenate.59), channel_id=1, source_target_pairs={{0,16},{1,17},{2,18},{3,19},{4,20},{5,21},{6,22},{7,23},{8,24},{9,... | collective-permute-start | bytes 233480 | tf_op jit(solution)/shard_map/ppermute | solution.py:45
  123.5 5.3 %collective-permute-start.11 = (f16[304,128]{1,0:T(8,128)(2,1)S(1)}, f16[304,128]{1,0:T(8,128)(2,1)S(1)}, u32[]{:S(2)}, u32[]{:S(2)}) collective-permute-start(f16[304,128]{1,0:T(8,128)(2,1)S(1)} %concatenate.59), channel_id=1, source_target_pairs={{0,32},{1,33},{2,34},{3,35},{4,36},{5,37},{6,38},{7,39},{8,40},{9,... | collective-permute-start | bytes 233480 | tf_op jit(solution)/shard_map/ppermute | solution.py:45
  125.5 4.2 %collective-permute-start.12 = (f16[304,128]{1,0:T(8,128)(2,1)S(1)}, f16[304,128]{1,0:T(8,128)(2,1)S(1)}, u32[]{:S(2)}, u32[]{:S(2)}) collective-permute-start(f16[304,128]{1,0:T(8,128)(2,1)S(1)} %concatenate.59), channel_id=1, source_target_pairs={{0,48},{1,49},{2,50},{3,51},{4,52},{5,53},{6,54},{7,55},{8,56},{9,... | collective-permute-start | bytes 233480 | tf_op jit(solution)/shard_map/ppermute | solution.py:45
  130.1 6.1 %collective-permute-start.13 = (f16[304,128]{1,0:T(8,128)(2,1)S(1)}, f16[304,128]{1,0:T(8,128)(2,1)S(1)}, u32[]{:S(2)}, u32[]{:S(2)}) collective-permute-start(f16[304,128]{1,0:T(8,128)(2,1)S(1)} %concatenate.60), channel_id=1, source_target_pairs={{0,64},{1,65},{2,66},{3,67},{4,68},{5,69},{6,70},{7,71},{8,72},{9,... | collective-permute-start | bytes 233480 | tf_op jit(solution)/shard_map/ppermute | solution.py:45
  132.4 5.9 %collective-permute-start.14 = (f16[304,128]{1,0:T(8,128)(2,1)S(1)}, f16[304,128]{1,0:T(8,128)(2,1)S(1)}, u32[]{:S(2)}, u32[]{:S(2)}) collective-permute-start(f16[304,128]{1,0:T(8,128)(2,1)S(1)} %concatenate.60), channel_id=1, source_target_pairs={{0,2},{1,3},{2,0},{3,1},{4,6},{5,7},{6,4},{7,5},{8,10},{9,11},{10,... | collective-permute-start | bytes 233480 | tf_op jit(solution)/shard_map/ppermute | solution.py:45
  135.6 3.6 %collective-permute-start.15 = (f16[304,128]{1,0:T(8,128)(2,1)S(1)}, f16[304,128]{1,0:T(8,128)(2,1)S(1)}, u32[]{:S(2)}, u32[]{:S(2)}) collective-permute-start(f16[304,128]{1,0:T(8,128)(2,1)S(1)} %concatenate.60), channel_id=1, source_target_pairs={{0,66},{1,67},{2,64},{3,65},{4,70},{5,71},{6,68},{7,69},{8,74},{9,... | collective-permute-start | bytes 233480 | tf_op jit(solution)/shard_map/ppermute | solution.py:45
  139.3 7.1 %copy-start.4 = (f32[1,128]{1,0:T(1,128)}, f32[1,128]{1,0:T(1,128)S(1)}, u32[]{:S(2)}) copy-start(f32[1,128]{1,0:T(1,128)S(1)} %get-tuple-element.40) | copy-start | bytes 1540
  139.6 11.4 %copy-start.3 = (f32[4,1,384]{2,1,0:T(1,128)S(1)}, f32[4,1,384]{2,1,0:T(1,128)}, u32[]{:S(2)}) copy-start(f32[4,1,384]{2,1,0:T(1,128)} %get-tuple-element.36) | copy-start | bytes 18436
  139.7 4.5 %collective-permute-start.16 = (f16[304,128]{1,0:T(8,128)(2,1)S(1)}, f16[304,128]{1,0:T(8,128)(2,1)S(1)}, u32[]{:S(2)}, u32[]{:S(2)}) collective-permute-start(f16[304,128]{1,0:T(8,128)(2,1)S(1)} %concatenate.61), channel_id=1, source_target_pairs={{0,4},{1,5},{2,6},{3,7},{4,8},{5,9},{6,10},{7,11},{8,12},{9,13},{1... | collective-permute-start | bytes 233480 | tf_op jit(solution)/shard_map/ppermute | solution.py:45
  139.7 5.9 %collective-permute-start.17 = (f16[304,128]{1,0:T(8,128)(2,1)S(1)}, f16[304,128]{1,0:T(8,128)(2,1)S(1)}, u32[]{:S(2)}, u32[]{:S(2)}) collective-permute-start(f16[304,128]{1,0:T(8,128)(2,1)S(1)} %concatenate.61), channel_id=1, source_target_pairs={{0,8},{1,9},{2,10},{3,11},{4,12},{5,13},{6,14},{7,15},{8,0},{9,1},... | collective-permute-start | bytes 233480 | tf_op jit(solution)/shard_map/ppermute | solution.py:45
  143.0 3.2 %collective-permute-start.18 = (f16[304,128]{1,0:T(8,128)(2,1)S(1)}, f16[304,128]{1,0:T(8,128)(2,1)S(1)}, u32[]{:S(2)}, u32[]{:S(2)}) collective-permute-start(f16[304,128]{1,0:T(8,128)(2,1)S(1)} %concatenate.61), channel_id=1, source_target_pairs={{0,12},{1,13},{2,14},{3,15},{4,0},{5,1},{6,2},{7,3},{8,4},{9,5},{1... | collective-permute-start | bytes 233480 | tf_op jit(solution)/shard_map/ppermute | solution.py:45
  146.4 6.2 %collective-permute-start.19 = (f32[1152,128]{1,0:T(8,128)S(1)}, f32[1152,128]{1,0:T(8,128)S(1)}, u32[]{:S(2)}, u32[]{:S(2)}) collective-permute-start(f32[1152,128]{1,0:T(8,128)S(1)} %pad_maximum_fusion.1), channel_id=1, source_target_pairs={{0,1},{1,0},{2,3},{3,2},{4,5},{5,4},{6,7},{7,6},{8,9},{9,8},{10,11... | collective-permute-start | bytes 1769480 | tf_op jit(solution)/shard_map/ppermute | solution.py:45

commit v7 on v6

--- a/solution.py
+++ b/solution.py
@@ -227,7 +227,7 @@
         edge_kernel,
         out_shape=(rows(4), rows(2), rows(1), jax.ShapeDtypeStruct((8, C), F32)),
         in_specs=[smem, smem, hbm, hbm],
-        out_specs=(hbm, hbm, hbm, vmem),
+        out_specs=(vmem,) * 4,
         scratch_shapes=[pltpu.SemaphoreType.DMA((7, 2))],
         name="edge_rows",
     )(counts, place, state, target)

time: 154 us -> 114 us (0.74)
  Pallas kernels: 75.1 us -> 35.1 us
    pallas_call x1, Pallas kernels: 43.5 us -> 3.45 us  [edges(): pl.pallas_call(edge_kernel, out_shape=(rows(4), rows(2), rows(1), jax.Sha...]
  transfers between devices with their start and end apart: 20 -> 20, of which waited for: 15 -> 15; matrix products, arithmetic and copies ran while one was open for 4% -> 5% of each run, Pallas kernels for 28% -> 3%
where the time goes in v7:
time: 114 us
  Pallas kernels  35.1 us (31%)
  starting transfers between devices  33.8 us (30%)
  waiting for transfers between devices  29.3 us (26%)
  other arithmetic  8.15 us (7%)
  local copies, waits for them, and re-layouts  5.72 us (5%)
  between operations  1.65 us (1%)
    pallas_call x1, Pallas kernels, local_step(): pl.pallas_call(kernel, out_shape=(jax.ShapeDtypeStruct((2, G + 8, C), F32...  31.6 us
    ppermute x17, starting transfers between devices, permute(): lax.ppermute(value, BM, [(i, index(move(coords(i)))) for i in range(128)])  26.1 us
    ppermute x17, waiting for transfers between devices, permute(): lax.ppermute(value, BM, [(i, index(move(coords(i)))) for i in range(128)])  18.6 us
    ppermute x3, waiting for transfers between devices, send(): return lax.ppermute(value, BM, pairs)  10.7 us
    ppermute x3, starting transfers between devices, send(): return lax.ppermute(value, BM, pairs)  7.69 us
    pallas_call x1, Pallas kernels, edges(): pl.pallas_call(edge_kernel, out_shape=(rows(4), rows(2), rows(1), jax.Sha...  3.45 us
  transfers between devices with their start and end apart: 20, of which 15 were waited for; matrix products, arithmetic and copies ran while one was open for 5% of the time, Pallas kernels for 3%

profile of v7, /device:TPU:1, one launch (start us, length us, event | category | flops | bytes accessed | tf_op | source)
XLA Modules:
  0.0 113.7 jit_solution(5282312754552482784)
XLA Ops:
  1.3 1.5 %collective-permute-start = (s32[4]{0:T(128)S(1)}, s32[4]{0:T(128)S(1)}, u32[]{:S(2)}, u32[]{:S(2)}) collective-permute-start(s32[4]{0:T(128)S(1)} %compare_select_fusion), channel_id=1, source_target_pairs={{0,1},{1,0},{2,3},{3,2},{4,5},{5,4},{6,7},{7,6},{8,9},{9,8},{10,11... | collective-permute-start | bytes 56 | tf_op jit(solution)/shard_map/ppermute | solution.py:45
  3.4 3.5 %edge_rows.1 = (bf16[4,752,128]{2,1,0:T(8,128)(2,1)}, bf16[2,752,128]{2,1,0:T(8,128)(2,1)}, bf16[1,752,128]{2,1,0:T(8,128)(2,1)}, f32[8,128]{1,0:T(8,128)}) custom-call(s32[32]{0:T(128)} %counts_ref.3, s32[2]{0:T(128)} %pad_add_fusion.place_ref, bf16[4,1440,128]{2,1,0:T(8,128)(2,1)} %state_ref.3, bf16[4,1440,128]{2,1,0:T(8,128)(2,1)} %target_ref.3), custom_call_target="tpu_custom_call" | custom-call | tf_op jit(solution)/shard_map/edge_rows/pallas_call | solution.py:226
  6.9 6.5 %collective-permute-start.2 = (bf16[4,752,128]{2,1,0:T(8,128)(2,1)}, bf16[4,752,128]{2,1,0:T(8,128)(2,1)S(1)}, u32[]{:S(2)}, u32[]{:S(2)}) collective-permute-start(bf16[4,752,128]{2,1,0:T(8,128)(2,1)} %get-tuple-element.26), channel_id=1, source_target_pairs={{0,4},{1,125},{2,6},{3,127},{4,8},{5,1},{6,10},{7,3},{8,12},{9,5},... | collective-permute-start | bytes 2310152 | tf_op jit(solution)/shard_map/ppermute | solution.py:596
  13.3 0.8 compare_bitcast_fusion.3
  14.2 3.3 %collective-permute-start.1 = (s32[4]{0:T(128)S(1)}, s32[4]{0:T(128)S(1)}, u32[]{:S(2)}, u32[]{:S(2)}) collective-permute-start(s32[4]{0:T(128)S(1)} %fusion.108), channel_id=1, source_target_pairs={{0,2},{1,3},{2,0},{3,1},{4,6},{5,7},{6,4},{7,5},{8,10},{9,11},{10,... | collective-permute-start | bytes 56 | tf_op jit(solution)/shard_map/ppermute | solution.py:45
  17.5 1.3 %collective-permute-done.1 = s32[4]{0:T(128)S(1)} collective-permute-done((s32[4]{0:T(128)S(1)}, s32[4]{0:T(128)S(1)}, u32[]{:S(2)}, u32[]{:S(2)}) %collective-permute-start.1) | collective-permute-done | bytes 48 | tf_op jit(solution)/shard_map/ppermute | solution.py:45
  19.3 1.2 %collective-permute-start.3 = (bf16[2,752,128]{2,1,0:T(8,128)(2,1)}, bf16[2,752,128]{2,1,0:T(8,128)(2,1)S(1)}, u32[]{:S(2)}, u32[]{:S(2)}) collective-permute-start(bf16[2,752,128]{2,1,0:T(8,128)(2,1)} %get-tuple-element.28), channel_id=1, source_target_pairs={{0,8},{1,121},{2,10},{3,123},{4,12},{5,125},{6,14},{7,127},{8,16},... | collective-permute-start | bytes 1155080 | tf_op jit(solution)/shard_map/ppermute | solution.py:596
  20.5 1.3 %fusion.6 = (bf16[1536,256]{1,0:T(8,128)(2,1)}, bf16[1536,256]{1,0:T(8,128)(2,1)}) fusion(bf16[1152,128]{1,0:T(8,128)(2,1)S(1)} %bitcast.249, bf16[1152,128]{1,0:T(8,128)(2,1)S(1)} %bitcast.244), kind=kLoop, calls=%fused_computation.8 | loop fusion | flops 5505024 | bytes 2162688 | tf_op jit(solution)/shard_map/concatenate | solution.py:577
  22.1 1.0 fusion.8.wt_ref
  23.0 10.7 %collective-permute-done.4 = bf16[1,752,128]{2,1,0:T(8,128)(2,1)S(1)} collective-permute-done((bf16[1,752,128]{2,1,0:T(8,128)(2,1)}, bf16[1,752,128]{2,1,0:T(8,128)(2,1)S(1)}, u32[]{:S(2)}, u32[]{:S(2)}) %collective-permute-start.4) | collective-permute-done | bytes 192544 | tf_op jit(solution)/shard_map/ppermute | solution.py:596
  33.9 0.8 constant_dynamic-slice_fusion
  34.8 1.7 %collective-permute-start.5 = (bf16[4,384,128]{2,1,0:T(8,128)(2,1)S(1)}, bf16[4,384,128]{2,1,0:T(8,128)(2,1)S(1)}, u32[]{:S(2)}, u32[]{:S(2)}) collective-permute-start(bf16[4,384,128]{2,1,0:T(8,128)(2,1)S(1)} %get-tuple-element.64), channel_id=1, source_target_pairs={{0,1},{1,0},{2,3},{3,2},{4,5},{5,4},{6,7},{7,6},{8,9},{9,8},{10,11... | collective-permute-start | bytes 1179656 | tf_op jit(solution)/shard_map/ppermute | solution.py:45
  36.5 1.3 %collective-permute-done.5.other_ref = bf16[4,384,128]{2,1,0:T(8,128)(2,1)S(1)} collective-permute-done((bf16[4,384,128]{2,1,0:T(8,128)(2,1)S(1)}, bf16[4,384,128]{2,1,0:T(8,128)(2,1)S(1)}, u32[]{:S(2)}, u32[]{:S(2)}) %collective-permute-start.5) | collective-permute-done | bytes 393248 | tf_op jit(solution)/shard_map/ppermute | solution.py:45
  38.6 31.6 %ensemble_step.1 = (f32[2,1160,128]{2,1,0:T(8,128)}, f32[4,1,384]{2,1,0:T(1,128)}) custom-call(s32[32]{0:T(128)} %counts_ref.3, s32[4]{0:T(128)} %add.301.seeds_ref, s32[2]{0:T(128)} %pad_add_fusion.place_ref, f32[96]{0:T(128)} %constant.203.clone.weight_ref, bf16[4,1440,128]{2,1,0:T(8,128)(2,1)} %state_ref.3, bf16[4,1440,128]{2,1,0:T(8,128)(2,1)} %target_ref.3, ...), custom_call_target="tpu_custom_call" | custom-call | tf_op jit(solution)/shard_map/ensemble_step/pallas_call | solution.py:544
  70.2 1.1 slice_bitcast_fusion
  71.8 1.7 %collective-permute-done.6 = f32[1160,128]{1,0:T(8,128)S(1)} collective-permute-done((f32[1160,128]{1,0:T(8,128)S(1)}, f32[1160,128]{1,0:T(8,128)S(1)}, u32[]{:S(2)}, u32[]{:S(2)}) %collective-permute-start.6) | collective-permute-done | bytes 593952 | tf_op jit(solution)/shard_map/ppermute | solution.py:45
  74.3 1.2 %fusion.10 = f16[1152,128]{1,0:T(8,128)(2,1)S(1)} fusion(f32[1160,128]{1,0:T(8,128)S(1)} %collective-permute-done.6, f32[2,1160,128]{2,1,0:T(8,128)} %get-tuple-element.37, f32[128]{0:T(128)S(1)} %divide_bitcast_fusion.3), kind=kLoop, calls=%fused_computation.15 | loop fusion | flops 442368 | bytes 1475072 | tf_op jit(solution)/shard_map/convert_element_type | solution.py:75
  76.2 0.9 collective-permute-start.8
  77.3 2.1 %collective-permute-start.9 = (f16[304,128]{1,0:T(8,128)(2,1)S(1)}, f16[304,128]{1,0:T(8,128)(2,1)S(1)}, u32[]{:S(2)}, u32[]{:S(2)}) collective-permute-start(f16[304,128]{1,0:T(8,128)(2,1)S(1)} %concatenate.58), channel_id=1, source_target_pairs={{0,12},{1,13},{2,14},{3,15},{4,0},{5,1},{6,2},{7,3},{8,4},{9,5},{1... | collective-permute-start | bytes 233480 | tf_op jit(solution)/shard_map/ppermute | solution.py:45
  79.5 3.0 %collective-permute-done.7 = f16[304,128]{1,0:T(8,128)(2,1)S(1)} collective-permute-done((f16[304,128]{1,0:T(8,128)(2,1)S(1)}, f16[304,128]{1,0:T(8,128)(2,1)S(1)}, u32[]{:S(2)}, u32[]{:S(2)}) %collective-permute-start.7) | collective-permute-done | bytes 77856 | tf_op jit(solution)/shard_map/ppermute | solution.py:45
  83.6 2.0 %collective-permute-start.11 = (f16[304,128]{1,0:T(8,128)(2,1)S(1)}, f16[304,128]{1,0:T(8,128)(2,1)S(1)}, u32[]{:S(2)}, u32[]{:S(2)}) collective-permute-start(f16[304,128]{1,0:T(8,128)(2,1)S(1)} %concatenate.59), channel_id=1, source_target_pairs={{0,32},{1,33},{2,34},{3,35},{4,36},{5,37},{6,38},{7,39},{8,40},{9,... | collective-permute-start | bytes 233480 | tf_op jit(solution)/shard_map/ppermute | solution.py:45
  86.3 2.5 %collective-permute-done.10 = f16[304,128]{1,0:T(8,128)(2,1)S(1)} collective-permute-done((f16[304,128]{1,0:T(8,128)(2,1)S(1)}, f16[304,128]{1,0:T(8,128)(2,1)S(1)}, u32[]{:S(2)}, u32[]{:S(2)}) %collective-permute-start.10) | collective-permute-done | bytes 77856 | tf_op jit(solution)/shard_map/ppermute | solution.py:45
  90.2 2.2 %collective-permute-start.13 = (f16[304,128]{1,0:T(8,128)(2,1)S(1)}, f16[304,128]{1,0:T(8,128)(2,1)S(1)}, u32[]{:S(2)}, u32[]{:S(2)}) collective-permute-start(f16[304,128]{1,0:T(8,128)(2,1)S(1)} %concatenate.60), channel_id=1, source_target_pairs={{0,64},{1,65},{2,66},{3,67},{4,68},{5,69},{6,70},{7,71},{8,72},{9,... | collective-permute-start | bytes 233480 | tf_op jit(solution)/shard_map/ppermute | solution.py:45
  92.3 3.3 %collective-permute-start.14 = (f16[304,128]{1,0:T(8,128)(2,1)S(1)}, f16[304,128]{1,0:T(8,128)(2,1)S(1)}, u32[]{:S(2)}, u32[]{:S(2)}) collective-permute-start(f16[304,128]{1,0:T(8,128)(2,1)S(1)} %concatenate.60), channel_id=1, source_target_pairs={{0,2},{1,3},{2,0},{3,1},{4,6},{5,7},{6,4},{7,5},{8,10},{9,11},{10,... | collective-permute-start | bytes 233480 | tf_op jit(solution)/shard_map/ppermute | solution.py:45
  96.3 2.0 %collective-permute-done.14 = f16[304,128]{1,0:T(8,128)(2,1)S(1)} collective-permute-done((f16[304,128]{1,0:T(8,128)(2,1)S(1)}, f16[304,128]{1,0:T(8,128)(2,1)S(1)}, u32[]{:S(2)}, u32[]{:S(2)}) %collective-permute-start.14) | collective-permute-done | bytes 77856 | tf_op jit(solution)/shard_map/ppermute | solution.py:45
  98.3 0.9 collective-permute-done.15
  99.8 3.0 %collective-permute-start.17 = (f16[304,128]{1,0:T(8,128)(2,1)S(1)}, f16[304,128]{1,0:T(8,128)(2,1)S(1)}, u32[]{:S(2)}, u32[]{:S(2)}) collective-permute-start(f16[304,128]{1,0:T(8,128)(2,1)S(1)} %concatenate.61), channel_id=1, source_target_pairs={{0,8},{1,9},{2,10},{3,11},{4,12},{5,13},{6,14},{7,15},{8,0},{9,1},... | collective-permute-start | bytes 233480 | tf_op jit(solution)/shard_map/ppermute | solution.py:45
  103.0 1.3 %collective-permute-done.16 = f16[304,128]{1,0:T(8,128)(2,1)S(1)} collective-permute-done((f16[304,128]{1,0:T(8,128)(2,1)S(1)}, f16[304,128]{1,0:T(8,128)(2,1)S(1)}, u32[]{:S(2)}, u32[]{:S(2)}) %collective-permute-start.16) | collective-permute-done | bytes 77856 | tf_op jit(solution)/shard_map/ppermute | solution.py:45
  104.3 1.2 %collective-permute-done.17 = f16[304,128]{1,0:T(8,128)(2,1)S(1)} collective-permute-done((f16[304,128]{1,0:T(8,128)(2,1)S(1)}, f16[304,128]{1,0:T(8,128)(2,1)S(1)}, u32[]{:S(2)}, u32[]{:S(2)}) %collective-permute-start.17) | collective-permute-done | bytes 77856 | tf_op jit(solution)/shard_map/ppermute | solution.py:45
  106.3 4.7 %collective-permute-start.19 = (f32[1152,128]{1,0:T(8,128)S(1)}, f32[1152,128]{1,0:T(8,128)S(1)}, u32[]{:S(2)}, u32[]{:S(2)}) collective-permute-start(f32[1152,128]{1,0:T(8,128)S(1)} %pad_maximum_fusion.1), channel_id=1, source_target_pairs={{0,1},{1,0},{2,3},{3,2},{4,5},{5,4},{6,7},{7,6},{8,9},{9,8},{10,11... | collective-permute-start | bytes 1769480 | tf_op jit(solution)/shard_map/ppermute | solution.py:45
  111.7 0.9 collective-permute-done.19
  112.6 1.1 broadcast_select_fusion
  (93 shorter events, 10.2 us)
Async XLA Ops:
  1.3 5.5 %collective-permute-start = (s32[4]{0:T(128)S(1)}, s32[4]{0:T(128)S(1)}, u32[]{:S(2)}, u32[]{:S(2)}) collective-permute-start(s32[4]{0:T(128)S(1)} %compare_select_fusion), channel_id=1, source_target_pairs={{0,1},{1,0},{2,3},{3,2},{4,5},{5,4},{6,7},{7,6},{8,9},{9,8},{10,11... | collective-permute-start | bytes 56 | tf_op jit(solution)/shard_map/ppermute | solution.py:45
  3.4 17.2 %copy-start = (bf16[3,3,128,128]{3,2,1,0:T(8,128)(2,1)S(1)}, bf16[3,3,128,128]{3,2,1,0:T(8,128)(2,1)}, u32[]{:S(2)}) copy-start(bf16[3,3,128,128]{3,2,1,0:T(8,128)(2,1)} %param.12) | copy-start | bytes 884740
  3.4 17.2 %copy-start.2 = (bf16[3,3,128,128]{3,2,1,0:T(8,128)(2,1)S(1)}, bf16[3,3,128,128]{3,2,1,0:T(8,128)(2,1)}, u32[]{:S(2)}) copy-start(bf16[3,3,128,128]{3,2,1,0:T(8,128)(2,1)} %param.11) | copy-start | bytes 884740
  6.9 26.9 %collective-permute-start.2 = (bf16[4,752,128]{2,1,0:T(8,128)(2,1)}, bf16[4,752,128]{2,1,0:T(8,128)(2,1)S(1)}, u32[]{:S(2)}, u32[]{:S(2)}) collective-permute-start(bf16[4,752,128]{2,1,0:T(8,128)(2,1)} %get-tuple-element.26), channel_id=1, source_target_pairs={{0,4},{1,125},{2,6},{3,127},{4,8},{5,1},{6,10},{7,3},{8,12},{9,5},... | collective-permute-start | bytes 2310152 | tf_op jit(solution)/shard_map/ppermute | solution.py:596
  14.2 4.6 %collective-permute-start.1 = (s32[4]{0:T(128)S(1)}, s32[4]{0:T(128)S(1)}, u32[]{:S(2)}, u32[]{:S(2)}) collective-permute-start(s32[4]{0:T(128)S(1)} %fusion.108), channel_id=1, source_target_pairs={{0,2},{1,3},{2,0},{3,1},{4,6},{5,7},{6,4},{7,5},{8,10},{9,11},{10,... | collective-permute-start | bytes 56 | tf_op jit(solution)/shard_map/ppermute | solution.py:45
  19.3 14.4 %collective-permute-start.4 = (bf16[1,752,128]{2,1,0:T(8,128)(2,1)}, bf16[1,752,128]{2,1,0:T(8,128)(2,1)S(1)}, u32[]{:S(2)}, u32[]{:S(2)}) collective-permute-start(bf16[1,752,128]{2,1,0:T(8,128)(2,1)} %get-tuple-element.29), channel_id=1, source_target_pairs={{0,12},{1,117},{2,14},{3,119},{4,16},{5,121},{6,18},{7,123},{8,20}... | collective-permute-start | bytes 577544 | tf_op jit(solution)/shard_map/ppermute | solution.py:596
  19.3 14.4 %collective-permute-start.3 = (bf16[2,752,128]{2,1,0:T(8,128)(2,1)}, bf16[2,752,128]{2,1,0:T(8,128)(2,1)S(1)}, u32[]{:S(2)}, u32[]{:S(2)}) collective-permute-start(bf16[2,752,128]{2,1,0:T(8,128)(2,1)} %get-tuple-element.28), channel_id=1, source_target_pairs={{0,8},{1,121},{2,10},{3,123},{4,12},{5,125},{6,14},{7,127},{8,16},... | collective-permute-start | bytes 1155080 | tf_op jit(solution)/shard_map/ppermute | solution.py:596
  34.8 3.1 %collective-permute-start.5 = (bf16[4,384,128]{2,1,0:T(8,128)(2,1)S(1)}, bf16[4,384,128]{2,1,0:T(8,128)(2,1)S(1)}, u32[]{:S(2)}, u32[]{:S(2)}) collective-permute-start(bf16[4,384,128]{2,1,0:T(8,128)(2,1)S(1)} %get-tuple-element.64), channel_id=1, source_target_pairs={{0,1},{1,0},{2,3},{3,2},{4,5},{5,4},{6,7},{7,6},{8,9},{9,8},{10,11... | collective-permute-start | bytes 1179656 | tf_op jit(solution)/shard_map/ppermute | solution.py:45
  37.8 0.7 copy-start.1
  71.4 2.1 %collective-permute-start.6 = (f32[1160,128]{1,0:T(8,128)S(1)}, f32[1160,128]{1,0:T(8,128)S(1)}, u32[]{:S(2)}, u32[]{:S(2)}) collective-permute-start(f32[1160,128]{1,0:T(8,128)S(1)} %slice_bitcast_fusion), channel_id=1, source_target_pairs={{0,1},{1,0},{2,3},{3,2},{4,5},{5,4},{6,7},{7,6},{8,9},{9,8},{10,11... | collective-permute-start | bytes 1781768 | tf_op jit(solution)/shard_map/ppermute | solution.py:45
  75.9 6.6 %collective-permute-start.7 = (f16[304,128]{1,0:T(8,128)(2,1)S(1)}, f16[304,128]{1,0:T(8,128)(2,1)S(1)}, u32[]{:S(2)}, u32[]{:S(2)}) collective-permute-start(f16[304,128]{1,0:T(8,128)(2,1)S(1)} %concatenate.56), channel_id=1, source_target_pairs={{0,4},{1,5},{2,6},{3,7},{4,8},{5,9},{6,10},{7,11},{8,12},{9,13},{1... | collective-permute-start | bytes 233480 | tf_op jit(solution)/shard_map/ppermute | solution.py:45
  76.2 6.4 %collective-permute-start.8 = (f16[304,128]{1,0:T(8,128)(2,1)S(1)}, f16[304,128]{1,0:T(8,128)(2,1)S(1)}, u32[]{:S(2)}, u32[]{:S(2)}) collective-permute-start(f16[304,128]{1,0:T(8,128)(2,1)S(1)} %concatenate.57), channel_id=1, source_target_pairs={{0,8},{1,9},{2,10},{3,11},{4,12},{5,13},{6,14},{7,15},{8,0},{9,1},... | collective-permute-start | bytes 233480 | tf_op jit(solution)/shard_map/ppermute | solution.py:45
  77.3 5.7 %collective-permute-start.9 = (f16[304,128]{1,0:T(8,128)(2,1)S(1)}, f16[304,128]{1,0:T(8,128)(2,1)S(1)}, u32[]{:S(2)}, u32[]{:S(2)}) collective-permute-start(f16[304,128]{1,0:T(8,128)(2,1)S(1)} %concatenate.58), channel_id=1, source_target_pairs={{0,12},{1,13},{2,14},{3,15},{4,0},{5,1},{6,2},{7,3},{8,4},{9,5},{1... | collective-permute-start | bytes 233480 | tf_op jit(solution)/shard_map/ppermute | solution.py:45
  83.5 5.4 %collective-permute-start.10 = (f16[304,128]{1,0:T(8,128)(2,1)S(1)}, f16[304,128]{1,0:T(8,128)(2,1)S(1)}, u32[]{:S(2)}, u32[]{:S(2)}) collective-permute-start(f16[304,128]{1,0:T(8,128)(2,1)S(1)} %concatenate.59), channel_id=1, source_target_pairs={{0,16},{1,17},{2,18},{3,19},{4,20},{5,21},{6,22},{7,23},{8,24},{9,... | collective-permute-start | bytes 233480 | tf_op jit(solution)/shard_map/ppermute | solution.py:45
  83.6 5.3 %collective-permute-start.11 = (f16[304,128]{1,0:T(8,128)(2,1)S(1)}, f16[304,128]{1,0:T(8,128)(2,1)S(1)}, u32[]{:S(2)}, u32[]{:S(2)}) collective-permute-start(f16[304,128]{1,0:T(8,128)(2,1)S(1)} %concatenate.59), channel_id=1, source_target_pairs={{0,32},{1,33},{2,34},{3,35},{4,36},{5,37},{6,38},{7,39},{8,40},{9,... | collective-permute-start | bytes 233480 | tf_op jit(solution)/shard_map/ppermute | solution.py:45
  85.5 4.2 %collective-permute-start.12 = (f16[304,128]{1,0:T(8,128)(2,1)S(1)}, f16[304,128]{1,0:T(8,128)(2,1)S(1)}, u32[]{:S(2)}, u32[]{:S(2)}) collective-permute-start(f16[304,128]{1,0:T(8,128)(2,1)S(1)} %concatenate.59), channel_id=1, source_target_pairs={{0,48},{1,49},{2,50},{3,51},{4,52},{5,53},{6,54},{7,55},{8,56},{9,... | collective-permute-start | bytes 233480 | tf_op jit(solution)/shard_map/ppermute | solution.py:45
  90.2 6.1 %collective-permute-start.13 = (f16[304,128]{1,0:T(8,128)(2,1)S(1)}, f16[304,128]{1,0:T(8,128)(2,1)S(1)}, u32[]{:S(2)}, u32[]{:S(2)}) collective-permute-start(f16[304,128]{1,0:T(8,128)(2,1)S(1)} %concatenate.60), channel_id=1, source_target_pairs={{0,64},{1,65},{2,66},{3,67},{4,68},{5,69},{6,70},{7,71},{8,72},{9,... | collective-permute-start | bytes 233480 | tf_op jit(solution)/shard_map/ppermute | solution.py:45
  92.3 6.0 %collective-permute-start.14 = (f16[304,128]{1,0:T(8,128)(2,1)S(1)}, f16[304,128]{1,0:T(8,128)(2,1)S(1)}, u32[]{:S(2)}, u32[]{:S(2)}) collective-permute-start(f16[304,128]{1,0:T(8,128)(2,1)S(1)} %concatenate.60), channel_id=1, source_target_pairs={{0,2},{1,3},{2,0},{3,1},{4,6},{5,7},{6,4},{7,5},{8,10},{9,11},{10,... | collective-permute-start | bytes 233480 | tf_op jit(solution)/shard_map/ppermute | solution.py:45
  95.7 3.6 %collective-permute-start.15 = (f16[304,128]{1,0:T(8,128)(2,1)S(1)}, f16[304,128]{1,0:T(8,128)(2,1)S(1)}, u32[]{:S(2)}, u32[]{:S(2)}) collective-permute-start(f16[304,128]{1,0:T(8,128)(2,1)S(1)} %concatenate.60), channel_id=1, source_target_pairs={{0,66},{1,67},{2,64},{3,65},{4,70},{5,71},{6,68},{7,69},{8,74},{9,... | collective-permute-start | bytes 233480 | tf_op jit(solution)/shard_map/ppermute | solution.py:45
  99.4 6.9 %copy-start.4 = (f32[1,128]{1,0:T(1,128)}, f32[1,128]{1,0:T(1,128)S(1)}, u32[]{:S(2)}) copy-start(f32[1,128]{1,0:T(1,128)S(1)} %get-tuple-element.40) | copy-start | bytes 1540
  99.8 11.2 %copy-start.3 = (f32[4,1,384]{2,1,0:T(1,128)S(1)}, f32[4,1,384]{2,1,0:T(1,128)}, u32[]{:S(2)}) copy-start(f32[4,1,384]{2,1,0:T(1,128)} %get-tuple-element.36) | copy-start | bytes 18436
  99.8 4.5 %collective-permute-start.16 = (f16[304,128]{1,0:T(8,128)(2,1)S(1)}, f16[304,128]{1,0:T(8,128)(2,1)S(1)}, u32[]{:S(2)}, u32[]{:S(2)}) collective-permute-start(f16[304,128]{1,0:T(8,128)(2,1)S(1)} %concatenate.61), channel_id=1, source_target_pairs={{0,4},{1,5},{2,6},{3,7},{4,8},{5,9},{6,10},{7,11},{8,12},{9,13},{1... | collective-permute-start | bytes 233480 | tf_op jit(solution)/shard_map/ppermute | solution.py:45
  99.8 5.6 %collective-permute-start.17 = (f16[304,128]{1,0:T(8,128)(2,1)S(1)}, f16[304,128]{1,0:T(8,128)(2,1)S(1)}, u32[]{:S(2)}, u32[]{:S(2)}) collective-permute-start(f16[304,128]{1,0:T(8,128)(2,1)S(1)} %concatenate.61), channel_id=1, source_target_pairs={{0,8},{1,9},{2,10},{3,11},{4,12},{5,13},{6,14},{7,15},{8,0},{9,1},... | collective-permute-start | bytes 233480 | tf_op jit(solution)/shard_map/ppermute | solution.py:45
  102.9 3.2 %collective-permute-start.18 = (f16[304,128]{1,0:T(8,128)(2,1)S(1)}, f16[304,128]{1,0:T(8,128)(2,1)S(1)}, u32[]{:S(2)}, u32[]{:S(2)}) collective-permute-start(f16[304,128]{1,0:T(8,128)(2,1)S(1)} %concatenate.61), channel_id=1, source_target_pairs={{0,12},{1,13},{2,14},{3,15},{4,0},{5,1},{6,2},{7,3},{8,4},{9,5},{1... | collective-permute-start | bytes 233480 | tf_op jit(solution)/shard_map/ppermute | solution.py:45
  106.3 6.4 %collective-permute-start.19 = (f32[1152,128]{1,0:T(8,128)S(1)}, f32[1152,128]{1,0:T(8,128)S(1)}, u32[]{:S(2)}, u32[]{:S(2)}) collective-permute-start(f32[1152,128]{1,0:T(8,128)S(1)} %pad_maximum_fusion.1), channel_id=1, source_target_pairs={{0,1},{1,0},{2,3},{3,2},{4,5},{5,4},{6,7},{7,6},{8,9},{9,8},{10,11... | collective-permute-start | bytes 1769480 | tf_op jit(solution)/shard_map/ppermute | solution.py:45
